TPU v7x, 32 devices: a whole 2x2x4 slice. The times are simulated.
32 devices in a mesh: dp: 8 (over z, x), tensor: 4 (over y, core).
Axes of the slice: x: 2, y: 2, z: 4, core: 2. Of those that a mesh axis runs over, the one named last changes fastest.
Arguments:
- tokens: bfloat16 [16384, 768], P(('dp', 'tensor')), may hold values from -6 to 6
- segment_ids: int32 [16384], P('dp'), may hold values from 0 to 39, never falling along the last dimension, each value on 1 to 800 neighbouring positions
- query_weight: bfloat16 [768, 768], P('dp', 'tensor'), may hold values from -0.21875 to 0.21875
- query_bias: bfloat16 [768], P('tensor'), may hold values from -3 to 3
- key_weight: bfloat16 [768, 768], P('dp', 'tensor'), may hold values from -0.21875 to 0.21875
- value_weight: bfloat16 [768, 768], P('dp', 'tensor'), may hold values from -0.21875 to 0.21875
- value_bias: bfloat16 [768], P('tensor'), may hold values from -3 to 3
- out_weight: bfloat16 [768, 768], P('tensor', 'dp'), may hold values from -1.25 to 1.25
- out_bias: bfloat16 [768], replicated, may hold values from -3 to 3
- first_gain: bfloat16 [768], replicated, may hold values from 0.5 to 1.5
- first_shift: bfloat16 [768], replicated, may hold values from -3 to 3
- hidden_weight: bfloat16 [768, 3072], P('dp', 'tensor'), may hold values from -0.21875 to 0.21875
- hidden_bias: bfloat16 [3072], P('tensor'), may hold values from -3 to 3
- down_weight: bfloat16 [3072, 768], P('tensor', 'dp'), may hold values from -0.21875 to 0.21875
- down_bias: bfloat16 [768], replicated, may hold values from -3 to 3
- second_gain: bfloat16 [768], replicated, may hold values from 0.5 to 1.5
- second_shift: bfloat16 [768], replicated, may hold values from -3 to 3
- output_cotangent: bfloat16 [16384, 768], P(('dp', 'tensor')), may hold values from -6 to 6
Outputs:
- layer_output: bfloat16 [16384, 768], P(('dp', 'tensor'))
- tokens_gradient: float32 [16384, 768], P(('dp', 'tensor'))
- query_weight_gradient: float32 [768, 768], P('dp', 'tensor')
- query_bias_gradient: float32 [768], P('tensor')
- key_weight_gradient: float32 [768, 768], P('dp', 'tensor')
- value_weight_gradient: float32 [768, 768], P('dp', 'tensor')
- value_bias_gradient: float32 [768], P('tensor')
- out_weight_gradient: float32 [768, 768], P('tensor', 'dp')
- out_bias_gradient: float32 [768], replicated
- first_gain_gradient: float32 [768], replicated
- first_shift_gradient: float32 [768], replicated
- hidden_weight_gradient: float32 [768, 3072], P('dp', 'tensor')
- hidden_bias_gradient: float32 [3072], P('tensor')
- down_weight_gradient: float32 [3072, 768], P('tensor', 'dp')
- down_bias_gradient: float32 [768], replicated
- second_gain_gradient: float32 [768], replicated
- second_shift_gradient: float32 [768], replicated
Inputs may be any that keep to these rules, and one draw needn't show every extreme that they name: `segment_ids`: each document is one run of equal numbers; numbers never fall along the tokens; a document holds at most 800 tokens and some document holds exactly that many. A document may run across the end of a sequence; attention still stays within a sequence.
All inputs are finite; a program needn't handle non-finite values.
Results may differ from a plain program's by a relative error of at most 0.023.
Values may be sent and summed in bfloat16 or wider, within the bound.
A program may use at most 192 MiB of HBM per device.

v0:
```python
import jax
import jax.numpy as jnp
from jax import lax
from jax.sharding import PartitionSpec as P

HEAD = 64
SEQ = 2048


EPSILON = 1e-06
NEGATIVE = -1e30


def normalize(total, gain, shift):
    center = total - jnp.mean(total, axis=-1, keepdims=True)
    inverse = lax.rsqrt(jnp.mean(center * center, axis=-1, keepdims=True) + EPSILON)
    normed = center * inverse
    return (normed * gain + shift, normed, inverse)


def normalize_back(upstream, normed, inverse, gain):
    scaled = upstream * gain
    inner = jnp.mean(scaled, axis=-1, keepdims=True) + normed * jnp.mean(
        scaled * normed, axis=-1, keepdims=True
    )
    return (
        inverse * (scaled - inner),
        jnp.sum(upstream * normed, axis=0),
        jnp.sum(upstream, axis=0),
    )


def times_transpose(left, right):
    return lax.dot_general(
        left, right, (((1,), (1,)), ((), ())), preferred_element_type=jnp.float32
    )


def transpose_times(left, right):
    return lax.dot_general(
        left, right, (((0,), (0,)), ((), ())), preferred_element_type=jnp.float32
    )


def block_scores(queries, keys, segments, index, width, length, scale):
    start = index * width
    base = start // length * length
    query_block = lax.dynamic_slice_in_dim(queries, start, width, 0)
    query_seg = lax.dynamic_slice_in_dim(segments, start, width, 0)
    scores = (
        jnp.einsum("qhd,khd->hqk", query_block, keys, preferred_element_type=jnp.float32) * scale
    )
    allowed = (query_seg[:, None] == segments[None, :])[None]
    return (jnp.where(allowed, scores, NEGATIVE), query_block, keys, base)


def body(
    tokens,
    segment_ids,
    query_weight,
    query_bias,
    key_weight,
    value_weight,
    value_bias,
    out_weight,
    out_bias,
    first_gain,
    first_shift,
    hidden_weight,
    hidden_bias,
    down_weight,
    down_bias,
    second_gain,
    second_shift,
    output_cotangent,
):
    parts = lax.axis_size("tensor")
    rank = lax.axis_index("tensor")
    local_rows = tokens.shape[0]
    group_rows = local_rows * parts
    head_width = query_weight.shape[1]
    heads_here = head_width // HEAD
    length = min(SEQ, group_rows)
    width = min(512, length)
    blocks = group_rows // width
    scale = HEAD ** (-0.5)
    indices = jnp.arange(blocks, dtype=jnp.int32)
    full_query, full_key, full_value, full_hidden, full_down = (
        lax.all_gather(query_weight, "dp", axis=0, tiled=True),
        lax.all_gather(key_weight, "dp", axis=0, tiled=True),
        lax.all_gather(value_weight, "dp", axis=0, tiled=True),
        lax.all_gather(hidden_weight, "dp", axis=0, tiled=True),
        lax.all_gather(down_weight, "dp", axis=1, tiled=True),
    )
    pieces = lax.all_gather(out_weight, ("dp", "tensor"), axis=0, tiled=True)
    shards = lax.axis_size("dp")
    whole_out = (
        pieces.reshape(shards, parts, head_width, -1)
        .transpose(1, 2, 0, 3)
        .reshape(parts * head_width, -1)
    )
    out_heads = lax.dynamic_slice_in_dim(whole_out, rank * head_width, head_width, 0)
    gathered = lax.all_gather(tokens, "tensor", axis=0, tiled=True)
    joined = jnp.concatenate([full_query, full_key, full_value], axis=1)
    projected = jnp.dot(gathered, joined, preferred_element_type=jnp.float32)
    queries = (projected[:, :head_width] + query_bias.astype(jnp.float32)).astype(jnp.bfloat16)
    keys = projected[:, head_width : 2 * head_width].astype(jnp.bfloat16)
    values = (projected[:, 2 * head_width :] + value_bias.astype(jnp.float32)).astype(jnp.bfloat16)
    queries = queries.reshape(group_rows, heads_here, HEAD)
    keys = keys.reshape(group_rows, heads_here, HEAD)
    values = values.reshape(group_rows, heads_here, HEAD)

    def forward_block(index):
        scores, query_block, key_rows, base = block_scores(
            queries, keys, segment_ids, index, width, length, scale
        )
        top = jnp.max(scores, axis=-1, keepdims=True)
        weights = jnp.exp(scores - top)
        total = jnp.sum(weights, axis=-1, keepdims=True)
        shares = (weights / total).astype(jnp.bfloat16)
        mixed = jnp.einsum("hqk,khd->qhd", shares, values, preferred_element_type=jnp.float32)
        return (mixed.astype(jnp.bfloat16), (top + jnp.log(total))[:, :, 0])

    contexts, log_totals = lax.map(forward_block, indices)
    context = contexts.reshape(group_rows, head_width)
    row_context = lax.all_to_all(context, "tensor", split_axis=0, concat_axis=1, tiled=True)
    attended = jnp.dot(row_context, whole_out, preferred_element_type=jnp.float32)
    first_sum = tokens.astype(jnp.float32) + attended + out_bias.astype(jnp.float32)
    first_norm, first_normed, first_inverse = normalize(
        first_sum, first_gain.astype(jnp.float32), first_shift.astype(jnp.float32)
    )
    first_low = first_norm.astype(jnp.bfloat16)
    gathered_mid = lax.all_gather(first_low, "tensor", axis=0, tiled=True)
    hidden_pre = jnp.dot(
        gathered_mid, full_hidden, preferred_element_type=jnp.float32
    ) + hidden_bias.astype(jnp.float32)
    activation = jax.nn.gelu(hidden_pre, approximate=False).astype(jnp.bfloat16)
    second_sum = (
        first_norm
        + lax.psum_scatter(
            jnp.dot(activation, full_down, preferred_element_type=jnp.float32).astype(jnp.bfloat16),
            "tensor",
            scatter_dimension=0,
            tiled=True,
        ).astype(jnp.float32)
        + down_bias.astype(jnp.float32)
    )
    second_norm, second_normed, second_inverse = normalize(
        second_sum, second_gain.astype(jnp.float32), second_shift.astype(jnp.float32)
    )
    layer_output = second_norm.astype(jnp.bfloat16)
    second_grad, second_gain_gradient, second_shift_gradient = normalize_back(
        output_cotangent.astype(jnp.float32),
        second_normed,
        second_inverse,
        second_gain.astype(jnp.float32),
    )
    down_bias_gradient = jnp.sum(second_grad, axis=0)
    second_low = second_grad.astype(jnp.bfloat16)
    gathered_second = lax.all_gather(second_low, "tensor", axis=0, tiled=True)
    down_weight_gradient = transpose_times(activation, gathered_second)
    activation_grad = times_transpose(gathered_second, full_down)
    unused, gelu_back = jax.vjp(lambda inner: jax.nn.gelu(inner, approximate=False), hidden_pre)
    hidden_grad = gelu_back(activation_grad)[0].astype(jnp.bfloat16)
    hidden_bias_gradient = jnp.sum(hidden_grad, axis=0, dtype=jnp.float32)
    hidden_weight_gradient = transpose_times(gathered_mid, hidden_grad)
    first_grad_in = second_grad + lax.psum_scatter(
        times_transpose(hidden_grad, full_hidden).astype(jnp.bfloat16),
        "tensor",
        scatter_dimension=0,
        tiled=True,
    ).astype(jnp.float32)
    first_grad, first_gain_gradient, first_shift_gradient = normalize_back(
        first_grad_in, first_normed, first_inverse, first_gain.astype(jnp.float32)
    )
    out_bias_gradient = jnp.sum(first_grad, axis=0)
    first_low_grad = first_grad.astype(jnp.bfloat16)
    gathered_first = lax.all_gather(first_low_grad, "tensor", axis=0, tiled=True)
    out_weight_gradient = transpose_times(context, gathered_first)
    context_grad = (
        times_transpose(gathered_first, out_heads)
        .astype(jnp.bfloat16)
        .reshape(group_rows, heads_here, HEAD)
    )

    def backward_block(index):
        scores, query_block, key_rows, base = block_scores(
            queries, keys, segment_ids, index, width, length, scale
        )
        upstream = lax.dynamic_slice_in_dim(context_grad, index * width, width, 0)
        log_total = lax.dynamic_index_in_dim(log_totals, index, 0, keepdims=False)
        shares = jnp.exp(scores - log_total[:, :, None])
        share_grad = jnp.einsum(
            "qhd,khd->hqk", upstream, values, preferred_element_type=jnp.float32
        )
        score_grad = (
            shares * (share_grad - jnp.sum(shares * share_grad, axis=-1, keepdims=True))
        ).astype(jnp.bfloat16)
        query_part = (
            jnp.einsum("hqk,khd->qhd", score_grad, key_rows, preferred_element_type=jnp.float32)
            * scale
        )
        key_part = (
            jnp.einsum("hqk,qhd->khd", score_grad, query_block, preferred_element_type=jnp.float32)
            * scale
        )
        value_part = jnp.einsum(
            "hqk,qhd->khd",
            shares.astype(jnp.bfloat16),
            upstream,
            preferred_element_type=jnp.float32,
        )
        return (query_part, key_part, value_part)

    query_parts, key_parts, value_parts = lax.map(backward_block, indices)
    per_sequence = length // width
    sequences = group_rows // length
    query_grad = query_parts.reshape(group_rows, head_width).astype(jnp.bfloat16)
    key_grad = (
        key_parts.reshape(sequences, per_sequence, length, head_width)
        .sum(axis=1)
        .reshape(group_rows, head_width)
        .astype(jnp.bfloat16)
    )
    value_grad = (
        value_parts.reshape(sequences, per_sequence, length, head_width)
        .sum(axis=1)
        .reshape(group_rows, head_width)
        .astype(jnp.bfloat16)
    )
    query_bias_gradient = jnp.sum(query_grad, axis=0, dtype=jnp.float32)
    value_bias_gradient = jnp.sum(value_grad, axis=0, dtype=jnp.float32)
    projected_grad = jnp.concatenate([query_grad, key_grad, value_grad], axis=1)
    joined_gradient = transpose_times(gathered, projected_grad)
    query_weight_gradient = joined_gradient[:, :head_width]
    key_weight_gradient = joined_gradient[:, head_width : 2 * head_width]
    value_weight_gradient = joined_gradient[:, 2 * head_width :]
    tokens_gradient = first_grad + lax.psum_scatter(
        times_transpose(projected_grad, joined).astype(jnp.bfloat16),
        "tensor",
        scatter_dimension=0,
        tiled=True,
    ).astype(jnp.float32)
    (
        query_weight_gradient,
        key_weight_gradient,
        value_weight_gradient,
        out_weight_gradient,
        hidden_weight_gradient,
        down_weight_gradient,
    ) = (
        lax.psum_scatter(
            query_weight_gradient.astype(jnp.bfloat16), "dp", scatter_dimension=0, tiled=True
        ).astype(jnp.float32),
        lax.psum_scatter(
            key_weight_gradient.astype(jnp.bfloat16), "dp", scatter_dimension=0, tiled=True
        ).astype(jnp.float32),
        lax.psum_scatter(
            value_weight_gradient.astype(jnp.bfloat16), "dp", scatter_dimension=0, tiled=True
        ).astype(jnp.float32),
        lax.psum_scatter(
            out_weight_gradient.astype(jnp.bfloat16), "dp", scatter_dimension=1, tiled=True
        ).astype(jnp.float32),
        lax.psum_scatter(
            hidden_weight_gradient.astype(jnp.bfloat16), "dp", scatter_dimension=0, tiled=True
        ).astype(jnp.float32),
        lax.psum_scatter(
            down_weight_gradient.astype(jnp.bfloat16), "dp", scatter_dimension=1, tiled=True
        ).astype(jnp.float32),
    )
    head_terms = jnp.concatenate([query_bias_gradient, value_bias_gradient, hidden_bias_gradient])
    chooser = (jnp.arange(parts, dtype=jnp.int32) == rank).astype(jnp.float32)
    head_table = chooser[:, None] * head_terms[None, :]
    row_table = jnp.stack(
        [
            out_bias_gradient,
            first_gain_gradient,
            first_shift_gradient,
            down_bias_gradient,
            second_gain_gradient,
            second_shift_gradient,
        ]
    )
    head_table, row_table = lax.psum((head_table, row_table), ("dp", "tensor"))
    own_terms = lax.dynamic_index_in_dim(head_table, rank, 0, keepdims=False)
    query_bias_gradient = own_terms[:head_width]
    value_bias_gradient = own_terms[head_width : 2 * head_width]
    hidden_bias_gradient = own_terms[2 * head_width :]
    return (
        layer_output,
        tokens_gradient,
        query_weight_gradient,
        query_bias_gradient,
        key_weight_gradient,
        value_weight_gradient,
        value_bias_gradient,
        out_weight_gradient,
        row_table[0],
        row_table[1],
        row_table[2],
        hidden_weight_gradient,
        hidden_bias_gradient,
        down_weight_gradient,
        row_table[3],
        row_table[4],
        row_table[5],
    )


def solution(mesh):
    in_specs = (
        P(("dp", "tensor"), None),
        P("dp"),
        P("dp", "tensor"),
        P("tensor"),
        P("dp", "tensor"),
        P("dp", "tensor"),
        P("tensor"),
        P("tensor", "dp"),
        P(),
        P(),
        P(),
        P("dp", "tensor"),
        P("tensor"),
        P("tensor", "dp"),
        P(),
        P(),
        P(),
        P(("dp", "tensor"), None),
    )
    out_specs = (
        P(("dp", "tensor"), None),
        P(("dp", "tensor"), None),
        P("dp", "tensor"),
        P("tensor"),
        P("dp", "tensor"),
        P("dp", "tensor"),
        P("tensor"),
        P("tensor", "dp"),
        P(),
        P(),
        P(),
        P("dp", "tensor"),
        P("tensor"),
        P("tensor", "dp"),
        P(),
        P(),
        P(),
    )
    return jax.shard_map(body, mesh=mesh, in_specs=in_specs, out_specs=out_specs, check_vma=False)
```

profile of v0, /device:TPU:0, one launch (start us, length us, event | category | flops | bytes accessed | tf_op | source)
XLA Modules:
  0.0 910.9 jit_solution(8267732935702413759)
XLA Ops:
  10.7 33.2 %all_gather.30 = bf16[768,192]{1,0:T(8,128)(2,1)S(1)} all-gather(bf16[96,192]{1,0:T(8,128)(2,1)} %param.24), channel_id=1, replica_groups=mesh['dp'=8,'tensor'=4] {'dp'}, dimensions={0}, use_global_device_ids=true | all-gather | bytes 331776 | tf_op jit(solution)/shard_map/all_gather | solution.py:89
  43.9 31.3 %all_gather.31 = bf16[768,192]{1,0:T(8,128)(2,1)S(1)} all-gather(bf16[96,192]{1,0:T(8,128)(2,1)} %param.26), channel_id=1, replica_groups=mesh['dp'=8,'tensor'=4] {'dp'}, dimensions={0}, use_global_device_ids=true | all-gather | bytes 331776 | tf_op jit(solution)/shard_map/all_gather | solution.py:90
  75.2 31.7 %all_gather.32 = bf16[768,192]{1,0:T(8,128)(2,1)S(1)} all-gather(bf16[96,192]{1,0:T(8,128)(2,1)} %param.27), channel_id=1, replica_groups=mesh['dp'=8,'tensor'=4] {'dp'}, dimensions={0}, use_global_device_ids=true | all-gather | bytes 331776 | tf_op jit(solution)/shard_map/all_gather | solution.py:91
  107.0 4.6 convolution_bitcast_fusion
  112.3 88.2 %while.26 = (s32[]{:T(128)}, bf16[4,512,3,64]{1,3,2,0:T(8,128)(2,1)}, f32[4,3,512]{2,1,0:T(4,128)S(1)}, s32[4]{0:T(128)S(1)}, s32[2048]{0:T(1024)S(1)}, /*index=...) while((s32[]{:T(128)}, ...), condition=%wide.region_3.4_spmd, body=%wide.region_0.3_spmd.sunk | while | flops 844200448 | bytes 43978948 | solution.py:124
  114.3 6.0 fusion.113
  120.2 6.8 fusion.114
  127.0 7.3 fusion.115
  136.3 6.0 fusion.113
  142.3 6.8 fusion.114
  149.1 7.3 fusion.115
  158.4 6.0 fusion.113
  164.4 6.8 fusion.114
  171.1 7.3 fusion.115
  180.5 6.0 fusion.113
  186.4 6.8 fusion.114
  193.2 7.3 fusion.115
  200.5 3.5 all-to-all-start
  204.4 3.6 copy.61
  207.9 3.8 reshape.221
  211.8 3.9 all-to-all-done
  221.5 27.6 %all-gather.12.cloned.1.call-done = bf16[2048,768]{1,0:T(8,128)(2,1)} async-done(((bf16[512,768]{1,0:T(8,128)(2,1)}), bf16[2048,768]{1,0:T(8,128)(2,1)}) %all-gather.12.cloned.1.call-update) | async-done | bytes 3145744 | tf_op jit(solution)/shard_map/all_gather | solution.py:133
  249.1 18.9 %multiply_convert_fusion.1 = (bf16[2048,768]{1,0:T(8,128)(2,1)}, f32[2048,768]{1,0:T(8,128)}, f32[2048,768]{1,0:T(8,128)}) fusion(f32[768]{0:T(1024)S(1)} %convert_element_type.173, bf16[2048,768]{1,0:T(8,128)(2,1)} %all-gather.12.cloned.1.call-done, bf16[768,768]{1,0:T(8,128)(2,1)} %all-gather.14.cloned.1.call-done), kind=kOutput, calls=%fused_computation.48 | convolution fusion | flops 2519728128 | bytes 20057088 | tf_op jit(solution)/shard_map/dot_general | solution.py:134
  268.0 24.2 %all-gather.16.cloned.1.call-done = bf16[768,768]{0,1:T(8,128)(2,1)} async-done(((bf16[768,96]{0,1:T(8,128)(2,1)}), bf16[768,768]{0,1:T(8,128)(2,1)}) %all-gather.16.cloned.1.call-update) | async-done | bytes 1179664 | tf_op jit(solution)/shard_map/all_gather | solution.py:93
  292.2 6.5 convolution_convert_fusion.2
  299.2 36.4 %reduce-scatter.18.cloned.1.call-done = bf16[512,768]{1,0:T(8,128)(2,1)} async-done(((bf16[2048,768]{1,0:T(8,128)(2,1)}), bf16[512,768]{1,0:T(8,128)(2,1)}) %reduce-scatter.18.cloned.1.call-update) | async-done | bytes 786448 | tf_op jit(solution)/shard_map/reduce_scatter | solution.py:140
  341.5 28.6 %all-gather.18.cloned.1.call-done = bf16[2048,768]{1,0:T(8,128)(2,1)} async-done(((bf16[512,768]{1,0:T(8,128)(2,1)}), bf16[2048,768]{1,0:T(8,128)(2,1)}) %all-gather.18.cloned.1.call-update) | async-done | bytes 3145744 | tf_op jit(solution)/shard_map/all_gather | solution.py:160
  370.1 11.2 %convert_reduce_fusion = (f32[768]{0:T(1024)}, bf16[2048,768]{1,0:T(8,128)(2,1)S(1)}) fusion(f32[2048,768]{1,0:T(8,128)} %get-tuple-element.239, f32[2048,768]{1,0:T(8,128)} %get-tuple-element.254, f32[768]{0:T(1024)S(1)} %convert_element_type.173, bf16[2048,768]{1,0:T(8,128)(2,1)} %all-gather.18.cloned.1.call-done, ...), kind=kOutput, calls=%fused_computation.46 | convolution fusion | flops 2442657024 | bytes 20060160 | tf_op jit(solution)/shard_map/dot_general | solution.py:34
  383.0 4.1 convolution_convert_fusion.1
  387.1 38.0 %reduce-scatter.20.cloned.1.call-done = bf16[512,768]{1,0:T(8,128)(2,1)} async-done(((bf16[2048,768]{1,0:T(8,128)(2,1)}), bf16[512,768]{1,0:T(8,128)(2,1)}) %reduce-scatter.20.cloned.1.call-update) | async-done | bytes 786448 | tf_op jit(solution)/shard_map/reduce_scatter | solution.py:167
  425.1 3.2 multiply_reduce_fusion.1
  431.8 6.6 convolution_convert_fusion.4
  438.4 7.2 convolution_convert_fusion.5
  445.7 14.7 %all-gather.20.cloned.1.call-done = bf16[2048,768]{1,0:T(8,128)(2,1)} async-done(((bf16[512,768]{1,0:T(8,128)(2,1)}), bf16[2048,768]{1,0:T(8,128)(2,1)}) %all-gather.20.cloned.1.call-update) | async-done | bytes 3145744 | tf_op jit(solution)/shard_map/all_gather | solution.py:178
  463.5 132.5 %while.27 = (s32[]{:T(128)}, bf16[4,512,3,64]{1,3,2,0:T(8,128)(2,1)}, f32[4,2048,3,64]{1,3,2,0:T(8,128)}, f32[4,2048,3,64]{1,3,2,0:T(8,128)}, s32[4]{0:T(128)S(1...) while((s32[]{:T(128)}, ...), condition=%wide.region_16.17_spmd, body=%wide.region_14.16_spmd.sunk | while | flops 2061990400 | bytes 153545232 | solution.py:215
  470.8 4.6 fusion.128
  475.4 5.8 multiply_reduce_fusion.7
  481.2 6.2 multiply_convert_fusion.3
  487.3 5.8 fusion.126
  493.2 3.6 fusion.127
  503.9 4.6 fusion.128
  508.5 5.8 multiply_reduce_fusion.7
  514.3 6.2 multiply_convert_fusion.3
  520.5 5.8 fusion.126
  526.3 3.5 fusion.127
  536.9 4.6 fusion.128
  541.6 5.8 multiply_reduce_fusion.7
  547.3 6.2 multiply_convert_fusion.3
  553.5 5.8 fusion.126
  559.3 3.5 fusion.127
  570.0 4.6 fusion.128
  574.6 5.8 multiply_reduce_fusion.7
  580.3 6.2 multiply_convert_fusion.3
  586.5 5.8 fusion.126
  592.3 3.5 fusion.127
  596.0 3.5 reduce_sum.202
  599.5 3.6 reduce_sum.201
  604.8 3.9 fusion.52
  617.5 6.0 convolution_convert_fusion
  629.2 40.0 %all-reduce = (f32[4,1152]{1,0:T(4,128)S(1)}, f32[6,768]{1,0:T(8,128)S(1)}) all-reduce(f32[4,1152]{1,0:T(4,128)S(1)} %broadcast_multiply_fusion, f32[6,768]{1,0:T(8,128)S(1)} %stack.27), channel_id=1, replica_groups=mesh['dp'=8,'tensor'=4] {'dp','tensor'}, use_global_device_ids=true, to_apply=%region_24.25 | all-reduce | flops 9216 | bytes 73728 | tf_op jit(solution)/shard_map/psum | solution.py:284
  673.0 62.1 %reduce-scatter.34.cloned.1.call-done = bf16[96,192]{1,0:T(8,128)(2,1)} async-done(((bf16[768,192]{1,0:T(8,128)(2,1)}), bf16[96,192]{1,0:T(8,128)(2,1)}) %reduce-scatter.34.cloned.1.call-update) | async-done | bytes 36880
  736.7 62.0 %reduce-scatter.30.cloned.1.call-done = bf16[96,192]{1,0:T(8,128)(2,1)} async-done(((bf16[768,192]{1,0:T(8,128)(2,1)}), bf16[96,192]{1,0:T(8,128)(2,1)}) %reduce-scatter.30.cloned.1.call-update) | async-done | bytes 36880
  800.4 61.9 %reduce-scatter.28.cloned.1.call-done = bf16[96,192]{1,0:T(8,128)(2,1)} async-done(((bf16[768,192]{1,0:T(8,128)(2,1)}), bf16[96,192]{1,0:T(8,128)(2,1)}) %reduce-scatter.28.cloned.1.call-update) | async-done | bytes 36880
  864.0 37.7 %reduce-scatter.22.cloned.1.call-done = bf16[512,768]{1,0:T(8,128)(2,1)} async-done(((bf16[2048,768]{1,0:T(8,128)(2,1)}), bf16[512,768]{1,0:T(8,128)(2,1)}) %reduce-scatter.22.cloned.1.call-update) | async-done | bytes 786448 | tf_op jit(solution)/shard_map/reduce_scatter | solution.py:238
  (271 shorter events, 75.0 us)
Async XLA Ops:
  7.2 99.7 %all-gather.8.cloned.1.call-start = ((), (), s32[]{:S(2)}) async-start(), calls=%async_computation.10 | async-start | bytes 3932160 | tf_op jit(solution)/shard_map/all_gather | solution.py:103
  7.9 196.4 %all-gather.10.cloned.1.call-start = ((), (), s32[]{:S(2)}) async-start(), calls=%async_computation.11 | async-start | bytes 1622016 | tf_op jit(solution)/shard_map/all_gather | solution.py:95
  8.7 212.8 %all-gather.14.cloned.1.call-start = ((), (), s32[]{:S(2)}) async-start(), calls=%async_computation.13 | async-start | bytes 1327104 | tf_op jit(solution)/shard_map/all_gather | solution.py:92
  43.9 63.0 %copy-start.19 = (bf16[768,192]{1,0:T(8,128)(2,1)}, bf16[768,192]{1,0:T(8,128)(2,1)S(1)}, u32[]{:S(2)}) copy-start(bf16[768,192]{1,0:T(8,128)(2,1)S(1)} %all_gather.30) | copy-start | bytes 884740
  75.2 31.7 %copy-start.21 = (bf16[768,192]{1,0:T(8,128)(2,1)}, bf16[768,192]{1,0:T(8,128)(2,1)S(1)}, u32[]{:S(2)}) copy-start(bf16[768,192]{1,0:T(8,128)(2,1)S(1)} %all_gather.31) | copy-start | bytes 884740
  106.9 4.6 copy-start.23
  112.3 92.0 %copy-start.29 = (bf16[768]{0:T(1024)(128)(2,1)S(1)}, bf16[768]{0:T(1024)(128)(2,1)}, u32[]{:S(2)}) copy-start(bf16[768]{0:T(1024)(128)(2,1)} %param.31) | copy-start | bytes 4612
  112.3 92.0 %copy-start.30 = (bf16[768]{0:T(1024)(128)(2,1)S(1)}, bf16[768]{0:T(1024)(128)(2,1)}, u32[]{:S(2)}) copy-start(bf16[768]{0:T(1024)(128)(2,1)} %param.32) | copy-start | bytes 4612
  112.3 92.1 %copy-start.31 = (bf16[768]{0:T(1024)(128)(2,1)S(1)}, bf16[768]{0:T(1024)(128)(2,1)}, u32[]{:S(2)}) copy-start(bf16[768]{0:T(1024)(128)(2,1)} %param.30) | copy-start | bytes 4612
  200.5 15.1 %copy-start.9 = (bf16[2048,3,64]{0,2,1:T(8,128)(2,1)}, bf16[2048,3,64]{0,2,1:T(8,128)(2,1)S(1)}, u32[]{:S(2)}) copy-start(bf16[2048,3,64]{0,2,1:T(8,128)(2,1)S(1)} %get-tuple-element.483) | copy-start | bytes 2359300
  200.5 15.1 %all-to-all-start = ((bf16[4,512,192]{1,2,0:T(8,128)(2,1)}), bf16[4,512,192]{1,2,0:T(8,128)(2,1)S(1)}, u32[]{:S(2)}, u32[]{:S(2)}) async-start(bf16[4,512,192]{1,2,0:T(8,128)(2,1)} %bitcast.16), calls=%async_computation | async-start | bytes 1572864 | tf_op jit(solution)/shard_map/all_to_all | solution.py:126
  204.1 45.0 %all-gather.12.cloned.1.call-start = ((), (), s32[]{:S(2)}) async-start(), calls=%async_computation.12 | async-start | bytes 3932160 | tf_op jit(solution)/shard_map/all_gather | solution.py:133
  216.6 4.8 copy-start.32
  220.8 71.4 %all-gather.16.cloned.1.call-start = ((), (), s32[]{:S(2)}) async-start(), calls=%async_computation.14 | async-start | bytes 1327104 | tf_op jit(solution)/shard_map/all_gather | solution.py:93
  221.4 114.3 %reduce-scatter.18.cloned.1.call-start = ((), (), s32[]{:S(2)}) async-start(), calls=%async_computation.15 | async-start | bytes 3932160 | tf_op jit(solution)/shard_map/reduce_scatter | solution.py:140
  292.2 7.0 copy-start.33
  292.2 7.0 copy-start.34
  292.2 7.1 copy-start.35
  298.7 71.4 %all-gather.18.cloned.1.call-start = ((), (), s32[]{:S(2)}) async-start(), calls=%async_computation.16 | async-start | bytes 3932160 | tf_op jit(solution)/shard_map/all_gather | solution.py:160
  341.5 83.7 %reduce-scatter.20.cloned.1.call-start = ((), (), s32[]{:S(2)}) async-start(), calls=%async_computation.17 | async-start | bytes 3932160 | tf_op jit(solution)/shard_map/reduce_scatter | solution.py:167
  370.1 12.8 %copy-start.36 = (bf16[768,768]{1,0:T(8,128)(2,1)S(1)}, bf16[768,768]{1,0:T(8,128)(2,1)}, u32[]{:S(2)}) copy-start(bf16[768,768]{1,0:T(8,128)(2,1)} %all-gather.14.cloned.1.call-done) | copy-start | bytes 3538948
  387.1 73.3 %all-gather.20.cloned.1.call-start = ((), (), s32[]{:S(2)}) async-start(), calls=%async_computation.18 | async-start | bytes 3932160 | tf_op jit(solution)/shard_map/all_gather | solution.py:178
  431.7 191.9 %reduce-scatter.26.cloned.1.call-start = ((), (), s32[]{:S(2)}) async-start(), calls=%async_computation.21 | async-start | bytes 1327104 | tf_op jit(solution)/shard_map/reduce_scatter | solution.py:267
  438.3 187.0 %reduce-scatter.24.cloned.1.call-start = ((), (), s32[]{:S(2)}) async-start(), calls=%async_computation.20 | async-start | bytes 1327104 | tf_op jit(solution)/shard_map/reduce_scatter | solution.py:264
  445.7 225.7 %reduce-scatter.32.cloned.1.call-start = ((), (), s32[]{:S(2)}) async-start(), calls=%async_computation.24 | async-start | bytes 442368
  463.7 7.1 copy-start.2
  463.7 7.1 copy-start.4
  463.7 7.1 copy-start.14
  487.3 5.8 copy-start
  493.2 3.6 copy-start.3
  493.2 3.6 copy-start.5
  493.2 3.6 copy-start.15
  496.8 7.1 copy-start.2
  496.8 7.1 copy-start.4
  496.8 7.1 copy-start.14
  520.5 5.8 copy-start
  526.3 3.5 copy-start.15
  529.8 7.1 copy-start.2
  529.8 7.1 copy-start.4
  529.8 7.1 copy-start.14
  553.5 5.8 copy-start
  559.3 3.5 copy-start.3
  559.3 3.5 copy-start.5
  559.3 3.5 copy-start.15
  562.8 7.1 copy-start.2
  562.8 7.1 copy-start.4
  562.8 7.1 copy-start.14
  586.5 5.8 copy-start
  592.3 3.5 copy-start.3
  592.3 3.5 copy-start.5
  592.3 3.5 copy-start.15
  599.5 3.6 copy-start.10
  609.7 125.5 %reduce-scatter.34.cloned.1.call-start = ((), (), s32[]{:S(2)}) async-start(), calls=%async_computation.25 | async-start | bytes 442368
  611.5 6.0 copy-start.20
  611.5 6.0 copy-start.22
  615.4 183.4 %reduce-scatter.30.cloned.1.call-start = ((), (), s32[]{:S(2)}) async-start(), calls=%async_computation.23 | async-start | bytes 442368
  616.4 246.0 %reduce-scatter.28.cloned.1.call-start = ((), (), s32[]{:S(2)}) async-start(), calls=%async_computation.22 | async-start | bytes 442368
  617.4 6.1 copy-start.25
  617.4 6.1 copy-start.24
  617.4 11.0 %copy-start.27 = (f32[768]{0:T(1024)S(1)}, f32[768]{0:T(1024)}, u32[]{:S(2)}) copy-start(f32[768]{0:T(1024)} %get-tuple-element.180) | copy-start | bytes 9220
  617.4 11.0 %copy-start.26 = (f32[768]{0:T(1024)S(1)}, f32[768]{0:T(1024)}, u32[]{:S(2)}) copy-start(f32[768]{0:T(1024)} %get-tuple-element.181) | copy-start | bytes 9220
  617.5 284.3 %reduce-scatter.22.cloned.1.call-start = ((), (), s32[]{:S(2)}) async-start(), calls=%async_computation.19 | async-start | bytes 3932160 | tf_op jit(solution)/shard_map/reduce_scatter | solution.py:238
  623.5 5.5 copy-start.28
  623.5 278.3 %copy-start.7 = (f32[512,768]{1,0:T(8,128)S(1)}, f32[512,768]{1,0:T(8,128)}, u32[]{:S(2)}) copy-start(f32[512,768]{1,0:T(8,128)} %copy-done.6) | copy-start | bytes 4718596
  (15 other events, 33.9 us)
Sparse Core Ops, SparseCore 0:
  9.6 31.2 all-gather.7
  43.7 56.0 all-gather.9
  102.0 40.2 all-gather.13
  220.9 28.1 all-gather.11
  251.1 41.0 all-gather.15
  298.9 36.7 reduce-scatter.17
  341.6 28.5 all-gather.17
  387.2 37.9 reduce-scatter.19
  431.8 28.5 all-gather.19
  463.6 64.1 reduce-scatter.25
  531.3 63.0 reduce-scatter.23
  609.8 61.5 reduce-scatter.31
  674.7 60.4 reduce-scatter.33
  738.3 60.4 reduce-scatter.29
  801.9 60.4 reduce-scatter.27
  864.8 36.9 reduce-scatter.21
where the time goes:
time: 919 us; the launch traced here: 911 us
  waiting for transfers between devices  400 us (44%)
  matrix products  221 us (24%)
  blocking collectives  136 us (15%)
  other arithmetic  85.2 us (9%)
  local copies, waits for them, and re-layouts  34.3 us (4%)
  between operations  14.8 us (2%)
  loops' own time  14 us (2%)
    unnamed x20, waiting for transfers between devices  189 us
    psum x1, blocking collectives, body(): head_table, row_table = lax.psum((head_table, row_table), ('dp', 'tensor'))  40 us
    reduce_scatter x1, waiting for transfers between devices, body(): lax.psum_scatter(times_transpose(hidden_grad, full_hidden).astype(jnp.bfl...  38 us
    reduce_scatter x1, waiting for transfers between devices, body(): lax.psum_scatter(times_transpose(projected_grad, joined).astype(jnp.bfloa...  37.7 us
    reduce_scatter x1, waiting for transfers between devices, body(): lax.psum_scatter(jnp.dot(activation, full_down, preferred_element_type=jn...  36.4 us
    dot_general x8, matrix products, block_scores(): jnp.einsum('qhd,khd->hqk', query_block, keys, preferred_element_type=jnp....  35.9 us
    all_gather x1, blocking collectives, body(): lax.all_gather(query_weight, 'dp', axis=0, tiled=True)  33.2 us
    all_gather x1, blocking collectives, body(): lax.all_gather(value_weight, 'dp', axis=0, tiled=True)  31.7 us
  transfers between devices with their start and end apart: 17, of which 12 were waited for; matrix products, arithmetic and copies ran while one was open for 33% of the time, Pallas kernels for 0%

commit v1 on v0

v1 whole, which is shorter than its diff:
```python
import functools

import jax
import jax.numpy as jnp
from jax import lax
from jax.experimental import pallas as pl
from jax.experimental.pallas import tpu as pltpu
from jax.sharding import PartitionSpec as P

HEAD = 64
EPSILON = 1e-06
NEGATIVE = -1e30
PARTS = 4
MESH = pl.DeviceIdType.MESH
VMEM_LIMIT = 60000 * 1024
F32 = jnp.float32
BF16 = jnp.bfloat16


def dot(left, right):
    return lax.dot_general(left, right, (((1,), (0,)), ((), ())), preferred_element_type=F32)


def dot_t(left, right):
    return lax.dot_general(left, right, (((1,), (1,)), ((), ())), preferred_element_type=F32)


def vmem():
    return pl.BlockSpec(memory_space=pltpu.VMEM)


def smem():
    return pl.BlockSpec(memory_space=pltpu.SMEM)


def anywhere():
    return pl.BlockSpec(memory_space=pl.ANY)


def ring_place(index, shards):
    if shards == 8:
        z, x = index // 2, index % 2
        return z + x * (7 - 2 * z)
    return index


def ring_index(place, shards):
    if shards == 8:
        x = place // 4
        z = place + x * (7 - 2 * place)
        return z * 2 + x
    return place


class Links:
    def __init__(self, shards, send, recv, local=None):
        self.shards = shards
        self.send, self.recv, self.local = send, recv, local
        self.used, self.used_local = 0, 0
        self.sent, self.copies = [], []
        self.dp = lax.axis_index("dp")
        self.part = lax.axis_index("tensor")
        self.core = self.part % 2
        self.row = self.part // 2
        self.other_core = self.part + 1 - 2 * self.core
        self.other_row = (self.part + 2) % PARTS
        self.place = ring_place(self.dp, shards)
        self.right = self.at(1)
        self.left = self.at(-1)

    def at(self, offset):
        return ring_index((self.place + offset + self.shards) % self.shards, self.shards)

    def barrier(self, tensor=True, ring=True, diagonal=False, cube=False):
        partners = []
        if tensor:
            partners += [{"tensor": self.other_core}, {"tensor": self.other_row}]
        if diagonal:
            partners += [{"tensor": (self.other_core + 2) % PARTS}]
        if ring:
            partners += [{"dp": self.right}, {"dp": self.left}]
        if cube:
            partners += [{"dp": index} for index in self.cube()]
        semaphore = pltpu.get_barrier_semaphore()
        for partner in partners:
            pl.semaphore_signal(semaphore, inc=1, device_id=partner, device_id_type=MESH)
        pl.semaphore_wait(semaphore, len(partners))

    def cube(self):
        found, step = [], 1
        while step < self.shards:
            found.append(self.dp + step - 2 * step * (self.dp // step % 2))
            step *= 2
        return found

    def number(self):
        self.used += 1
        return self.used - 1

    def copy(self, number, source, target, partner):
        return pltpu.make_async_remote_copy(
            src_ref=source,
            dst_ref=target,
            send_sem=self.send.at[number],
            recv_sem=self.recv.at[number],
            device_id=partner,
            device_id_type=MESH,
        )

    def start(self, number, source, target, partner):
        copy = self.copy(number, source, target, partner)
        copy.start()
        self.sent.append(copy)

    def arrive(self, number, target, partner):
        self.copy(number, target, target, partner).wait_recv()

    def keep(self, source, target):
        copy = pltpu.make_async_copy(source, target, self.local.at[self.used_local])
        self.used_local += 1
        copy.start()
        self.copies.append(copy)

    def finish(self):
        for copy in self.sent:
            copy.wait_send()
        for copy in self.copies:
            copy.wait()


class RingGather:
    def __init__(self, links, rows, own, slot):
        self.links, self.own, self.slot, self.rows = links, own, slot, rows
        self.half = links.shards // 2
        self.split = rows % 32 == 0
        self.numbers = {}

    def part(self, ref, step, way):
        if step < self.half or not self.split:
            return ref
        start = 0 if way > 0 else self.rows // 2
        return ref.at[pl.ds(start, self.rows // 2)]

    def ways(self, step):
        return (1, -1) if step < self.half or self.split else (1,)

    def send(self, step):
        for way in self.ways(step):
            j = self.links.at(-way * (step - 1))
            source = self.own if step == 1 else self.slot(j)
            number = self.links.number()
            self.numbers[step, way] = number
            partner = {"dp": self.links.right if way > 0 else self.links.left}
            self.links.start(
                number, self.part(source, step, way), self.part(self.slot(j), step, way), partner
            )

    def arrive(self, step):
        found = []
        for way in self.ways(step):
            j = self.links.at(-way * step)
            ref = self.part(self.slot(j), step, way)
            self.links.arrive(self.numbers[step, way], ref, {"dp": self.links.left})
            found.append((j, way))
        return found


def gather_copies(shards):
    return 40 + 26 * shards


def gather_kernel(
    shards,
    x_ref,
    joined_ref,
    hidden_ref,
    down_ref,
    out_ref,
    bias_ref,
    all_x,
    all_joined,
    all_hidden,
    all_down,
    all_out,
    all_bias,
    send,
    recv,
    local,
):
    links = Links(shards, send, recv, local)
    me, part = links.dp, links.part
    across, beside = {"tensor": links.other_row}, {"tensor": links.other_core}
    far = links.other_row
    links.barrier()
    rows = hidden_ref.shape[0]
    half = shards // 2
    later = []

    def share(make, source_part, ref_of):
        number = links.number()
        ref = make(source_part)
        links.start(number, ref_of if ref_of is not None else ref, ref, beside)
        partner_part = source_part + 1 - 2 * links.core
        later.append((number, make(partner_part)))

    joined = RingGather(links, rows, joined_ref, lambda j: all_joined.at[j])
    hidden = RingGather(links, rows, hidden_ref, lambda j: all_hidden.at[part, j])
    joined.send(1)
    down_number, out_number, x_number, bias_number = (links.number() for _ in range(4))
    links.start(bias_number, bias_ref, all_bias.at[part], across)
    links.start(down_number, down_ref, all_down.at[part, me], across)
    links.start(out_number, out_ref, all_out.at[part, me], across)
    links.start(x_number, x_ref, all_x.at[part], across)
    down_own = RingGather(links, rows, down_ref, lambda j: all_down.at[part, j])
    out_own = RingGather(links, rows, out_ref, lambda j: all_out.at[part, j])
    down_own.send(1)
    hidden.send(1)
    out_own.send(1)
    hidden_numbers = {}

    def hidden_across(j_send, j_get, key, piece):
        number = links.number()
        source = hidden_ref if key == 0 else piece(all_hidden.at[part, j_send])
        links.start(number, source, piece(all_hidden.at[part, j_send]), across)
        hidden_numbers[key] = (number, piece(all_hidden.at[far, j_get]), j_get, piece)

    whole = lambda ref: ref
    hidden_across(me, me, 0, whole)
    links.keep(x_ref, all_x.at[part])
    links.keep(joined_ref, all_joined.at[me])
    links.keep(hidden_ref, all_hidden.at[part, me])
    links.keep(down_ref, all_down.at[part, me])
    links.keep(out_ref, all_out.at[part, me])
    links.keep(bias_ref, all_bias.at[part])
    share(lambda t: all_bias.at[t], part, bias_ref)
    share(lambda t: all_x.at[t], part, x_ref)
    share(lambda t: all_hidden.at[t, me], part, hidden_ref)
    share(lambda t: all_down.at[t, me], part, down_ref)
    share(lambda t: all_out.at[t, me], part, out_ref)

    links.arrive(down_number, all_down.at[far, me], across)
    down_far = RingGather(links, rows, all_down.at[far, me], lambda j: all_down.at[far, j])
    down_far.send(1)
    share(lambda t: all_down.at[t, me], far, None)
    links.arrive(out_number, all_out.at[far, me], across)
    out_far = RingGather(links, rows, all_out.at[far, me], lambda j: all_out.at[far, j])
    out_far.send(1)
    share(lambda t: all_out.at[t, me], far, None)

    def pieces(stream, step, way):
        return lambda ref: stream.part(ref, step, way)

    def far_hidden(key):
        number, ref, j, piece = hidden_numbers[key]
        links.arrive(number, ref, across)
        share(lambda t: piece(all_hidden.at[t, j]), far, None)

    for step in range(1, half + 1):
        for stream in (joined, hidden, down_own, down_far, out_own, out_far):
            arrived = stream.arrive(step)
            if step < half:
                stream.send(step + 1)
            for j, way in arrived:
                piece = pieces(stream, step, way)
                if stream is hidden:
                    hidden_across(j, j, (step, way), piece)
                    share(lambda t, j=j, piece=piece: piece(all_hidden.at[t, j]), part, None)
                elif stream is not joined:
                    ref = all_down if stream in (down_own, down_far) else all_out
                    owner = part if stream in (down_own, out_own) else far
                    share(lambda t, j=j, piece=piece, ref=ref: piece(ref.at[t, j]), owner, None)
        if step == 1:
            links.arrive(x_number, all_x.at[far], across)
            share(lambda t: all_x.at[t], far, None)
            links.arrive(bias_number, all_bias.at[far], across)
            share(lambda t: all_bias.at[t], far, None)
            far_hidden(0)
        else:
            for way in hidden.ways(step - 1):
                far_hidden((step - 1, way))
    for way in hidden.ways(half):
        far_hidden((half, way))
    for number, ref in later:
        links.arrive(number, ref, beside)
    links.finish()
    assert links.used <= gather_copies(shards), links.used


def gather(shards, x, joined, hidden, down, out, bias):
    shape = lambda *dims: jax.ShapeDtypeStruct(dims, BF16)
    count = gather_copies(shards)
    return pl.pallas_call(
        functools.partial(gather_kernel, shards),
        out_shape=(
            shape(PARTS, *x.shape),
            shape(shards, *joined.shape),
            shape(PARTS, shards, *hidden.shape),
            shape(PARTS, shards, *down.shape),
            shape(PARTS, shards, *out.shape),
            jax.ShapeDtypeStruct((PARTS, *bias.shape), F32),
        ),
        in_specs=[vmem()] * 6,
        out_specs=[anywhere()] * 6,
        scratch_shapes=[
            pltpu.SemaphoreType.DMA((count,)),
            pltpu.SemaphoreType.DMA((count,)),
            pltpu.SemaphoreType.DMA((6,)),
        ],
        compiler_params=pltpu.CompilerParams(
            collective_id=0, has_side_effects=True, vmem_limit_bytes=VMEM_LIMIT
        ),
        name="gather",
    )(x, joined, hidden, down, out, bias)


def exchange_kernel(shards, source, target, send, recv):
    links = Links(shards, send, recv)
    part = links.part
    diagonal = (links.other_core + 2) % PARTS
    links.barrier(ring=False, diagonal=True)
    partners = (links.other_row, diagonal, links.other_core)
    for number, partner in enumerate(partners):
        links.start(number, source.at[partner], target.at[part], {"tensor": partner})
    target[part] = source[part]
    for number, partner in enumerate(partners):
        links.arrive(number, target.at[partner], {"tensor": partner})
    links.finish()


def exchange(shards, identity, pieces):
    return pl.pallas_call(
        functools.partial(exchange_kernel, shards),
        out_shape=jax.ShapeDtypeStruct(pieces.shape, pieces.dtype),
        in_specs=[vmem()],
        out_specs=vmem(),
        scratch_shapes=[pltpu.SemaphoreType.DMA((3,)), pltpu.SemaphoreType.DMA((3,))],
        compiler_params=pltpu.CompilerParams(collective_id=identity, has_side_effects=True),
        name=f"exchange_{identity}",
    )(pieces)


def plus(left, right):
    return (left.astype(F32) + right.astype(F32)).astype(BF16)


class RingSum:
    def __init__(self, links, rows, term, slots):
        self.links, self.term, self.slots, self.rows = links, term, slots, rows
        self.half = links.shards // 2
        self.split = rows % 32 == 0
        self.numbers = {}

    def part(self, ref, step, way):
        if step > 1 or not self.split:
            return ref
        start = 0 if way > 0 else self.rows // 2
        return ref.at[pl.ds(start, self.rows // 2)]

    def ways(self, step):
        return (1, -1) if step > 1 or self.split else (1,)

    def slot(self, step, way):
        return self.slots.at[step - 1, 0 if way > 0 else 1]

    def send(self, step):
        for way in self.ways(step):
            number = self.links.number()
            self.numbers[step, way] = number
            partner = {"dp": self.links.right if way > 0 else self.links.left}
            j = self.links.at(way * (self.half - step + 1))
            if step == 1:
                source = self.part(self.term(j), 1, way)
            else:
                source = self.slot(step - 1, way)
            self.links.start(
                number, source, self.part(self.slot(step, way), step, way), partner
            )

    def arrive(self, step):
        for way in self.ways(step):
            ref = self.part(self.slot(step, way), step, way)
            self.links.arrive(self.numbers[step, way], ref, {"dp": self.links.left})
        if step == self.half:
            return
        for way in (1, -1):
            j = self.links.at(way * (self.half - step))
            term, slot = self.term(j), self.slot(step, way)
            if way not in self.ways(step):
                slot[...] = term[...]
            elif step == 1 and self.split:
                cut = self.rows // 2
                got, other = (0, cut) if way > 0 else (cut, 0)
                slot[pl.ds(got, cut)] = plus(slot[pl.ds(got, cut)], term[pl.ds(got, cut)])
                slot[pl.ds(other, cut)] = term[pl.ds(other, cut)]
            else:
                slot[...] = plus(slot[...], term[...])

    def total(self):
        own = self.term(self.links.dp)[...].astype(F32)
        total = own + self.slot(self.half, 1)[...].astype(F32)
        if self.half > 1 or self.split:
            total = total + self.slot(self.half, -1)[...].astype(F32)
        return total


def reduce_copies(shards):
    return 40 + 6 * shards


def reduce_kernel(
    shards,
    rows_ref,
    base_ref,
    joined_ref,
    hidden_ref,
    down_ref,
    out_ref,
    small_ref,
    rows_out,
    joined_out,
    hidden_out,
    down_out,
    out_out,
    small_out,
    rows_two,
    rows_far,
    hidden_two,
    hidden_far,
    down_two,
    out_two,
    joined_slots,
    hidden_slots,
    down_slots,
    out_slots,
    down_pair,
    out_pair,
    small_slots,
    small_sums,
    send,
    recv,
):
    links = Links(shards, send, recv)
    core, row = links.core, links.row
    across, beside = {"tensor": links.other_row}, {"tensor": links.other_core}
    links.barrier(cube=True)
    half = shards // 2
    rows = joined_ref.shape[1]

    beside_numbers = {}

    def to_core(name, array, slots, y):
        number = links.number()
        beside_numbers[name, y] = number
        links.start(number, array.at[2 * y + 1 - core], slots.at[y], beside)

    joined = RingSum(links, rows, lambda j: joined_ref.at[j], joined_slots)
    joined.send(1)
    for y in range(2):
        to_core("down", down_ref, down_two, y)
    for y in range(2):
        to_core("out", out_ref, out_two, y)
    for y in range(2):
        to_core("hidden", hidden_ref, hidden_two, y)
    for y in range(2):
        to_core("rows", rows_ref, rows_two, y)

    def add_core(name, array, slots, y, count):
        links.arrive(beside_numbers[name, y], slots.at[y], beside)

        def one(i, carry):
            slots[y, i] = plus(slots[y, i], array[2 * y + core, i])
            return carry

        lax.fori_loop(0, count, one, 0)

    small_numbers = []

    def small_send(step, source):
        number = links.number()
        small_numbers.append(number)
        links.start(number, source, small_slots.at[step], small_partners[step])

    small_partners = [{"dp": index} for index in links.cube()] + [beside, across]
    small_send(0, small_ref)

    def small_step(step):
        links.arrive(small_numbers[step], small_slots.at[step], small_partners[step])
        mine = small_ref[...] if step == 0 else small_sums[step - 1]
        got = small_slots[step]
        if step >= len(small_partners) - 2:
            common = lax.broadcasted_iota(jnp.int32, got.shape, 0) < 10
            got = jnp.where(common, got, 0.0)
        total = mine + got
        if step == len(small_partners) - 1:
            small_out[...] = total
        else:
            small_sums[step] = total
            small_send(step + 1, small_sums.at[step])

    down_rings, out_rings = [], []
    for y in range(2):
        add_core("down", down_ref, down_two, y, shards)
        ring = RingSum(links, rows, lambda j, y=y: down_two.at[y, j], down_slots.at[y])
        ring.send(1)
        down_rings.append(ring)
    for y in range(2):
        add_core("out", out_ref, out_two, y, shards)
        ring = RingSum(links, rows, lambda j, y=y: out_two.at[y, j], out_slots.at[y])
        ring.send(1)
        out_rings.append(ring)
    joined.arrive(1)
    joined.send(2)
    for y in range(2):
        add_core("hidden", hidden_ref, hidden_two, y, shards)
    hidden_number = links.number()
    links.start(hidden_number, hidden_two.at[1 - row], hidden_far, across)
    for y in range(2):
        add_core("rows", rows_ref, rows_two, y, rows_ref.shape[1])
    rows_number = links.number()
    links.start(rows_number, rows_two.at[1 - row], rows_far, across)
    small_step(0)
    for ring in down_rings + out_rings:
        ring.arrive(1)
        ring.send(2)
    if half > 2:
        joined.arrive(2)
        joined.send(3)
    links.arrive(hidden_number, hidden_far, across)

    def one(i, carry):
        hidden_far[i] = plus(hidden_far[i], hidden_two[row, i])
        return carry

    lax.fori_loop(0, shards, one, 0)
    hidden = RingSum(links, rows, lambda j: hidden_far.at[j], hidden_slots)
    hidden.send(1)
    small_step(1)
    for step in range(2, half + 1):
        for ring in down_rings + out_rings:
            ring.arrive(step)
            if step < half:
                ring.send(step + 1)
        if step + 1 <= half:
            joined.arrive(step + 1)
            if step + 1 < half:
                joined.send(step + 2)
        if step < len(small_partners):
            small_step(step)
        hidden.arrive(step - 1)
        hidden.send(step)
    for step in range(half + 1, len(small_partners)):
        small_step(step)
    links.arrive(rows_number, rows_far, across)

    def last(i, carry):
        rows_out[i] = (
            base_ref[i]
            + rows_two[row, i].astype(F32)
            + rows_far[i].astype(F32)
        )
        return carry

    lax.fori_loop(0, rows_out.shape[0], last, 0)
    pairs = []
    for rings, pair, result in ((down_rings, down_pair, down_out), (out_rings, out_pair, out_out)):
        for y in range(2):
            pair[y] = rings[y].total().astype(BF16)
        number = links.number()
        links.start(number, pair.at[1 - row], pair.at[2], across)
        pairs.append((number, pair, result))
    joined_out[...] = joined.total()
    hidden.arrive(half)
    hidden_out[...] = hidden.total()
    for number, pair, result in pairs:
        links.arrive(number, pair.at[2], across)
        result[...] = pair[row].astype(F32) + pair[2].astype(F32)
    links.finish()
    assert links.used <= reduce_copies(shards), links.used


def reduce(shards, rows, base, joined, hidden, down, out, small):
    half = shards // 2
    count = reduce_copies(shards)
    stages = (shards - 1).bit_length() + 2
    scratch = lambda *dims: pltpu.VMEM(dims, BF16)
    result = lambda *dims: jax.ShapeDtypeStruct(dims, F32)
    return pl.pallas_call(
        functools.partial(reduce_kernel, shards),
        out_shape=(
            result(*base.shape),
            result(*joined.shape[1:]),
            result(*hidden.shape[2:]),
            result(*down.shape[2:]),
            result(*out.shape[2:]),
            result(*small.shape),
        ),
        in_specs=[vmem()] * 7,
        out_specs=[vmem()] * 6,
        scratch_shapes=[
            scratch(2, *rows.shape[1:]),
            scratch(*rows.shape[1:]),
            scratch(2, *hidden.shape[1:]),
            scratch(*hidden.shape[1:]),
            scratch(2, *down.shape[1:]),
            scratch(2, *out.shape[1:]),
            scratch(half, 2, *joined.shape[1:]),
            scratch(half, 2, *hidden.shape[2:]),
            scratch(2, half, 2, *down.shape[2:]),
            scratch(2, half, 2, *out.shape[2:]),
            scratch(3, *down.shape[2:]),
            scratch(3, *out.shape[2:]),
            pltpu.VMEM((stages, *small.shape), F32),
            pltpu.VMEM((stages, *small.shape), F32),
            pltpu.SemaphoreType.DMA((count,)),
            pltpu.SemaphoreType.DMA((count,)),
        ],
        compiler_params=pltpu.CompilerParams(
            collective_id=3, has_side_effects=True, vmem_limit_bytes=VMEM_LIMIT
        ),
        name="reduce",
    )(rows, base, joined, hidden, down, out, small)


QUERY_BLOCK = 256
KEY_BLOCK = 256


def fold_rows(block):
    return block.reshape(block.shape[0] // 8, 8, block.shape[1])


def forward_kernel(
    low_ref,
    high_ref,
    x_ref,
    weight_ref,
    query_bias_ref,
    value_bias_ref,
    key_seg_ref,
    query_seg_ref,
    query_out,
    key_out,
    value_out,
    context_out,
    total_out,
    value_turned,
    score_store,
):
    heads = query_out.shape[0]
    width = heads * HEAD
    scale = HEAD ** (-0.5)
    rows = x_ref.shape[0]

    def project(i, carry):
        at = pl.ds(pl.multiple_of(i * QUERY_BLOCK, QUERY_BLOCK), QUERY_BLOCK)
        all_three = dot(x_ref[at, :], weight_ref[...])
        queries = (all_three[:, :width] + query_bias_ref[...]).astype(BF16)
        queries = (queries.astype(F32) * scale).astype(BF16)
        keys = all_three[:, width : 2 * width].astype(BF16)
        values = all_three[:, 2 * width :] + value_bias_ref[...]
        turned = jnp.transpose(values).astype(BF16)
        values = values.astype(BF16)
        for h in range(heads):
            columns = slice(h * HEAD, (h + 1) * HEAD)
            query_out[h, at, :] = queries[:, columns]
            key_out[h, at, :] = keys[:, columns]
            value_out[h, at, :] = values[:, columns]
        value_turned[:, at] = turned
        return carry

    lax.fori_loop(0, rows // QUERY_BLOCK, project, 0)

    def attend(i, carry):
        at = pl.ds(pl.multiple_of(i * QUERY_BLOCK, QUERY_BLOCK), QUERY_BLOCK)
        query_seg = query_seg_ref[:, at]
        queries = [query_out[h, at, :] for h in range(heads)]

        def scores(j, tops):
            there = pl.ds(pl.multiple_of(j * KEY_BLOCK, KEY_BLOCK), KEY_BLOCK)
            allowed = key_seg_ref[there, :] == query_seg
            found = []
            for h in range(heads):
                block = dot_t(key_out[h, there, :], queries[h])
                block = jnp.where(allowed, block, NEGATIVE)
                score_store[h, there, :] = block
                found.append(jnp.maximum(tops[h], jnp.max(fold_rows(block), axis=0)))
            return tuple(found)

        start = jnp.full((8, QUERY_BLOCK), NEGATIVE, F32)
        tops = lax.fori_loop(low_ref[i], high_ref[i], scores, (start,) * heads)
        tops = [jnp.max(top, axis=0, keepdims=True) for top in tops]

        def mix(j, state):
            there = pl.ds(pl.multiple_of(j * KEY_BLOCK, KEY_BLOCK), KEY_BLOCK)
            found = []
            for h in range(heads):
                total, mixed = state[h]
                weights = jnp.exp(score_store[h, there, :] - tops[h])
                total = total + jnp.sum(fold_rows(weights), axis=0)
                turned = value_turned[h * HEAD : (h + 1) * HEAD, there]
                mixed = mixed + dot(turned, weights.astype(BF16))
                found.append((total, mixed))
            return tuple(found)

        empty = (jnp.zeros((8, QUERY_BLOCK), F32), jnp.zeros((HEAD, QUERY_BLOCK), F32))
        state = lax.fori_loop(low_ref[i], high_ref[i], mix, (empty,) * heads)
        parts = []
        for h in range(heads):
            total = jnp.sum(state[h][0], axis=0, keepdims=True)
            parts.append(state[h][1] / total)
            total_out[h, :, at] = tops[h] + jnp.log(total)
        context_out[at, :] = jnp.transpose(jnp.concatenate(parts, axis=0)).astype(BF16)
        return carry

    lax.fori_loop(0, rows // QUERY_BLOCK, attend, 0)


def attention_forward(low, high, x, weight, query_bias, value_bias, key_seg, query_seg):
    rows = x.shape[0]
    width = weight.shape[1] // 3
    heads = width // HEAD
    per_head = jax.ShapeDtypeStruct((heads, rows, HEAD), BF16)
    return pl.pallas_call(
        forward_kernel,
        out_shape=(
            per_head,
            per_head,
            per_head,
            jax.ShapeDtypeStruct((rows, width), BF16),
            jax.ShapeDtypeStruct((heads, 1, rows), F32),
        ),
        in_specs=[smem()] * 2 + [vmem()] * 6,
        out_specs=[vmem()] * 5,
        scratch_shapes=[
            pltpu.VMEM((width, rows), BF16),
            pltpu.VMEM((heads, rows, QUERY_BLOCK), F32),
        ],
        compiler_params=pltpu.CompilerParams(vmem_limit_bytes=VMEM_LIMIT),
        name="attention_forward",
    )(low, high, x, weight, query_bias, value_bias, key_seg, query_seg)


def backward_kernel(
    low_ref,
    high_ref,
    x_ref,
    weight_ref,
    query_ref,
    key_ref,
    value_ref,
    context_ref,
    upstream_ref,
    total_ref,
    key_seg_ref,
    query_seg_ref,
    weight_out,
    x_out,
    bias_out,
    upstream_heads,
    key_turned,
    inner_rows,
    key_sum,
    value_sum,
    projected,
    weight_sum,
):
    heads = query_ref.shape[0]
    width = heads * HEAD
    scale = HEAD ** (-0.5)
    rows = x_ref.shape[0]
    steps = rows // QUERY_BLOCK

    def prepare(i, carry):
        at = pl.ds(pl.multiple_of(i * QUERY_BLOCK, QUERY_BLOCK), QUERY_BLOCK)
        upstream = upstream_ref[at, :]
        product = upstream.astype(F32) * context_ref[at, :].astype(F32)
        chooser = (
            lax.broadcasted_iota(jnp.int32, (8, width), 1) // HEAD
            == lax.broadcasted_iota(jnp.int32, (8, width), 0)
        ).astype(F32)
        inner_rows[:, at] = lax.dot_general(
            chooser,
            product,
            (((1,), (1,)), ((), ())),
            preferred_element_type=F32,
            precision=lax.Precision.HIGHEST,
        )
        for h in range(heads):
            upstream_heads[h, at, :] = upstream[:, h * HEAD : (h + 1) * HEAD]
            key_turned[h, :, at] = jnp.transpose(key_ref[h, at, :].astype(F32)).astype(BF16)
            key_sum[h, at, :] = jnp.zeros((QUERY_BLOCK, HEAD), F32)
            value_sum[h, at, :] = jnp.zeros((QUERY_BLOCK, HEAD), F32)
        return carry

    lax.fori_loop(0, steps, prepare, 0)

    def attend(i, carry):
        at = pl.ds(pl.multiple_of(i * QUERY_BLOCK, QUERY_BLOCK), QUERY_BLOCK)
        query_seg = query_seg_ref[:, at]
        inner = [inner_rows[h : h + 1, at] for h in range(heads)]
        totals = [total_ref[h, :, at] for h in range(heads)]

        def block(j, sums):
            there = pl.ds(pl.multiple_of(j * KEY_BLOCK, KEY_BLOCK), KEY_BLOCK)
            allowed = key_seg_ref[there, :] == query_seg
            found = []
            for h in range(heads):
                queries = query_ref[h, at, :]
                upstream = upstream_heads[h, at, :]
                scores = dot_t(key_ref[h, there, :], queries)
                shares = jnp.exp(jnp.where(allowed, scores, NEGATIVE) - totals[h])
                share_grad = dot_t(value_ref[h, there, :], upstream)
                score_grad = (shares * (share_grad - inner[h])).astype(BF16)
                value_sum[h, there, :] += dot(shares.astype(BF16), upstream)
                key_sum[h, there, :] += dot(score_grad, queries)
                found.append(sums[h] + dot(key_turned[h, :, there], score_grad))
            return tuple(found)

        empty = jnp.zeros((HEAD, QUERY_BLOCK), F32)
        sums = lax.fori_loop(low_ref[i], high_ref[i], block, (empty,) * heads)
        queries = jnp.transpose(jnp.concatenate(sums, axis=0)) * scale
        projected[at, :width] = queries.astype(BF16)
        return carry

    lax.fori_loop(0, steps, attend, 0)
    weight_sum[...] = jnp.zeros_like(weight_sum)
    bias_out[...] = jnp.zeros_like(bias_out)

    def finish(i, carry):
        at = pl.ds(pl.multiple_of(i * QUERY_BLOCK, QUERY_BLOCK), QUERY_BLOCK)
        for h in range(heads):
            columns = slice(width + h * HEAD, width + (h + 1) * HEAD)
            projected[at, columns] = key_sum[h, at, :].astype(BF16)
            columns = slice(2 * width + h * HEAD, 2 * width + (h + 1) * HEAD)
            projected[at, columns] = value_sum[h, at, :].astype(BF16)
        block = projected[at, :]
        bias_out[...] += jnp.sum(fold_rows(block.astype(F32)), axis=0)
        weight_sum[...] += lax.dot_general(
            x_ref[at, :], block, (((0,), (0,)), ((), ())), preferred_element_type=F32
        )
        x_out[at, :] = dot_t(block, weight_ref[...]).astype(BF16)
        return carry

    lax.fori_loop(0, steps, finish, 0)
    weight_out[...] = weight_sum[...].astype(BF16)


def attention_backward(
    low, high, x, weight, queries, keys, values, context, upstream, totals, key_seg, query_seg
):
    rows, model = x.shape
    heads = queries.shape[0]
    width = heads * HEAD
    return pl.pallas_call(
        backward_kernel,
        out_shape=(
            jax.ShapeDtypeStruct((model, 3 * width), BF16),
            jax.ShapeDtypeStruct((rows, model), BF16),
            jax.ShapeDtypeStruct((8, 3 * width), F32),
        ),
        in_specs=[smem()] * 2 + [vmem()] * 10,
        out_specs=[vmem()] * 3,
        scratch_shapes=[
            pltpu.VMEM((heads, rows, HEAD), BF16),
            pltpu.VMEM((heads, HEAD, rows), BF16),
            pltpu.VMEM((8, rows), F32),
            pltpu.VMEM((heads, rows, HEAD), F32),
            pltpu.VMEM((heads, rows, HEAD), F32),
            pltpu.VMEM((rows, 3 * width), BF16),
            pltpu.VMEM((model, 3 * width), F32),
        ],
        compiler_params=pltpu.CompilerParams(vmem_limit_bytes=VMEM_LIMIT),
        name="attention_backward",
    )(low, high, x, weight, queries, keys, values, context, upstream, totals, key_seg, query_seg)


ROW_BLOCK = 128
ROOT_HALF = 0.7071067811865476
PHI_ZERO = 0.3989422804014327


def column_sum(block):
    return jnp.sum(block, axis=0, keepdims=True)


def middle_kernel(
    context_ref,
    x_ref,
    cotangent_ref,
    out_ref,
    hidden_ref,
    down_ref,
    vectors_ref,
    hidden_bias_ref,
    layer_out,
    first_grad_out,
    context_grad_out,
    out_grad,
    hidden_grad_out,
    down_grad_out,
    small_out,
    first_norm,
    first_normed,
    first_scale,
    first_low,
    second_sum,
    activation,
    slope,
    second_low,
    turned,
    back_low,
):
    rows, model = x_ref.shape
    width = context_ref.shape[2]
    blocks = rows // ROW_BLOCK
    out_bias, first_gain, first_shift = (vectors_ref[i : i + 1, :] for i in range(3))
    down_bias, second_gain, second_shift = (vectors_ref[i : i + 1, :] for i in range(3, 6))
    small_out[...] = jnp.zeros_like(small_out)

    def span(i):
        return pl.ds(pl.multiple_of(i * ROW_BLOCK, ROW_BLOCK), ROW_BLOCK)

    def first(i, carry):
        at = span(i)
        total = x_ref[at, :].astype(F32) + out_bias
        for t in range(PARTS):
            total = total + dot_t(context_ref[t, at, :], out_ref[t])
        center = total - jnp.mean(total, axis=-1, keepdims=True)
        inverse = lax.rsqrt(jnp.mean(center * center, axis=-1, keepdims=True) + EPSILON)
        normed = center * inverse
        norm = normed * first_gain + first_shift
        first_norm[at, :] = norm
        first_normed[at, :] = normed
        first_scale[at, :] = inverse
        first_low[at, :] = norm.astype(BF16)
        second_sum[at, :] = norm + down_bias
        return carry

    lax.fori_loop(0, blocks, first, 0)

    def up(k, carry):
        t, i = k // blocks, k % blocks
        at = span(i)
        pre = dot(first_low[at, :], hidden_ref[t]) + hidden_bias_ref[t]
        cumulative = 0.5 * (1.0 + lax.erf(pre * ROOT_HALF))
        slope[t, at, :] = cumulative + pre * (PHI_ZERO * jnp.exp(-0.5 * pre * pre))
        active = (pre * cumulative).astype(BF16)
        activation[t, at, :] = active
        second_sum[at, :] += dot_t(active, down_ref[t])
        return carry

    lax.fori_loop(0, PARTS * blocks, up, 0)

    def second(i, carry):
        at = span(i)
        total = second_sum[at, :]
        center = total - jnp.mean(total, axis=-1, keepdims=True)
        inverse = lax.rsqrt(jnp.mean(center * center, axis=-1, keepdims=True) + EPSILON)
        normed = center * inverse
        layer_out[at, :] = (normed * second_gain + second_shift).astype(BF16)
        upstream = cotangent_ref[at, :].astype(F32)
        small_out[4:5, :] += column_sum(upstream * normed)
        small_out[5:6, :] += column_sum(upstream)
        scaled = upstream * second_gain
        inner = jnp.mean(scaled, axis=-1, keepdims=True)
        inner = inner + normed * jnp.mean(scaled * normed, axis=-1, keepdims=True)
        grad = inverse * (scaled - inner)
        small_out[3:4, :] += column_sum(grad)
        second_sum[at, :] = grad
        second_low[at, :] = grad.astype(BF16)
        return carry

    lax.fori_loop(0, blocks, second, 0)
    turned[...] = jnp.transpose(second_low[...])
    model_blocks = model // ROW_BLOCK

    def down_back(k, carry):
        t, i = k // model_blocks, k % model_blocks
        at = span(i)
        down_grad_out[t, at, :] = dot(turned[at, :], activation[t]).astype(BF16)
        return carry

    lax.fori_loop(0, PARTS * model_blocks, down_back, 0)
    turned[...] = jnp.transpose(first_low[...])

    def back(t, carry):
        def one(i, inner_carry):
            at = span(i)
            grad = dot(second_low[at, :], down_ref[t]) * slope[t, at, :]
            low = grad.astype(BF16)
            small_out[pl.ds(6 + t, 1), :] += column_sum(low.astype(F32))
            back_low[at, :] = low
            second_sum[at, :] += dot_t(low, hidden_ref[t])
            return inner_carry

        lax.fori_loop(0, blocks, one, 0)

        def weight(i, inner_carry):
            at = span(i)
            hidden_grad_out[t, at, :] = dot(turned[at, :], back_low[...]).astype(BF16)
            return inner_carry

        lax.fori_loop(0, model_blocks, weight, 0)
        return carry

    lax.fori_loop(0, PARTS, back, 0)

    def last(i, carry):
        at = span(i)
        upstream = second_sum[at, :]
        normed = first_normed[at, :]
        small_out[1:2, :] += column_sum(upstream * normed)
        small_out[2:3, :] += column_sum(upstream)
        scaled = upstream * first_gain
        inner = jnp.mean(scaled, axis=-1, keepdims=True)
        inner = inner + normed * jnp.mean(scaled * normed, axis=-1, keepdims=True)
        grad = first_scale[at, :] * (scaled - inner)
        small_out[0:1, :] += column_sum(grad)
        first_grad_out[at, :] = grad
        low = grad.astype(BF16)
        second_low[at, :] = low
        for t in range(PARTS):
            context_grad_out[t, at, :] = dot(low, out_ref[t]).astype(BF16)
        return carry

    lax.fori_loop(0, blocks, last, 0)
    turned[...] = jnp.transpose(second_low[...])

    def out_back(k, carry):
        t, i = k // model_blocks, k % model_blocks
        at = span(i)
        out_grad[t, at, :] = dot(turned[at, :], context_ref[t]).astype(BF16)
        return carry

    lax.fori_loop(0, PARTS * model_blocks, out_back, 0)


def middle(context, x, cotangent, out, hidden, down, vectors, hidden_bias):
    rows, model = x.shape
    width, units = context.shape[2], hidden.shape[2]
    big = pltpu.VMEM((rows, model), F32)
    low = pltpu.VMEM((rows, model), BF16)
    return pl.pallas_call(
        middle_kernel,
        out_shape=(
            jax.ShapeDtypeStruct((rows, model), BF16),
            jax.ShapeDtypeStruct((rows, model), F32),
            jax.ShapeDtypeStruct((PARTS, rows, width), BF16),
            jax.ShapeDtypeStruct((PARTS, model, width), BF16),
            jax.ShapeDtypeStruct((PARTS, model, units), BF16),
            jax.ShapeDtypeStruct((PARTS, model, units), BF16),
            jax.ShapeDtypeStruct((16, model), F32),
        ),
        in_specs=[vmem()] * 8,
        out_specs=[vmem()] * 7,
        scratch_shapes=[
            big,
            big,
            pltpu.VMEM((rows, 1), F32),
            low,
            big,
            pltpu.VMEM((PARTS, rows, units), BF16),
            pltpu.VMEM((PARTS, rows, units), F32),
            low,
            pltpu.VMEM((model, rows), BF16),
            pltpu.VMEM((rows, units), BF16),
        ],
        compiler_params=pltpu.CompilerParams(vmem_limit_bytes=VMEM_LIMIT),
        name="middle",
    )(context, x, cotangent, out, hidden, down, vectors, hidden_bias)


def body(
    shards,
    tokens,
    segment_ids,
    query_weight,
    query_bias,
    key_weight,
    value_weight,
    value_bias,
    out_weight,
    out_bias,
    first_gain,
    first_shift,
    hidden_weight,
    hidden_bias,
    down_weight,
    down_bias,
    second_gain,
    second_shift,
    output_cotangent,
):
    part = lax.axis_index("tensor")
    local_rows, model = tokens.shape
    group_rows = local_rows * PARTS
    width = query_weight.shape[1]
    units = hidden_weight.shape[1]
    joined = jnp.concatenate([query_weight, key_weight, value_weight], axis=1)
    all_x, all_joined, all_hidden, all_down, all_out, all_bias = gather(
        shards,
        tokens,
        joined,
        hidden_weight,
        down_weight.T,
        out_weight.T,
        hidden_bias.astype(F32)[None, :],
    )
    all_x = all_x.reshape(group_rows, model)
    all_joined = all_joined.reshape(model, 3 * width)
    all_hidden = all_hidden.reshape(PARTS, model, units)
    all_down = all_down.reshape(PARTS, model, units)
    all_out = all_out.reshape(PARTS, model, width)

    blocks = group_rows // QUERY_BLOCK
    edges = segment_ids.reshape(blocks, QUERY_BLOCK)
    low = jnp.sum((segment_ids[None, :] < edges[:, :1]).astype(jnp.int32), axis=1)
    high = jnp.sum((segment_ids[None, :] <= edges[:, -1:]).astype(jnp.int32), axis=1)
    low, high = low // KEY_BLOCK, (high + KEY_BLOCK - 1) // KEY_BLOCK
    key_seg, query_seg = segment_ids[:, None], segment_ids[None, :]

    queries, keys, values, context, totals = attention_forward(
        low,
        high,
        all_x,
        all_joined,
        query_bias.astype(F32)[None, :],
        value_bias.astype(F32)[None, :],
        key_seg,
        query_seg,
    )
    row_context = exchange(shards, 1, context.reshape(PARTS, local_rows, width))
    vectors = jnp.stack(
        [out_bias, first_gain, first_shift, down_bias, second_gain, second_shift]
        + [jnp.zeros_like(out_bias)] * 2
    ).astype(F32)
    (
        layer_output,
        first_grad,
        context_grad,
        out_grad,
        hidden_grad,
        down_grad,
        small,
    ) = middle(row_context, tokens, output_cotangent, all_out, all_hidden, all_down, vectors, all_bias)
    upstream = exchange(shards, 2, context_grad).reshape(group_rows, width)
    joined_grad, x_grad, bias_grad = attention_backward(
        low,
        high,
        all_x,
        all_joined,
        queries,
        keys,
        values,
        context,
        upstream,
        totals,
        key_seg,
        query_seg,
    )
    bias_grad = jnp.sum(bias_grad, axis=0)
    bias_row = jnp.concatenate(
        [bias_grad[:width], bias_grad[2 * width :], jnp.zeros((model - 2 * width,), F32)]
    )
    small = lax.dynamic_update_slice(small, bias_row[None, :], (10, 0))
    rows = model // shards
    chunks = local_rows // 128
    tokens_gradient, joined_grad, hidden_grad, down_grad, out_grad, small = reduce(
        shards,
        x_grad.reshape(PARTS, chunks, 128, model),
        first_grad.reshape(chunks, 128, model),
        joined_grad.reshape(shards, rows, 3 * width),
        hidden_grad.reshape(PARTS, shards, rows, units),
        down_grad.reshape(PARTS, shards, rows, units),
        out_grad.reshape(PARTS, shards, rows, width),
        small,
    )
    hidden_bias_gradient = lax.dynamic_index_in_dim(small[6:10], part, 0, keepdims=False)
    return (
        layer_output,
        tokens_gradient.reshape(local_rows, model),
        joined_grad[:, :width],
        small[10, :width],
        joined_grad[:, width : 2 * width],
        joined_grad[:, 2 * width :],
        small[10, width : 2 * width],
        out_grad.T,
        small[0],
        small[1],
        small[2],
        hidden_grad,
        hidden_bias_gradient,
        down_grad.T,
        small[3],
        small[4],
        small[5],
    )


def solution(mesh):
    shards = mesh.shape["dp"]
    split = P("dp", "tensor")
    turned = P("tensor", "dp")
    rows = P(("dp", "tensor"), None)
    head = P("tensor")
    in_specs = (
        rows,
        P("dp"),
        split,
        head,
        split,
        split,
        head,
        turned,
        P(),
        P(),
        P(),
        split,
        head,
        turned,
        P(),
        P(),
        P(),
        rows,
    )
    out_specs = (
        rows,
        rows,
        split,
        head,
        split,
        split,
        head,
        turned,
        P(),
        P(),
        P(),
        split,
        head,
        turned,
        P(),
        P(),
        P(),
    )
    return jax.shard_map(
        functools.partial(body, shards),
        mesh=mesh,
        in_specs=in_specs,
        out_specs=out_specs,
        check_vma=False,
    )
```

time: 919 us -> 341 us (0.37)
  waiting for transfers between devices: 400 us -> 0 us
  Pallas kernels: 0 us -> 316 us
  matrix products: 221 us -> 0 us
  blocking collectives: 136 us -> 0 us
  other arithmetic: 85.2 us -> 5.6 us
  local copies, waits for them, and re-layouts: 34.3 us -> 18.7 us
  loops' own time: 14 us -> 0 us
  between operations: 14.8 us -> 0.89 us
    pallas_call x0 -> x7, Pallas kernels: none -> 316 us  [the longest x1 82.6 us: reduce(): pl.pallas_call(functools.partial(reduce_kernel, shards), out_shape=(resul...]
    dot_general x40 -> x0, matrix products: 221 us -> none  [the longest x8 35.9 us: block_scores(): jnp.einsum('qhd,khd->hqk', query_block, keys, preferred_element_type=jnp....]
    unnamed x20 -> x0, waiting for transfers between devices: 189 us -> none
    reduce_scatter x5 -> x0, waiting for transfers between devices: 112 us -> none  [the longest x1 38 us: body(): lax.psum_scatter(times_transpose(hidden_grad, full_hidden).astype(jnp.bfl...]
    all_gather x3 -> x0, blocking collectives: 96.2 us -> none  [the longest x1 33.2 us: body(): lax.all_gather(query_weight, 'dp', axis=0, tiled=True)]
    all_gather x7 -> x0, waiting for transfers between devices: 95.2 us -> none  [the longest x1 28.6 us: body(): gathered_second = lax.all_gather(second_low, 'tensor', axis=0, tiled=True)]
    reduce_sum x14 -> x2, other arithmetic: 42.6 us -> 1.66 us  [the longest x1 0.92 us: body(): jnp.sum((segment_ids[None, :] <= edges[:, -1:]).astype(jnp.int32), axis=1)]
    psum x1 -> x0, blocking collectives: 40 us -> none  [body(): head_table, row_table = lax.psum((head_table, row_table), ('dp', 'tensor'))]
  transfers between devices with their start and end apart: 17 -> 0, of which waited for: 12 -> 0; matrix products, arithmetic and copies ran while one was open for 33% -> 0% of each run, Pallas kernels for 0% -> 0%
where the time goes in v1:
time: 341 us; the launch traced here: 342 us
  Pallas kernels  316 us (93%)
  local copies, waits for them, and re-layouts  18.7 us (5%)
  other arithmetic  5.6 us (2%)
    pallas_call x1, Pallas kernels, reduce(): pl.pallas_call(functools.partial(reduce_kernel, shards), out_shape=(resul...  82.6 us
    pallas_call x1, Pallas kernels, gather(): pl.pallas_call(functools.partial(gather_kernel, shards), out_shape=(shape...  63.8 us
    pallas_call x1, Pallas kernels, middle(): pl.pallas_call(middle_kernel, out_shape=(jax.ShapeDtypeStruct((rows, mode...  60.6 us
    pallas_call x1, Pallas kernels, attention_backward(): pl.pallas_call(backward_kernel, out_shape=(jax.ShapeDtypeStruct((model, 3...  48.3 us
    pallas_call x2, Pallas kernels, exchange(): pl.pallas_call(functools.partial(exchange_kernel, shards), out_shape=jax....  32.2 us
    pallas_call x1, Pallas kernels, attention_forward(): pl.pallas_call(forward_kernel, out_shape=(per_head, per_head, per_head, j...  28.9 us
    unnamed x27, local copies, waits for them, and re-layouts  7.34 us

profile of v1, /device:TPU:0, one launch (start us, length us, event | category | flops | bytes accessed | tf_op | source)
XLA Modules:
  0.0 341.5 jit_solution(1708332676931073913)
XLA Ops:
  0.7 0.0 copy-start.2
  0.7 0.0 copy-start.9
  0.7 0.0 copy-start.10
  0.7 0.7 reshape.80
  1.4 0.2 slice_reduce_fusion
  1.6 0.9 convert_reduce_fusion
  2.5 0.5 and_select_fusion
  3.1 1.6 pad_maximum_fusion.joined_ref
  4.7 1.5 copy.45
  6.2 1.3 reshape.95.bias_ref
  7.4 63.8 %gather.1 = (bf16[4,512,768]{2,1,0:T(8,128)(2,1)}, bf16[8,96,576]{2,1,0:T(8,128)(2,1)}, bf16[4,8,96,768]{3,2,1,0:T(8,128)(2,1)}, bf16[4,8,96,768]{3,2,1,0:T(8,12...) custom-call(bf16[512,768]{1,0:T(8,128)(2,1)} %x_ref.3, bf16[96,576]{1,0:T(8,128)(2,1)} %pad_maximum_fusion.joined_ref, ...), custom_call_target="tpu_custom_call" | custom-call | tf_op jit(solution)/shard_map/gather/pallas_call | solution.py:292
  71.3 0.0 copy-done.2
  71.3 1.4 copy.46.key_seg_ref
  72.6 0.0 copy-done.9
  72.6 0.6 broadcast_in_dim.40
  73.2 0.0 copy-done.10
  73.2 0.6 broadcast_in_dim.41
  73.8 28.9 %attention_forward.1 = (bf16[3,2048,64]{2,1,0:T(8,128)(2,1)}, bf16[3,2048,64]{2,1,0:T(8,128)(2,1)}, bf16[3,2048,64]{2,1,0:T(8,128)(2,1)}, bf16[2048,192]{1,0:T(8,128)(2,1)}, f32[3,1,2048]{2,1,0:T(1,128)}) custom-call(s32[8]{0:T(128)} %get-tuple-element.157.low_ref, s32[8]{0:T(128)} %get-tuple-element.156.high_ref, bf16[2048,768]{1,0:T(8,128)(2,1)} %bitcast.24, ...), custom_call_target="tpu_custom_call" | custom-call | tf_op jit(solution)/shard_map/attention_forward/pallas_call | solution.py:723
  102.6 0.0 copy-start.3
  102.6 0.0 copy-start.4
  102.6 0.0 copy-start.5
  102.7 0.0 copy-start.6
  102.7 0.0 copy-start.7
  102.7 0.0 copy-start.8
  102.7 16.1 %exchange_1.1.context_ref = bf16[4,512,192]{2,1,0:T(8,128)(2,1)} custom-call(bf16[4,512,192]{2,1,0:T(8,128)(2,1)} %bitcast.30), custom_call_target="tpu_custom_call" | custom-call | tf_op jit(solution)/shard_map/exchange_1/pallas_call | solution.py:331
  118.8 0.0 copy-done.3
  118.9 0.0 copy-done.4
  118.9 0.0 copy-done.5
  118.9 0.0 copy-done.6
  118.9 0.0 copy-done.7
  119.0 0.0 copy-done.8
  119.0 0.6 convert_element_type.14.vectors_ref
  119.7 60.6 %middle.1 = (bf16[512,768]{1,0:T(8,128)(2,1)}, f32[512,768]{1,0:T(8,128)}, bf16[4,512,192]{2,1,0:T(8,128)(2,1)}, bf16[4,768,192]{2,1,0:T(8,128)(2,1)}, bf16[4,76...) custom-call(bf16[4,512,192]{2,1,0:T(8,128)(2,1)} %exchange_1.1.context_ref, ...), custom_call_target="tpu_custom_call" | custom-call | tf_op jit(solution)/shard_map/middle/pallas_call | solution.py:1043
  180.3 16.0 %exchange_2.1 = bf16[4,512,192]{2,1,0:T(8,128)(2,1)} custom-call(bf16[4,512,192]{2,1,0:T(8,128)(2,1)} %get-tuple-element.55.source), custom_call_target="tpu_custom_call" | custom-call | tf_op jit(solution)/shard_map/exchange_2/pallas_call | solution.py:331
  196.3 48.3 %attention_backward.1 = (bf16[768,576]{1,0:T(8,128)(2,1)}, bf16[2048,768]{1,0:T(8,128)(2,1)}, f32[8,576]{1,0:T(8,128)}) custom-call(s32[8]{0:T(128)} %get-tuple-element.157.low_ref, s32[8]{0:T(128)} %get-tuple-element.156.high_ref, bf16[2048,768]{1,0:T(8,128)(2,1)} %bitcast.25, bf16[768,576]{1,0:T(8,128)(2,1)} %bitcast.33, ...), custom_call_target="tpu_custom_call" | custom-call | tf_op jit(solution)/shard_map/attention_backward/pallas_call | solution.py:854
  244.6 0.7 reduce_sum.29
  245.4 0.1 pad_maximum_fusion.1
  245.4 1.4 dynamic_update_slice.3.small_ref
  246.8 82.6 %reduce.19 = (f32[4,128,768]{2,1,0:T(8,128)}, f32[96,576]{1,0:T(8,128)}, f32[96,768]{1,0:T(8,128)}, f32[96,768]{1,0:T(8,128)}, f32[96,192]{1,0:T(8,128)}, /*index=5*/f32[16,768]{1,0:T(8,128)}) custom-call(bf16[4,4,128,768]{3,2,1,0:T(8,128)(2,1)} %bitcast.34, f32[4,128,768]{2,1,0:T(8,128)} %bitcast.35, bf16[8,96,576]{2,1,0:T(8,128)(2,1)} %bitcast.39, ...), custom_call_target="tpu_custom_call" | custom-call | tf_op jit(solution)/shard_map/reduce/pallas_call | solution.py:587
  329.4 1.8 fusion
  331.2 1.6 copy.48
  332.8 1.8 slice_reduce_fusion.2
  334.6 0.8 slice.60
  335.4 0.6 dynamic-slice_reduce_fusion
  336.0 1.4 fusion.1
  337.4 0.0 copy-start.1
  337.4 0.0 copy-start
  337.4 2.7 copy.53
  340.1 0.0 copy-done.1
  340.1 0.7 copy.54
  340.8 0.0 copy-done
  340.8 0.7 copy.55
  (11 shorter events, 0.1 us)
Async XLA Ops:
  0.7 70.6 %copy-start.2 = (s32[2048]{0:T(1024)S(1)}, s32[2048]{0:T(1024)}, u32[]{:S(2)}) copy-start(s32[2048]{0:T(1024)} %param.19) | copy-start | bytes 24580
  0.7 72.0 %copy-start.9 = (bf16[192]{0:T(256)(128)(2,1)S(1)}, bf16[192]{0:T(256)(128)(2,1)}, u32[]{:S(2)}) copy-start(bf16[192]{0:T(256)(128)(2,1)} %param.21) | copy-start | bytes 1156
  0.7 72.5 %copy-start.10 = (bf16[192]{0:T(256)(128)(2,1)S(1)}, bf16[192]{0:T(256)(128)(2,1)}, u32[]{:S(2)}) copy-start(bf16[192]{0:T(256)(128)(2,1)} %param.24) | copy-start | bytes 1156
  102.6 16.2 %copy-start.3 = (bf16[768]{0:T(1024)(128)(2,1)S(1)}, bf16[768]{0:T(1024)(128)(2,1)}, u32[]{:S(2)}) copy-start(bf16[768]{0:T(1024)(128)(2,1)} %param.26) | copy-start | bytes 4612
  102.6 16.2 %copy-start.4 = (bf16[768]{0:T(1024)(128)(2,1)S(1)}, bf16[768]{0:T(1024)(128)(2,1)}, u32[]{:S(2)}) copy-start(bf16[768]{0:T(1024)(128)(2,1)} %param.27) | copy-start | bytes 4612
  102.6 16.2 %copy-start.5 = (bf16[768]{0:T(1024)(128)(2,1)S(1)}, bf16[768]{0:T(1024)(128)(2,1)}, u32[]{:S(2)}) copy-start(bf16[768]{0:T(1024)(128)(2,1)} %param.28) | copy-start | bytes 4612
  102.7 16.3 %copy-start.6 = (bf16[768]{0:T(1024)(128)(2,1)S(1)}, bf16[768]{0:T(1024)(128)(2,1)}, u32[]{:S(2)}) copy-start(bf16[768]{0:T(1024)(128)(2,1)} %param.32) | copy-start | bytes 4612
  102.7 16.3 %copy-start.7 = (bf16[768]{0:T(1024)(128)(2,1)S(1)}, bf16[768]{0:T(1024)(128)(2,1)}, u32[]{:S(2)}) copy-start(bf16[768]{0:T(1024)(128)(2,1)} %param.33) | copy-start | bytes 4612
  102.7 16.3 %copy-start.8 = (bf16[768]{0:T(1024)(128)(2,1)S(1)}, bf16[768]{0:T(1024)(128)(2,1)}, u32[]{:S(2)}) copy-start(bf16[768]{0:T(1024)(128)(2,1)} %param.34) | copy-start | bytes 4612
  337.4 2.7 copy-start.1
  337.4 3.4 %copy-start = (f32[96,768]{1,0:T(8,128)S(1)}, f32[96,768]{1,0:T(8,128)}, u32[]{:S(2)}) copy-start(f32[96,768]{1,0:T(8,128)} %get-tuple-element.70) | copy-start | bytes 884740

commit v2 on v1

--- a/solution.py
+++ b/solution.py
@@ -23,6 +23,10 @@
 
 def dot_t(left, right):
     return lax.dot_general(left, right, (((1,), (1,)), ((), ())), preferred_element_type=F32)
+
+
+def fold_rows(block):
+    return block.reshape(block.shape[0] // 8, 8, block.shape[1])
 
 
 def vmem():
@@ -64,19 +68,21 @@
         self.row = self.part // 2
         self.other_core = self.part + 1 - 2 * self.core
         self.other_row = (self.part + 2) % PARTS
-        self.place = ring_place(self.dp, shards)
+        self.diagonal = (self.other_core + 2) % PARTS
+        place = ring_place(self.dp, shards)
+        self.table = [ring_index((place + i) % shards, shards) for i in range(shards)]
         self.right = self.at(1)
         self.left = self.at(-1)
 
     def at(self, offset):
-        return ring_index((self.place + offset + self.shards) % self.shards, self.shards)
+        return self.table[offset % self.shards]
 
     def barrier(self, tensor=True, ring=True, diagonal=False, cube=False):
         partners = []
         if tensor:
             partners += [{"tensor": self.other_core}, {"tensor": self.other_row}]
         if diagonal:
-            partners += [{"tensor": (self.other_core + 2) % PARTS}]
+            partners += [{"tensor": self.diagonal}]
         if ring:
             partners += [{"dp": self.right}, {"dp": self.left}]
         if cube:
@@ -165,11 +171,31 @@
         return found
 
 
-def gather_copies(shards):
-    return 40 + 26 * shards
-
-
-def gather_kernel(
+def forward_copies(shards):
+    return 60 + 26 * shards
+
+
+BLOCK = 512
+MOST = 800
+REACH = (MOST + BLOCK - 2) // BLOCK
+
+
+def near(i, blocks):
+    return jnp.maximum(i - REACH, 0), jnp.minimum(i + REACH + 1, blocks)
+
+
+def turned_segments(segment_ref, key_segments):
+    for j in range(PARTS):
+        row = jnp.broadcast_to(segment_ref[j], (128, BLOCK))
+        key_segments[j] = jnp.transpose(row)
+
+
+def allowed_block(key_segments, segment_ref, i, j):
+    keys = jnp.concatenate([key_segments[j]] * (BLOCK // 128), axis=1)
+    return keys == jnp.broadcast_to(segment_ref[i], (BLOCK, BLOCK))
+
+
+def forward_kernel(
     shards,
     x_ref,
     joined_ref,
@@ -177,12 +203,33 @@
     down_ref,
     out_ref,
     bias_ref,
+    query_bias_ref,
+    value_bias_ref,
+    segment_ref,
     all_x,
     all_joined,
     all_hidden,
     all_down,
     all_out,
     all_bias,
+    query_out,
+    key_out,
+    value_out,
+    key_turned_out,
+    context_out,
+    total_out,
+    row_context,
+    x_here,
+    joined_here,
+    joined_turned,
+    query_turned,
+    key_turned,
+    value_turned,
+    key_here,
+    value_here,
+    context_here,
+    score_store,
+    key_segments,
     send,
     recv,
     local,
@@ -191,126 +238,264 @@
     me, part = links.dp, links.part
     across, beside = {"tensor": links.other_row}, {"tensor": links.other_core}
     far = links.other_row
-    links.barrier()
+    links.barrier(diagonal=True)
     rows = hidden_ref.shape[0]
     half = shards // 2
+    width = query_bias_ref.shape[0]
+    heads = width // HEAD
+    scale = HEAD ** (-0.5)
     later = []
 
-    def share(make, source_part, ref_of):
+    def share(make, source_part, source=None):
         number = links.number()
         ref = make(source_part)
-        links.start(number, ref_of if ref_of is not None else ref, ref, beside)
-        partner_part = source_part + 1 - 2 * links.core
-        later.append((number, make(partner_part)))
-
-    joined = RingGather(links, rows, joined_ref, lambda j: all_joined.at[j])
+        links.start(number, ref if source is None else source, ref, beside)
+        later.append((number, make(source_part + 1 - 2 * links.core)))
+        return later[-1]
+
+    def settle(entry):
+        links.arrive(*entry, beside)
+        later.remove(entry)
+
+    joined = RingGather(links, rows, joined_ref, lambda j: joined_here.at[j])
     hidden = RingGather(links, rows, hidden_ref, lambda j: all_hidden.at[part, j])
+    down_own = RingGather(links, rows, down_ref, lambda j: all_down.at[part, j])
+    out_own = RingGather(links, rows, out_ref, lambda j: all_out.at[part, j])
+    down_far = RingGather(links, rows, all_down.at[far, me], lambda j: all_down.at[far, j])
+    out_far = RingGather(links, rows, all_out.at[far, me], lambda j: all_out.at[far, j])
     joined.send(1)
-    down_number, out_number, x_number, bias_number = (links.number() for _ in range(4))
+    cut = x_ref.shape[0] // 2
+    x_numbers = [links.number() for _ in range(2)]
+    pieces = [pl.ds(0, cut), pl.ds(cut, cut)]
+    for number, piece in zip(x_numbers, pieces):
+        links.start(number, x_ref.at[piece], x_here.at[part, piece], across)
+    x_beside = share(lambda t: x_here.at[t], part, x_ref)
+    bias_number, down_number, out_number = (links.number() for _ in range(3))
     links.start(bias_number, bias_ref, all_bias.at[part], across)
     links.start(down_number, down_ref, all_down.at[part, me], across)
     links.start(out_number, out_ref, all_out.at[part, me], across)
-    links.start(x_number, x_ref, all_x.at[part], across)
-    down_own = RingGather(links, rows, down_ref, lambda j: all_down.at[part, j])
-    out_own = RingGather(links, rows, out_ref, lambda j: all_out.at[part, j])
-    down_own.send(1)
     hidden.send(1)
-    out_own.send(1)
     hidden_numbers = {}
 
-    def hidden_across(j_send, j_get, key, piece):
+    def hidden_across(j, key, piece):
         number = links.number()
-        source = hidden_ref if key == 0 else piece(all_hidden.at[part, j_send])
-        links.start(number, source, piece(all_hidden.at[part, j_send]), across)
-        hidden_numbers[key] = (number, piece(all_hidden.at[far, j_get]), j_get, piece)
-
-    whole = lambda ref: ref
-    hidden_across(me, me, 0, whole)
+        target = piece(all_hidden.at[part, j])
+        links.start(number, hidden_ref if key == 0 else target, target, across)
+        hidden_numbers[key] = (number, j, piece)
+
+    def far_hidden(key):
+        number, j, piece = hidden_numbers[key]
+        links.arrive(number, piece(all_hidden.at[far, j]), across)
+        share(lambda t: piece(all_hidden.at[t, j]), far)
+
+    hidden_across(me, 0, lambda ref: ref)
+    share(lambda t: all_hidden.at[t, me], part, hidden_ref)
+    share(lambda t: all_down.at[t, me], part, down_ref)
+    share(lambda t: all_out.at[t, me], part, out_ref)
+    share(lambda t: all_bias.at[t], part, bias_ref)
     links.keep(x_ref, all_x.at[part])
-    links.keep(joined_ref, all_joined.at[me])
     links.keep(hidden_ref, all_hidden.at[part, me])
     links.keep(down_ref, all_down.at[part, me])
     links.keep(out_ref, all_out.at[part, me])
     links.keep(bias_ref, all_bias.at[part])
-    share(lambda t: all_bias.at[t], part, bias_ref)
-    share(lambda t: all_x.at[t], part, x_ref)
-    share(lambda t: all_hidden.at[t, me], part, hidden_ref)
-    share(lambda t: all_down.at[t, me], part, down_ref)
-    share(lambda t: all_out.at[t, me], part, out_ref)
-
-    links.arrive(down_number, all_down.at[far, me], across)
-    down_far = RingGather(links, rows, all_down.at[far, me], lambda j: all_down.at[far, j])
-    down_far.send(1)
-    share(lambda t: all_down.at[t, me], far, None)
-    links.arrive(out_number, all_out.at[far, me], across)
-    out_far = RingGather(links, rows, all_out.at[far, me], lambda j: all_out.at[far, j])
-    out_far.send(1)
-    share(lambda t: all_out.at[t, me], far, None)
-
-    def pieces(stream, step, way):
-        return lambda ref: stream.part(ref, step, way)
-
-    def far_hidden(key):
-        number, ref, j, piece = hidden_numbers[key]
-        links.arrive(number, ref, across)
-        share(lambda t: piece(all_hidden.at[t, j]), far, None)
-
+
+    def take(stream, step):
+        arrived = stream.arrive(step)
+        if step < half:
+            stream.send(step + 1)
+        for j, way in arrived:
+            piece = lambda ref, way=way: stream.part(ref, step, way)
+            if stream is hidden:
+                hidden_across(j, (step, way), piece)
+                share(lambda t, j=j, piece=piece: piece(all_hidden.at[t, j]), part)
+            elif stream is not joined:
+                ref = all_down if stream in (down_own, down_far) else all_out
+                owner = part if stream in (down_own, out_own) else far
+                share(lambda t, j=j, piece=piece, ref=ref: piece(ref.at[t, j]), owner)
+
+    def from_far():
+        links.arrive(down_number, all_down.at[far, me], across)
+        down_far.send(1)
+        share(lambda t: all_down.at[t, me], far)
+        links.arrive(out_number, all_out.at[far, me], across)
+        out_far.send(1)
+        share(lambda t: all_out.at[t, me], far)
+        links.arrive(bias_number, all_bias.at[far], across)
+        share(lambda t: all_bias.at[t], far)
+        far_hidden(0)
+
+    def both(first, second, step):
+        take(first, step)
+        take(second, step)
+
+    def far_step(step):
+        for way in hidden.ways(step):
+            far_hidden((step, way))
+
+    turned_segments(segment_ref, key_segments)
+    joined_here[me] = joined_ref[...]
+    take(joined, 1)
+    down_own.send(1)
+    out_own.send(1)
+    for step in range(2, half + 1):
+        take(joined, step)
+        if step == 2:
+            take(hidden, 1)
+    model = x_ref.shape[1]
+    joined_turned[...] = jnp.transpose(joined_here[...].reshape(model, 3 * width))
+
+    def project(s, x):
+        three = dot_t(joined_turned[...], x[...])
+        queries = (three[:width] + query_bias_ref[...]).astype(BF16)
+        query_turned[s] = (queries.astype(F32) * scale).astype(BF16)
+        keys = three[width : 2 * width]
+        values = three[2 * width :] + value_bias_ref[...]
+        key_turned[s] = keys.astype(BF16)
+        value_turned[s] = values.astype(BF16)
+        for h in range(heads):
+            span = slice(h * HEAD, (h + 1) * HEAD)
+            key_here[s, h] = jnp.transpose(keys[span]).astype(BF16)
+            value_here[s, h] = jnp.transpose(values[span]).astype(BF16)
+
+    x_far = []
+    for number, piece in zip(x_numbers, pieces):
+        links.arrive(number, x_here.at[far, piece], across)
+        x_far.append(share(lambda t, piece=piece: x_here.at[t, piece], far))
+    project(part, x_ref)
+    settle(x_beside)
+    project(links.other_core, x_here.at[links.other_core])
+    project(far, x_here.at[far])
+    for entry in x_far:
+        settle(entry)
+    project(links.diagonal, x_here.at[links.diagonal])
+    for t in (links.other_core, far, links.diagonal):
+        links.keep(x_here.at[t], all_x.at[t])
+    for source, target in (
+        (joined_turned, all_joined),
+        (query_turned, query_out),
+        (key_turned, key_turned_out),
+        (key_here, key_out),
+        (value_here, value_out),
+    ):
+        links.keep(source, target)
+
+    queue = [lambda: from_far()]
     for step in range(1, half + 1):
-        for stream in (joined, hidden, down_own, down_far, out_own, out_far):
-            arrived = stream.arrive(step)
-            if step < half:
-                stream.send(step + 1)
-            for j, way in arrived:
-                piece = pieces(stream, step, way)
-                if stream is hidden:
-                    hidden_across(j, j, (step, way), piece)
-                    share(lambda t, j=j, piece=piece: piece(all_hidden.at[t, j]), part, None)
-                elif stream is not joined:
-                    ref = all_down if stream in (down_own, down_far) else all_out
-                    owner = part if stream in (down_own, out_own) else far
-                    share(lambda t, j=j, piece=piece, ref=ref: piece(ref.at[t, j]), owner, None)
-        if step == 1:
-            links.arrive(x_number, all_x.at[far], across)
-            share(lambda t: all_x.at[t], far, None)
-            links.arrive(bias_number, all_bias.at[far], across)
-            share(lambda t: all_bias.at[t], far, None)
-            far_hidden(0)
-        else:
-            for way in hidden.ways(step - 1):
-                far_hidden((step - 1, way))
-    for way in hidden.ways(half):
-        far_hidden((half, way))
+        queue.append(lambda step=step: both(down_own, out_own, step))
+        if step < half:
+            queue.append(lambda step=step: take(hidden, step + 1))
+            queue.append(lambda step=step: far_step(step))
+        queue.append(lambda step=step: both(down_far, out_far, step))
+    queue.append(lambda: far_step(half))
+
+    partners = (far, links.diagonal, links.other_core)
+    context_numbers = [links.number() for _ in partners]
+    places = partners + (part,)
+
+    for n in range(PARTS):
+        i = places[n]
+        low, high = near(i, PARTS)
+        queries = [query_turned[i, h * HEAD : (h + 1) * HEAD, :] for h in range(heads)]
+
+        def scores(j, tops):
+            allowed = allowed_block(key_segments, segment_ref, i, j)
+            found = []
+            for h in range(heads):
+                block = jnp.where(allowed, dot(key_here[j, h], queries[h]), NEGATIVE)
+                score_store[j, h] = block
+                found.append(jnp.maximum(tops[h], jnp.max(fold_rows(block), axis=0)))
+            return tuple(found)
+
+        start = jnp.full((8, BLOCK), NEGATIVE, F32)
+        tops = lax.fori_loop(low, high, scores, (start,) * heads)
+        tops = [jnp.max(top, axis=0, keepdims=True) for top in tops]
+
+        def mix(j, state):
+            found = []
+            for h in range(heads):
+                total, mixed = state[h]
+                weights = jnp.exp(score_store[j, h] - tops[h])
+                total = total + jnp.sum(fold_rows(weights), axis=0)
+                values = value_turned[j, h * HEAD : (h + 1) * HEAD, :]
+                mixed = mixed + dot(values, weights.astype(BF16))
+                found.append((total, mixed))
+            return tuple(found)
+
+        empty = (jnp.zeros((8, BLOCK), F32), jnp.zeros((HEAD, BLOCK), F32))
+        state = lax.fori_loop(low, high, mix, (empty,) * heads)
+        for h in range(heads):
+            total = jnp.sum(state[h][0], axis=0, keepdims=True)
+            context_here[i, h * HEAD : (h + 1) * HEAD, :] = (state[h][1] / total).astype(BF16)
+            total_out[i, h : h + 1, :] = tops[h] + jnp.log(total)
+        if n < 3:
+            links.start(
+                context_numbers[n],
+                context_here.at[i],
+                row_context.at[part],
+                {"tensor": i},
+            )
+        share_of = -(-len(queue) // PARTS)
+        for event in queue[n * share_of : (n + 1) * share_of]:
+            event()
+
+    links.keep(context_here, context_out)
+    links.keep(context_here.at[part], row_context.at[part])
     for number, ref in later:
         links.arrive(number, ref, beside)
+    for number, partner in zip(context_numbers, partners):
+        links.arrive(number, row_context.at[partner], {"tensor": partner})
     links.finish()
-    assert links.used <= gather_copies(shards), links.used
-
-
-def gather(shards, x, joined, hidden, down, out, bias):
+    assert links.used <= forward_copies(shards), links.used
+
+
+def forward(shards, x, joined, hidden, down, out, bias, query_bias, value_bias, segments):
     shape = lambda *dims: jax.ShapeDtypeStruct(dims, BF16)
-    count = gather_copies(shards)
+    count = forward_copies(shards)
+    rows, model = x.shape
+    width = query_bias.shape[0]
+    heads = width // HEAD
+    turned = (PARTS, width, rows)
+    headed = (PARTS, heads, rows, HEAD)
     return pl.pallas_call(
-        functools.partial(gather_kernel, shards),
+        functools.partial(forward_kernel, shards),
         out_shape=(
-            shape(PARTS, *x.shape),
-            shape(shards, *joined.shape),
+            shape(PARTS, rows, model),
+            shape(3 * width, model),
             shape(PARTS, shards, *hidden.shape),
             shape(PARTS, shards, *down.shape),
             shape(PARTS, shards, *out.shape),
             jax.ShapeDtypeStruct((PARTS, *bias.shape), F32),
+            shape(*turned),
+            shape(*headed),
+            shape(*headed),
+            shape(*turned),
+            shape(*turned),
+            jax.ShapeDtypeStruct((PARTS, 8, rows), F32),
+            shape(*turned),
         ),
-        in_specs=[vmem()] * 6,
-        out_specs=[anywhere()] * 6,
+        in_specs=[vmem()] * 9,
+        out_specs=[anywhere()] * 11 + [vmem()] + [anywhere()],
         scratch_shapes=[
+            pltpu.VMEM((PARTS, rows, model), BF16),
+            pltpu.VMEM((shards, *joined.shape), BF16),
+            pltpu.VMEM((3 * width, model), BF16),
+            pltpu.VMEM(turned, BF16),
+            pltpu.VMEM(turned, BF16),
+            pltpu.VMEM(turned, BF16),
+            pltpu.VMEM(headed, BF16),
+            pltpu.VMEM(headed, BF16),
+            pltpu.VMEM(turned, BF16),
+            pltpu.VMEM((PARTS, heads, BLOCK, BLOCK), F32),
+            pltpu.VMEM((PARTS, BLOCK, 128), F32),
             pltpu.SemaphoreType.DMA((count,)),
             pltpu.SemaphoreType.DMA((count,)),
-            pltpu.SemaphoreType.DMA((6,)),
+            pltpu.SemaphoreType.DMA((16,)),
         ],
         compiler_params=pltpu.CompilerParams(
             collective_id=0, has_side_effects=True, vmem_limit_bytes=VMEM_LIMIT
         ),
-        name="gather",
-    )(x, joined, hidden, down, out, bias)
+        name="forward",
+    )(x, joined, hidden, down, out, bias, query_bias, value_bias, segments)
 
 
 def exchange_kernel(shards, source, target, send, recv):
@@ -625,121 +810,6 @@
 KEY_BLOCK = 256
 
 
-def fold_rows(block):
-    return block.reshape(block.shape[0] // 8, 8, block.shape[1])
-
-
-def forward_kernel(
-    low_ref,
-    high_ref,
-    x_ref,
-    weight_ref,
-    query_bias_ref,
-    value_bias_ref,
-    key_seg_ref,
-    query_seg_ref,
-    query_out,
-    key_out,
-    value_out,
-    context_out,
-    total_out,
-    value_turned,
-    score_store,
-):
-    heads = query_out.shape[0]
-    width = heads * HEAD
-    scale = HEAD ** (-0.5)
-    rows = x_ref.shape[0]
-
-    def project(i, carry):
-        at = pl.ds(pl.multiple_of(i * QUERY_BLOCK, QUERY_BLOCK), QUERY_BLOCK)
-        all_three = dot(x_ref[at, :], weight_ref[...])
-        queries = (all_three[:, :width] + query_bias_ref[...]).astype(BF16)
-        queries = (queries.astype(F32) * scale).astype(BF16)
-        keys = all_three[:, width : 2 * width].astype(BF16)
-        values = all_three[:, 2 * width :] + value_bias_ref[...]
-        turned = jnp.transpose(values).astype(BF16)
-        values = values.astype(BF16)
-        for h in range(heads):
-            columns = slice(h * HEAD, (h + 1) * HEAD)
-            query_out[h, at, :] = queries[:, columns]
-            key_out[h, at, :] = keys[:, columns]
-            value_out[h, at, :] = values[:, columns]
-        value_turned[:, at] = turned
-        return carry
-
-    lax.fori_loop(0, rows // QUERY_BLOCK, project, 0)
-
-    def attend(i, carry):
-        at = pl.ds(pl.multiple_of(i * QUERY_BLOCK, QUERY_BLOCK), QUERY_BLOCK)
-        query_seg = query_seg_ref[:, at]
-        queries = [query_out[h, at, :] for h in range(heads)]
-
-        def scores(j, tops):
-            there = pl.ds(pl.multiple_of(j * KEY_BLOCK, KEY_BLOCK), KEY_BLOCK)
-            allowed = key_seg_ref[there, :] == query_seg
-            found = []
-            for h in range(heads):
-                block = dot_t(key_out[h, there, :], queries[h])
-                block = jnp.where(allowed, block, NEGATIVE)
-                score_store[h, there, :] = block
-                found.append(jnp.maximum(tops[h], jnp.max(fold_rows(block), axis=0)))
-            return tuple(found)
-
-        start = jnp.full((8, QUERY_BLOCK), NEGATIVE, F32)
-        tops = lax.fori_loop(low_ref[i], high_ref[i], scores, (start,) * heads)
-        tops = [jnp.max(top, axis=0, keepdims=True) for top in tops]
-
-        def mix(j, state):
-            there = pl.ds(pl.multiple_of(j * KEY_BLOCK, KEY_BLOCK), KEY_BLOCK)
-            found = []
-            for h in range(heads):
-                total, mixed = state[h]
-                weights = jnp.exp(score_store[h, there, :] - tops[h])
-                total = total + jnp.sum(fold_rows(weights), axis=0)
-                turned = value_turned[h * HEAD : (h + 1) * HEAD, there]
-                mixed = mixed + dot(turned, weights.astype(BF16))
-                found.append((total, mixed))
-            return tuple(found)
-
-        empty = (jnp.zeros((8, QUERY_BLOCK), F32), jnp.zeros((HEAD, QUERY_BLOCK), F32))
-        state = lax.fori_loop(low_ref[i], high_ref[i], mix, (empty,) * heads)
-        parts = []
-        for h in range(heads):
-            total = jnp.sum(state[h][0], axis=0, keepdims=True)
-            parts.append(state[h][1] / total)
-            total_out[h, :, at] = tops[h] + jnp.log(total)
-        context_out[at, :] = jnp.transpose(jnp.concatenate(parts, axis=0)).astype(BF16)
-        return carry
-
-    lax.fori_loop(0, rows // QUERY_BLOCK, attend, 0)
-
-
-def attention_forward(low, high, x, weight, query_bias, value_bias, key_seg, query_seg):
-    rows = x.shape[0]
-    width = weight.shape[1] // 3
-    heads = width // HEAD
-    per_head = jax.ShapeDtypeStruct((heads, rows, HEAD), BF16)
-    return pl.pallas_call(
-        forward_kernel,
-        out_shape=(
-            per_head,
-            per_head,
-            per_head,
-            jax.ShapeDtypeStruct((rows, width), BF16),
-            jax.ShapeDtypeStruct((heads, 1, rows), F32),
-        ),
-        in_specs=[smem()] * 2 + [vmem()] * 6,
-        out_specs=[vmem()] * 5,
-        scratch_shapes=[
-            pltpu.VMEM((width, rows), BF16),
-            pltpu.VMEM((heads, rows, QUERY_BLOCK), F32),
-        ],
-        compiler_params=pltpu.CompilerParams(vmem_limit_bytes=VMEM_LIMIT),
-        name="attention_forward",
-    )(low, high, x, weight, query_bias, value_bias, key_seg, query_seg)
-
-
 def backward_kernel(
     low_ref,
     high_ref,
@@ -880,7 +950,20 @@
 
 
 def column_sum(block):
-    return jnp.sum(block, axis=0, keepdims=True)
+    return jnp.sum(jnp.sum(fold_rows(block), axis=0), axis=0, keepdims=True)
+
+
+def normalized(total):
+    center = total - jnp.mean(total, axis=-1, keepdims=True)
+    inverse = lax.rsqrt(jnp.mean(center * center, axis=-1, keepdims=True) + EPSILON)
+    return center * inverse, inverse
+
+
+def normalized_back(upstream, normed, inverse, gain):
+    scaled = upstream * gain
+    inner = jnp.mean(scaled, axis=-1, keepdims=True)
+    inner = inner + normed * jnp.mean(scaled * normed, axis=-1, keepdims=True)
+    return inverse * (scaled - inner)
 
 
 def middle_kernel(
@@ -911,8 +994,6 @@
     back_low,
 ):
     rows, model = x_ref.shape
-    width = context_ref.shape[2]
-    blocks = rows // ROW_BLOCK
     out_bias, first_gain, first_shift = (vectors_ref[i : i + 1, :] for i in range(3))
     down_bias, second_gain, second_shift = (vectors_ref[i : i + 1, :] for i in range(3, 6))
     small_out[...] = jnp.zeros_like(small_out)
@@ -920,51 +1001,44 @@
     def span(i):
         return pl.ds(pl.multiple_of(i * ROW_BLOCK, ROW_BLOCK), ROW_BLOCK)
 
+    blocks = rows // ROW_BLOCK
+    attended = x_ref[...].astype(F32) + out_bias
+    for t in range(PARTS):
+        attended = attended + dot_t(context_ref[t], out_ref[t])
+    first_norm[...] = attended
+
     def first(i, carry):
         at = span(i)
-        total = x_ref[at, :].astype(F32) + out_bias
-        for t in range(PARTS):
-            total = total + dot_t(context_ref[t, at, :], out_ref[t])
-        center = total - jnp.mean(total, axis=-1, keepdims=True)
-        inverse = lax.rsqrt(jnp.mean(center * center, axis=-1, keepdims=True) + EPSILON)
-        normed = center * inverse
+        normed, inverse = normalized(first_norm[at, :])
         norm = normed * first_gain + first_shift
         first_norm[at, :] = norm
         first_normed[at, :] = normed
         first_scale[at, :] = inverse
         first_low[at, :] = norm.astype(BF16)
-        second_sum[at, :] = norm + down_bias
         return carry
 
     lax.fori_loop(0, blocks, first, 0)
-
-    def up(k, carry):
-        t, i = k // blocks, k % blocks
-        at = span(i)
-        pre = dot(first_low[at, :], hidden_ref[t]) + hidden_bias_ref[t]
+    second_sum[...] = first_norm[...] + down_bias
+
+    def up(t, carry):
+        pre = dot(first_low[...], hidden_ref[t]) + hidden_bias_ref[t]
         cumulative = 0.5 * (1.0 + lax.erf(pre * ROOT_HALF))
-        slope[t, at, :] = cumulative + pre * (PHI_ZERO * jnp.exp(-0.5 * pre * pre))
+        slope[t] = cumulative + pre * (PHI_ZERO * jnp.exp(-0.5 * pre * pre))
         active = (pre * cumulative).astype(BF16)
-        activation[t, at, :] = active
-        second_sum[at, :] += dot_t(active, down_ref[t])
+        activation[t] = active
+        second_sum[...] += dot_t(active, down_ref[t])
         return carry
 
-    lax.fori_loop(0, PARTS * blocks, up, 0)
+    lax.fori_loop(0, PARTS, up, 0)
 
     def second(i, carry):
         at = span(i)
-        total = second_sum[at, :]
-        center = total - jnp.mean(total, axis=-1, keepdims=True)
-        inverse = lax.rsqrt(jnp.mean(center * center, axis=-1, keepdims=True) + EPSILON)
-        normed = center * inverse
+        normed, inverse = normalized(second_sum[at, :])
         layer_out[at, :] = (normed * second_gain + second_shift).astype(BF16)
         upstream = cotangent_ref[at, :].astype(F32)
         small_out[4:5, :] += column_sum(upstream * normed)
         small_out[5:6, :] += column_sum(upstream)
-        scaled = upstream * second_gain
-        inner = jnp.mean(scaled, axis=-1, keepdims=True)
-        inner = inner + normed * jnp.mean(scaled * normed, axis=-1, keepdims=True)
-        grad = inverse * (scaled - inner)
+        grad = normalized_back(upstream, normed, inverse, second_gain)
         small_out[3:4, :] += column_sum(grad)
         second_sum[at, :] = grad
         second_low[at, :] = grad.astype(BF16)
@@ -972,35 +1046,20 @@
 
     lax.fori_loop(0, blocks, second, 0)
     turned[...] = jnp.transpose(second_low[...])
-    model_blocks = model // ROW_BLOCK
-
-    def down_back(k, carry):
-        t, i = k // model_blocks, k % model_blocks
-        at = span(i)
-        down_grad_out[t, at, :] = dot(turned[at, :], activation[t]).astype(BF16)
+
+    def down_back(t, carry):
+        down_grad_out[t] = dot(turned[...], activation[t]).astype(BF16)
         return carry
 
-    lax.fori_loop(0, PARTS * model_blocks, down_back, 0)
+    lax.fori_loop(0, PARTS, down_back, 0)
     turned[...] = jnp.transpose(first_low[...])
 
     def back(t, carry):
-        def one(i, inner_carry):
-            at = span(i)
-            grad = dot(second_low[at, :], down_ref[t]) * slope[t, at, :]
-            low = grad.astype(BF16)
-            small_out[pl.ds(6 + t, 1), :] += column_sum(low.astype(F32))
-            back_low[at, :] = low
-            second_sum[at, :] += dot_t(low, hidden_ref[t])
-            return inner_carry
-
-        lax.fori_loop(0, blocks, one, 0)
-
-        def weight(i, inner_carry):
-            at = span(i)
-            hidden_grad_out[t, at, :] = dot(turned[at, :], back_low[...]).astype(BF16)
-            return inner_carry
-
-        lax.fori_loop(0, model_blocks, weight, 0)
+        low = (dot(second_low[...], down_ref[t]) * slope[t]).astype(BF16)
+        small_out[pl.ds(6 + t, 1), :] += column_sum(low.astype(F32))
+        back_low[...] = low
+        second_sum[...] += dot_t(low, hidden_ref[t])
+        hidden_grad_out[t] = dot(turned[...], back_low[...]).astype(BF16)
         return carry
 
     lax.fori_loop(0, PARTS, back, 0)
@@ -1011,28 +1070,17 @@
         normed = first_normed[at, :]
         small_out[1:2, :] += column_sum(upstream * normed)
         small_out[2:3, :] += column_sum(upstream)
-        scaled = upstream * first_gain
-        inner = jnp.mean(scaled, axis=-1, keepdims=True)
-        inner = inner + normed * jnp.mean(scaled * normed, axis=-1, keepdims=True)
-        grad = first_scale[at, :] * (scaled - inner)
+        grad = normalized_back(upstream, normed, first_scale[at, :], first_gain)
         small_out[0:1, :] += column_sum(grad)
         first_grad_out[at, :] = grad
-        low = grad.astype(BF16)
-        second_low[at, :] = low
-        for t in range(PARTS):
-            context_grad_out[t, at, :] = dot(low, out_ref[t]).astype(BF16)
+        second_low[at, :] = grad.astype(BF16)
         return carry
 
     lax.fori_loop(0, blocks, last, 0)
     turned[...] = jnp.transpose(second_low[...])
-
-    def out_back(k, carry):
-        t, i = k // model_blocks, k % model_blocks
-        at = span(i)
-        out_grad[t, at, :] = dot(turned[at, :], context_ref[t]).astype(BF16)
-        return carry
-
-    lax.fori_loop(0, PARTS * model_blocks, out_back, 0)
+    for t in range(PARTS):
+        context_grad_out[t] = dot(second_low[...], out_ref[t]).astype(BF16)
+        out_grad[t] = dot(turned[...], context_ref[t]).astype(BF16)
 
 
 def middle(context, x, cotangent, out, hidden, down, vectors, hidden_bias):
@@ -1097,7 +1145,22 @@
     width = query_weight.shape[1]
     units = hidden_weight.shape[1]
     joined = jnp.concatenate([query_weight, key_weight, value_weight], axis=1)
-    all_x, all_joined, all_hidden, all_down, all_out, all_bias = gather(
+    segments = segment_ids.astype(F32).reshape(PARTS, 1, local_rows)
+    (
+        all_x,
+        joined_turned,
+        all_hidden,
+        all_down,
+        all_out,
+        all_bias,
+        queries,
+        keys,
+        values,
+        keys_turned,
+        context,
+        totals,
+        row_context,
+    ) = forward(
         shards,
         tokens,
         joined,
@@ -1105,31 +1168,29 @@
         down_weight.T,
         out_weight.T,
         hidden_bias.astype(F32)[None, :],
+        query_bias.astype(F32)[:, None],
+        value_bias.astype(F32)[:, None],
+        segments,
     )
     all_x = all_x.reshape(group_rows, model)
-    all_joined = all_joined.reshape(model, 3 * width)
     all_hidden = all_hidden.reshape(PARTS, model, units)
     all_down = all_down.reshape(PARTS, model, units)
     all_out = all_out.reshape(PARTS, model, width)
-
+    all_joined = joined_turned.T
+    heads = width // HEAD
+    queries = queries.reshape(PARTS, heads, HEAD, local_rows).transpose(1, 0, 3, 2)
+    queries = queries.reshape(heads, group_rows, HEAD)
+    keys = keys.transpose(1, 0, 2, 3).reshape(heads, group_rows, HEAD)
+    values = values.transpose(1, 0, 2, 3).reshape(heads, group_rows, HEAD)
+    context = context.transpose(0, 2, 1).reshape(group_rows, width)
+    totals = totals[:, :heads].transpose(1, 0, 2).reshape(heads, 1, group_rows)
+    row_context = row_context.transpose(0, 2, 1)
     blocks = group_rows // QUERY_BLOCK
     edges = segment_ids.reshape(blocks, QUERY_BLOCK)
     low = jnp.sum((segment_ids[None, :] < edges[:, :1]).astype(jnp.int32), axis=1)
     high = jnp.sum((segment_ids[None, :] <= edges[:, -1:]).astype(jnp.int32), axis=1)
     low, high = low // KEY_BLOCK, (high + KEY_BLOCK - 1) // KEY_BLOCK
     key_seg, query_seg = segment_ids[:, None], segment_ids[None, :]
-
-    queries, keys, values, context, totals = attention_forward(
-        low,
-        high,
-        all_x,
-        all_joined,
-        query_bias.astype(F32)[None, :],
-        value_bias.astype(F32)[None, :],
-        key_seg,
-        query_seg,
-    )
-    row_context = exchange(shards, 1, context.reshape(PARTS, local_rows, width))
     vectors = jnp.stack(
         [out_bias, first_gain, first_shift, down_bias, second_gain, second_shift]
         + [jnp.zeros_like(out_bias)] * 2

time: 341 us -> 296 us (0.87)
  Pallas kernels: 316 us -> 257 us
  local copies, waits for them, and re-layouts: 18.7 us -> 30.2 us
    pallas_call x1, Pallas kernels: 60.6 us -> 33.8 us  [middle(): pl.pallas_call(middle_kernel, out_shape=(jax.ShapeDtypeStruct((rows, mode...]
    pallas_call x2 -> x1, Pallas kernels: 92.7 us -> 75.6 us  [forward(): pl.pallas_call(functools.partial(forward_kernel, shards), out_shape=(shap...]
    pallas_call x2 -> x1, Pallas kernels: 32.2 us -> 16.2 us  [exchange(): pl.pallas_call(functools.partial(exchange_kernel, shards), out_shape=jax....]
    pallas_call x1, Pallas kernels: 82.6 us -> 90.2 us  [reduce(): pl.pallas_call(functools.partial(reduce_kernel, shards), out_shape=(resul...]
    pallas_call x1, Pallas kernels: 48.3 us -> 41.3 us  [attention_backward(): pl.pallas_call(backward_kernel, out_shape=(jax.ShapeDtypeStruct((model, 3...]
    transpose x0 -> x5, local copies, waits for them, and re-layouts: none -> 3.8 us  [the longest x1 1.28 us: body(): context = context.transpose(0, 2, 1).reshape(group_rows, width)]
    pallas_call x0 -> x2, local copies, waits for them, and re-layouts: none -> 3.76 us  [forward(): pl.pallas_call(functools.partial(forward_kernel, shards), out_shape=(shap...]
    unnamed x27 -> x35, local copies, waits for them, and re-layouts: 7.34 us -> 8.22 us
where the time goes in v2:
time: 296 us; the launch traced here: 295 us
  Pallas kernels  257 us (87%)
  local copies, waits for them, and re-layouts  30.2 us (10%)
  other arithmetic  6.39 us (2%)
    pallas_call x1, Pallas kernels, reduce(): pl.pallas_call(functools.partial(reduce_kernel, shards), out_shape=(resul...  90.2 us
    pallas_call x1, Pallas kernels, forward(): pl.pallas_call(functools.partial(forward_kernel, shards), out_shape=(shap...  75.6 us
    pallas_call x1, Pallas kernels, attention_backward(): pl.pallas_call(backward_kernel, out_shape=(jax.ShapeDtypeStruct((model, 3...  41.3 us
    pallas_call x1, Pallas kernels, middle(): pl.pallas_call(middle_kernel, out_shape=(jax.ShapeDtypeStruct((rows, mode...  33.8 us
    pallas_call x1, Pallas kernels, exchange(): pl.pallas_call(functools.partial(exchange_kernel, shards), out_shape=jax....  16.2 us
    unnamed x35, local copies, waits for them, and re-layouts  8.22 us

profile of v2, /device:TPU:0, one launch (start us, length us, event | category | flops | bytes accessed | tf_op | source)
XLA Modules:
  0.0 294.7 jit_solution(12308812949923269398)
XLA Ops:
  0.7 1.6 pad_maximum_fusion.joined_ref
  2.2 0.7 broadcast_in_dim.40
  2.9 0.8 copy.69.query_bias_ref
  3.7 0.7 broadcast_in_dim.41
  4.3 0.8 copy.70.value_bias_ref
  5.1 1.5 copy.68
  6.6 1.3 convert_element_type.15
  7.9 1.3 reshape.115.bias_ref
  9.2 0.0 copy-start.9
  9.2 0.0 copy-start.10
  9.2 0.0 copy-start.11
  9.2 0.0 copy-start.12
  9.2 0.0 copy-start.13
  9.2 0.0 copy-start.14
  9.2 75.6 %forward.1 = (bf16[4,512,768]{2,1,0:T(8,128)(2,1)}, bf16[576,768]{1,0:T(8,128)(2,1)}, bf16[4,8,96,768]{3,2,1,0:T(8,128)(2,1)}, bf16[4,8,96,768]{3,2,1,0:T(8,128)...) custom-call(bf16[512,768]{1,0:T(8,128)(2,1)} %x_ref.3, ...), custom_call_target="tpu_custom_call" | custom-call | tf_op jit(solution)/shard_map/forward/pallas_call | solution.py:459
  84.8 2.4 copy.71
  87.2 0.0 copy-done.9
  87.3 0.0 copy-done.10
  87.3 0.0 copy-done.11
  87.3 0.0 copy-done.12
  87.3 0.0 copy-done.13
  87.3 0.0 copy-done.14
  87.4 0.6 convert_element_type.16.vectors_ref
  88.0 33.8 %middle.1 = (bf16[512,768]{1,0:T(8,128)(2,1)}, f32[512,768]{1,0:T(8,128)}, bf16[4,512,192]{2,1,0:T(8,128)(2,1)}, bf16[4,768,192]{2,1,0:T(8,128)(2,1)}, bf16[4,76...) custom-call(bf16[4,512,192]{2,1,0:T(8,128)(2,1)} %bitcast.45, bf16[512,768]{1,0:T(8,128)(2,1)} %x_ref.3, ...), custom_call_target="tpu_custom_call" | custom-call | tf_op jit(solution)/shard_map/middle/pallas_call | solution.py:1091
  121.9 0.0 copy-start.4
  121.9 16.2 %exchange_2.1 = bf16[4,512,192]{2,1,0:T(8,128)(2,1)} custom-call(bf16[4,512,192]{2,1,0:T(8,128)(2,1)} %get-tuple-element.57.source), custom_call_target="tpu_custom_call" | custom-call | tf_op jit(solution)/shard_map/exchange_2/pallas_call | solution.py:516
  138.1 0.0 copy-start.1
  138.1 0.0 copy-done.4
  138.1 1.6 copy.73
  139.6 0.0 copy-done.1
  139.7 0.0 copy-start
  139.7 1.2 copy.74
  140.9 0.7 copy-done
  141.6 0.0 copy-start.3
  141.6 1.3 copy.75
  142.9 0.0 copy-start.2
  142.9 0.1 copy-done.3
  143.0 0.0 copy-start.8
  143.0 1.3 copy.76
  144.3 0.0 copy-done.2
  144.3 1.3 copy.72
  145.7 0.0 copy-done.8
  145.7 0.6 reshape.107.total_ref
  146.3 0.0 copy-done.7
  146.3 0.2 slice_reduce_fusion
  146.5 0.2 convert_reduce_fusion
  146.8 0.5 and_select_fusion
  147.3 1.4 copy.78.key_seg_ref
  148.7 41.3 %attention_backward.1 = (bf16[768,576]{1,0:T(8,128)(2,1)}, bf16[2048,768]{1,0:T(8,128)(2,1)}, f32[8,576]{1,0:T(8,128)}) custom-call(s32[8]{0:T(128)} %get-tuple-element.159.low_ref, s32[8]{0:T(128)} %get-tuple-element.158.high_ref, bf16[2048,768]{1,0:T(8,128)(2,1)} %bitcast.49, bf16[768,576]{1,0:T(8,128)(2,1)} %bitcast.47, bf16[3,2048,64]{2,1,0:T(8,128)(2,1)} %bitcast.37, ...), custom_call_target="tpu_custom_call" | custom-call | tf_op jit(solution)/shard_map/attention_backward/pallas_call | solution.py:924
  190.1 0.7 reduce_sum.29
  190.8 0.1 pad_maximum_fusion.1
  190.9 1.4 dynamic_update_slice.3.small_ref
  192.3 90.2 %reduce.19 = (f32[4,128,768]{2,1,0:T(8,128)}, f32[96,576]{1,0:T(8,128)}, f32[96,768]{1,0:T(8,128)}, f32[96,768]{1,0:T(8,128)}, f32[96,192]{1,0:T(8,128)}, /*index=5*/f32[16,768]{1,0:T(8,128)}) custom-call(bf16[4,4,128,768]{3,2,1,0:T(8,128)(2,1)} %bitcast.48, f32[4,128,768]{2,1,0:T(8,128)} %bitcast.50, bf16[8,96,576]{2,1,0:T(8,128)(2,1)} %bitcast.56, ...), custom_call_target="tpu_custom_call" | custom-call | tf_op jit(solution)/shard_map/reduce/pallas_call | solution.py:772
  282.5 1.8 fusion
  284.3 1.6 copy.79
  286.0 1.7 slice_reduce_fusion.2
  287.7 0.8 slice.64
  288.5 0.6 dynamic-slice_reduce_fusion
  289.1 1.4 fusion.1
  290.5 2.7 copy.84
  293.2 0.0 copy-done.6
  293.2 0.7 copy.85
  293.9 0.0 copy-done.5
  293.9 0.7 copy.86
  (17 shorter events, 0.1 us)
Async XLA Ops:
  9.2 78.1 %copy-start.9 = (bf16[768]{0:T(1024)(128)(2,1)S(1)}, bf16[768]{0:T(1024)(128)(2,1)}, u32[]{:S(2)}) copy-start(bf16[768]{0:T(1024)(128)(2,1)} %param.26) | copy-start | bytes 4612
  9.2 78.1 %copy-start.10 = (bf16[768]{0:T(1024)(128)(2,1)S(1)}, bf16[768]{0:T(1024)(128)(2,1)}, u32[]{:S(2)}) copy-start(bf16[768]{0:T(1024)(128)(2,1)} %param.27) | copy-start | bytes 4612
  9.2 78.1 %copy-start.11 = (bf16[768]{0:T(1024)(128)(2,1)S(1)}, bf16[768]{0:T(1024)(128)(2,1)}, u32[]{:S(2)}) copy-start(bf16[768]{0:T(1024)(128)(2,1)} %param.28) | copy-start | bytes 4612
  9.2 78.1 %copy-start.12 = (bf16[768]{0:T(1024)(128)(2,1)S(1)}, bf16[768]{0:T(1024)(128)(2,1)}, u32[]{:S(2)}) copy-start(bf16[768]{0:T(1024)(128)(2,1)} %param.32) | copy-start | bytes 4612
  9.2 78.1 %copy-start.13 = (bf16[768]{0:T(1024)(128)(2,1)S(1)}, bf16[768]{0:T(1024)(128)(2,1)}, u32[]{:S(2)}) copy-start(bf16[768]{0:T(1024)(128)(2,1)} %param.33) | copy-start | bytes 4612
  9.2 78.2 %copy-start.14 = (bf16[768]{0:T(1024)(128)(2,1)S(1)}, bf16[768]{0:T(1024)(128)(2,1)}, u32[]{:S(2)}) copy-start(bf16[768]{0:T(1024)(128)(2,1)} %param.34) | copy-start | bytes 4612
  121.9 16.2 %copy-start.4 = (bf16[4,192,512]{2,1,0:T(8,128)(2,1)S(1)}, bf16[4,192,512]{2,1,0:T(8,128)(2,1)}, u32[]{:S(2)}) copy-start(bf16[4,192,512]{2,1,0:T(8,128)(2,1)} %get-tuple-element.53) | copy-start | bytes 2359300
  138.1 1.6 copy-start.1
  139.7 2.0 copy-start
  141.6 1.4 copy-start.3
  142.9 1.4 copy-start.2
  143.0 2.6 copy-start.8
  143.0 3.3 %copy-start.7 = (s32[2048]{0:T(1024)S(1)}, s32[2048]{0:T(1024)}, u32[]{:S(2)}) copy-start(s32[2048]{0:T(1024)} %param.19) | copy-start | bytes 24580
  290.5 2.7 copy-start.6
  290.5 3.4 %copy-start.5 = (f32[96,768]{1,0:T(8,128)S(1)}, f32[96,768]{1,0:T(8,128)}, u32[]{:S(2)}) copy-start(f32[96,768]{1,0:T(8,128)} %get-tuple-element.72) | copy-start | bytes 884740

commit v3 on v2

--- a/solution.py
+++ b/solution.py
@@ -498,34 +498,8 @@
     )(x, joined, hidden, down, out, bias, query_bias, value_bias, segments)
 
 
-def exchange_kernel(shards, source, target, send, recv):
-    links = Links(shards, send, recv)
-    part = links.part
-    diagonal = (links.other_core + 2) % PARTS
-    links.barrier(ring=False, diagonal=True)
-    partners = (links.other_row, diagonal, links.other_core)
-    for number, partner in enumerate(partners):
-        links.start(number, source.at[partner], target.at[part], {"tensor": partner})
-    target[part] = source[part]
-    for number, partner in enumerate(partners):
-        links.arrive(number, target.at[partner], {"tensor": partner})
-    links.finish()
-
-
-def exchange(shards, identity, pieces):
-    return pl.pallas_call(
-        functools.partial(exchange_kernel, shards),
-        out_shape=jax.ShapeDtypeStruct(pieces.shape, pieces.dtype),
-        in_specs=[vmem()],
-        out_specs=vmem(),
-        scratch_shapes=[pltpu.SemaphoreType.DMA((3,)), pltpu.SemaphoreType.DMA((3,))],
-        compiler_params=pltpu.CompilerParams(collective_id=identity, has_side_effects=True),
-        name=f"exchange_{identity}",
-    )(pieces)
-
-
 def plus(left, right):
-    return (left.astype(F32) + right.astype(F32)).astype(BF16)
+    return left + right
 
 
 class RingSum:
@@ -552,9 +526,8 @@
             number = self.links.number()
             self.numbers[step, way] = number
             partner = {"dp": self.links.right if way > 0 else self.links.left}
-            j = self.links.at(way * (self.half - step + 1))
             if step == 1:
-                source = self.part(self.term(j), 1, way)
+                source = self.part(self.term(self.half), 1, way)
             else:
                 source = self.slot(step - 1, way)
             self.links.start(
@@ -568,8 +541,7 @@
         if step == self.half:
             return
         for way in (1, -1):
-            j = self.links.at(way * (self.half - step))
-            term, slot = self.term(j), self.slot(step, way)
+            term, slot = self.term(way * (self.half - step)), self.slot(step, way)
             if way not in self.ways(step):
                 slot[...] = term[...]
             elif step == 1 and self.split:
@@ -581,37 +553,57 @@
                 slot[...] = plus(slot[...], term[...])
 
     def total(self):
-        own = self.term(self.links.dp)[...].astype(F32)
+        own = self.term(0)[...].astype(F32)
         total = own + self.slot(self.half, 1)[...].astype(F32)
         if self.half > 1 or self.split:
             total = total + self.slot(self.half, -1)[...].astype(F32)
         return total
 
 
-def reduce_copies(shards):
-    return 40 + 6 * shards
-
-
-def reduce_kernel(
+def backward_copies(shards):
+    return 50 + 8 * shards
+
+
+def backward_kernel(
     shards,
-    rows_ref,
+    context_grad_ref,
     base_ref,
-    joined_ref,
     hidden_ref,
     down_ref,
     out_ref,
     small_ref,
+    x_ref,
+    joined_ref,
+    query_ref,
+    key_turned_ref,
+    key_ref,
+    value_ref,
+    context_ref,
+    total_ref,
+    segment_ref,
     rows_out,
     joined_out,
     hidden_out,
     down_out,
     out_out,
     small_out,
+    bias_out,
+    upstream,
+    key_segments,
+    key_sum,
+    value_sum,
+    projected,
+    weight_sum,
+    joined_terms,
+    rows_send,
     rows_two,
     rows_far,
+    hidden_own,
     hidden_two,
     hidden_far,
+    down_own,
     down_two,
+    out_own,
     out_two,
     joined_slots,
     hidden_slots,
@@ -621,327 +613,368 @@
     out_pair,
     small_slots,
     small_sums,
+    bias_slots,
+    bias_sums,
     send,
     recv,
+    local,
 ):
-    links = Links(shards, send, recv)
-    core, row = links.core, links.row
+    links = Links(shards, send, recv, local)
+    core, row, part = links.core, links.row, links.part
     across, beside = {"tensor": links.other_row}, {"tensor": links.other_core}
-    links.barrier(cube=True)
+    links.barrier(diagonal=True, cube=True)
     half = shards // 2
-    rows = joined_ref.shape[1]
-
-    beside_numbers = {}
+    rows = joined_terms.shape[1]
+    width = query_ref.shape[1]
+    heads = width // HEAD
+    scale = HEAD ** (-0.5)
+    places = (part, links.other_core, links.other_row, links.diagonal)
+
+    numbers = {}
 
     def to_core(name, array, slots, y):
-        number = links.number()
-        beside_numbers[name, y] = number
-        links.start(number, array.at[2 * y + 1 - core], slots.at[y], beside)
-
-    joined = RingSum(links, rows, lambda j: joined_ref.at[j], joined_slots)
-    joined.send(1)
+        numbers[name, y] = links.number()
+        links.start(numbers[name, y], array.at[2 * y + 1 - core], slots.at[y], beside)
+
+    def own_half(array, own):
+        for y in range(2):
+            links.keep(array.at[2 * y + core], own.at[y])
+        return links.copies[-2:]
+
+    for n in range(1, 4):
+        numbers["upstream", n] = links.number()
+        links.start(
+            numbers["upstream", n],
+            context_grad_ref.at[places[n]],
+            upstream.at[part],
+            {"tensor": places[n]},
+        )
     for y in range(2):
         to_core("down", down_ref, down_two, y)
     for y in range(2):
         to_core("out", out_ref, out_two, y)
-    for y in range(2):
-        to_core("hidden", hidden_ref, hidden_two, y)
-    for y in range(2):
-        to_core("rows", rows_ref, rows_two, y)
-
-    def add_core(name, array, slots, y, count):
-        links.arrive(beside_numbers[name, y], slots.at[y], beside)
+    numbers["hidden", 0] = links.number()
+    numbers["hidden", 1] = links.number()
+    links.start(
+        numbers["hidden", 0], hidden_ref.at[2 * (1 - row) + 1 - core], hidden_two.at[1 - row], beside
+    )
+    links.start(numbers["hidden", 1], hidden_ref.at[2 * row + 1 - core], hidden_two.at[row], beside)
+    copies = {
+        "down": own_half(down_ref, down_own),
+        "out": own_half(out_ref, out_own),
+        "hidden": own_half(hidden_ref, hidden_own),
+    }
+    upstream[part] = context_grad_ref[part]
+
+    cube = [{"dp": index} for index in links.cube()]
+
+    class Pairwise:
+        def __init__(self, source, slots, sums, result, partners):
+            self.source, self.slots, self.sums = source, slots, sums
+            self.result, self.partners, self.numbers = result, partners, []
+            self.send(source)
+
+        def send(self, source):
+            step = len(self.numbers)
+            self.numbers.append(links.number())
+            links.start(self.numbers[-1], source, self.slots.at[step], self.partners[step])
+
+        def step(self):
+            step = len(self.numbers) - 1
+            links.arrive(self.numbers[step], self.slots.at[step], self.partners[step])
+            mine = self.source[...] if step == 0 else self.sums[step - 1]
+            total = mine + self.slots[step]
+            if step == len(self.partners) - 1:
+                self.result[...] = total
+            else:
+                self.sums[step] = total
+                self.send(self.sums.at[step])
+
+    small = Pairwise(small_ref, small_slots, small_sums, small_out, cube + [beside, across])
+    small_left = [small.step] * len(small.partners)
+
+    def small_step():
+        if small_left:
+            small_left.pop()()
+
+    def add_core(name, own, slots, y, number):
+        if copies[name]:
+            for copy in copies.pop(name):
+                copy.wait()
+                links.copies.remove(copy)
+            copies[name] = None
+        links.arrive(number, slots.at[y], beside)
 
         def one(i, carry):
-            slots[y, i] = plus(slots[y, i], array[2 * y + core, i])
+            slots[y, i] = plus(slots[y, i], own[y, i])
             return carry
 
-        lax.fori_loop(0, count, one, 0)
-
-    small_numbers = []
-
-    def small_send(step, source):
-        number = links.number()
-        small_numbers.append(number)
-        links.start(number, source, small_slots.at[step], small_partners[step])
-
-    small_partners = [{"dp": index} for index in links.cube()] + [beside, across]
-    small_send(0, small_ref)
-
-    def small_step(step):
-        links.arrive(small_numbers[step], small_slots.at[step], small_partners[step])
-        mine = small_ref[...] if step == 0 else small_sums[step - 1]
-        got = small_slots[step]
-        if step >= len(small_partners) - 2:
-            common = lax.broadcasted_iota(jnp.int32, got.shape, 0) < 10
-            got = jnp.where(common, got, 0.0)
-        total = mine + got
-        if step == len(small_partners) - 1:
-            small_out[...] = total
-        else:
-            small_sums[step] = total
-            small_send(step + 1, small_sums.at[step])
-
-    down_rings, out_rings = [], []
-    for y in range(2):
-        add_core("down", down_ref, down_two, y, shards)
-        ring = RingSum(links, rows, lambda j, y=y: down_two.at[y, j], down_slots.at[y])
-        ring.send(1)
-        down_rings.append(ring)
-    for y in range(2):
-        add_core("out", out_ref, out_two, y, shards)
-        ring = RingSum(links, rows, lambda j, y=y: out_two.at[y, j], out_slots.at[y])
-        ring.send(1)
-        out_rings.append(ring)
-    joined.arrive(1)
-    joined.send(2)
-    for y in range(2):
-        add_core("hidden", hidden_ref, hidden_two, y, shards)
-    hidden_number = links.number()
-    links.start(hidden_number, hidden_two.at[1 - row], hidden_far, across)
-    for y in range(2):
-        add_core("rows", rows_ref, rows_two, y, rows_ref.shape[1])
-    rows_number = links.number()
-    links.start(rows_number, rows_two.at[1 - row], rows_far, across)
-    small_step(0)
-    for ring in down_rings + out_rings:
-        ring.arrive(1)
-        ring.send(2)
-    if half > 2:
-        joined.arrive(2)
-        joined.send(3)
-    links.arrive(hidden_number, hidden_far, across)
-
-    def one(i, carry):
-        hidden_far[i] = plus(hidden_far[i], hidden_two[row, i])
-        return carry
-
-    lax.fori_loop(0, shards, one, 0)
-    hidden = RingSum(links, rows, lambda j: hidden_far.at[j], hidden_slots)
-    hidden.send(1)
-    small_step(1)
-    for step in range(2, half + 1):
-        for ring in down_rings + out_rings:
+        lax.fori_loop(0, shards, one, 0)
+
+    rings = []
+
+    def begin():
+        for name, own, slots, ring_slots in (
+            ("down", down_own, down_two, down_slots),
+            ("out", out_own, out_two, out_slots),
+        ):
+            for y in range(2):
+                add_core(name, own, slots, y, numbers[name, y])
+                term = lambda o, y=y, slots=slots: slots.at[y, links.at(o)]
+                rings.append(RingSum(links, rows, term, ring_slots.at[y]))
+                rings[-1].send(1)
+        add_core("hidden", hidden_own, hidden_two, 1 - row, numbers["hidden", 0])
+        order = [half] + [way * o for o in range(half - 1, 0, -1) for way in (1, -1)] + [0]
+        for o in order:
+            numbers["far", o % shards] = links.number()
+            j = links.at(o)
+            links.start(
+                numbers["far", o % shards], hidden_two.at[1 - row, j], hidden_far.at[j], across
+            )
+
+    ready = set()
+
+    def hidden_term(o):
+        j = links.at(o)
+        if o % shards not in ready:
+            ready.add(o % shards)
+            links.arrive(numbers["far", o % shards], hidden_far.at[j], across)
+            hidden_far[j] = plus(hidden_far[j], hidden_two[row, j])
+        return hidden_far.at[j]
+
+    hidden = RingSum(links, rows, hidden_term, hidden_slots)
+
+    def ring_step(step):
+        for ring in rings:
             ring.arrive(step)
             if step < half:
                 ring.send(step + 1)
-        if step + 1 <= half:
-            joined.arrive(step + 1)
-            if step + 1 < half:
-                joined.send(step + 2)
-        if step < len(small_partners):
-            small_step(step)
-        hidden.arrive(step - 1)
-        hidden.send(step)
-    for step in range(half + 1, len(small_partners)):
-        small_step(step)
-    links.arrive(rows_number, rows_far, across)
-
-    def last(i, carry):
-        rows_out[i] = (
-            base_ref[i]
-            + rows_two[row, i].astype(F32)
-            + rows_far[i].astype(F32)
-        )
-        return carry
-
-    lax.fori_loop(0, rows_out.shape[0], last, 0)
+
+    def hidden_step(step):
+        if step == 0:
+            add_core("hidden", hidden_own, hidden_two, row, numbers["hidden", 1])
+        else:
+            hidden.arrive(step)
+        if step < half:
+            hidden.send(step + 1)
+
+    turned_segments(segment_ref, key_segments)
+    key_sum[...] = jnp.zeros_like(key_sum)
+    value_sum[...] = jnp.zeros_like(value_sum)
+
+    for n in range(PARTS):
+        i = places[n]
+        if n > 0:
+            links.arrive(numbers["upstream", n], upstream.at[i], {"tensor": i})
+        low, high = near(i, PARTS)
+        spans = [slice(h * HEAD, (h + 1) * HEAD) for h in range(heads)]
+        inner = [
+            jnp.sum(
+                upstream[i, span, :].astype(F32) * context_ref[i, span, :].astype(F32),
+                axis=0,
+                keepdims=True,
+            )
+            for span in spans
+        ]
+        totals = [total_ref[i, h : h + 1, :] for h in range(heads)]
+
+        def block(j, sums):
+            allowed = allowed_block(key_segments, segment_ref, i, j)
+            found = []
+            for h in range(heads):
+                span = spans[h]
+                queries, grads = query_ref[i, span, :], upstream[i, span, :]
+                scores = jnp.where(allowed, dot(key_ref[j, h], queries), NEGATIVE)
+                shares = jnp.exp(scores - totals[h])
+                share_grad = dot(value_ref[j, h], grads)
+                score_grad = (shares * (share_grad - inner[h])).astype(BF16)
+                value_sum[j, span, :] += dot_t(grads, shares.astype(BF16))
+                key_sum[j, span, :] += dot_t(queries, score_grad)
+                found.append(sums[h] + dot(key_turned_ref[j, span, :], score_grad))
+            return tuple(found)
+
+        empty = jnp.zeros((HEAD, BLOCK), F32)
+        sums = lax.fori_loop(low, high, block, (empty,) * heads)
+        for h in range(heads):
+            projected[i, spans[h], :] = (sums[h] * scale).astype(BF16)
+        if n == 0:
+            begin()
+        else:
+            ring_step(n)
+            hidden_step(n - 1)
+        small_step()
+
+    for s in range(PARTS):
+        projected[s, width : 2 * width, :] = key_sum[s].astype(BF16)
+        projected[s, 2 * width :, :] = value_sum[s].astype(BF16)
+
+    def x_grad(s):
+        return dot(jnp.transpose(projected[s]), joined_ref[...]).astype(BF16)
+
+    def x_across(s_beside, s_own, y, name):
+        rows_send[y] = x_grad(s_beside)
+        numbers[name] = links.number()
+        links.start(numbers[name], rows_send.at[y], rows_two.at[y], beside)
+        return x_grad(s_own)
+
+    mine = x_across(links.diagonal, links.other_row, 1 - row, "rows far")
+    rows_send_far = rows_send.at[2]
+    rows_send_far[...] = mine
+    ones = jnp.ones((8, BLOCK), BF16)
+    bias = dot_t(ones, projected[0])
+    for s in range(1, PARTS):
+        bias = bias + dot_t(ones, projected[s])
+    bias_sums[bias_sums.shape[0] - 1] = bias
+    sums_of = Pairwise(bias_sums.at[bias_sums.shape[0] - 1], bias_slots, bias_sums, bias_out, cube)
+    links.arrive(numbers["rows far"], rows_two.at[1 - row], beside)
+    rows_two[1 - row] = plus(rows_two[1 - row], rows_send_far[...])
+    rows_number = links.number()
+    links.start(rows_number, rows_two.at[1 - row], rows_far, across)
+
+    weight = dot(projected[0], x_ref[0])
+    for s in range(1, PARTS):
+        weight = weight + dot(projected[s], x_ref[s])
+    weight_sum[...] = weight
+    turned = jnp.transpose(weight_sum[...]).astype(BF16)
+    joined_terms[...] = turned.reshape(joined_terms.shape)
+    joined = RingSum(links, rows, lambda o: joined_terms.at[links.at(o)], joined_slots)
+    joined.send(1)
+
+    mine = x_across(links.other_core, part, row, "rows own")
+    rows_out[...] = base_ref[...] + mine.astype(F32)
+    sums_of.step()
+    small_step()
+    for step in range(PARTS, half + 1):
+        ring_step(step)
+        hidden_step(step - 1)
+        small_step()
     pairs = []
-    for rings, pair, result in ((down_rings, down_pair, down_out), (out_rings, out_pair, out_out)):
+    for pair_rings, pair, result in (
+        (rings[:2], down_pair, down_out),
+        (rings[2:], out_pair, out_out),
+    ):
         for y in range(2):
-            pair[y] = rings[y].total().astype(BF16)
+            pair[y] = pair_rings[y].total().astype(BF16)
         number = links.number()
         links.start(number, pair.at[1 - row], pair.at[2], across)
         pairs.append((number, pair, result))
-    joined_out[...] = joined.total()
+    joined.arrive(1)
+    joined.send(2)
+    links.arrive(numbers["rows own"], rows_two.at[row], beside)
+    rows_out[...] += rows_two[row].astype(F32)
+    for _ in range(len(cube) - 1):
+        sums_of.step()
+    while small_left:
+        small_step()
+    for step in range(2, half):
+        joined.arrive(step)
+        joined.send(step + 1)
     hidden.arrive(half)
     hidden_out[...] = hidden.total()
+    joined.arrive(half)
+    joined_out[...] = joined.total()
+    links.arrive(rows_number, rows_far, across)
+    rows_out[...] += rows_far[...].astype(F32)
     for number, pair, result in pairs:
         links.arrive(number, pair.at[2], across)
         result[...] = pair[row].astype(F32) + pair[2].astype(F32)
     links.finish()
-    assert links.used <= reduce_copies(shards), links.used
-
-
-def reduce(shards, rows, base, joined, hidden, down, out, small):
+    assert links.used <= backward_copies(shards), links.used
+
+
+def backward(
+    shards,
+    context_grad,
+    base,
+    hidden,
+    down,
+    out,
+    small,
+    x,
+    joined,
+    queries,
+    keys_turned,
+    keys,
+    values,
+    context,
+    totals,
+    segments,
+):
     half = shards // 2
-    count = reduce_copies(shards)
+    count = backward_copies(shards)
     stages = (shards - 1).bit_length() + 2
-    scratch = lambda *dims: pltpu.VMEM(dims, BF16)
+    rows, model = base.shape
+    width = queries.shape[1]
+    low = lambda *dims: pltpu.VMEM(dims, BF16)
+    wide = lambda *dims: pltpu.VMEM(dims, F32)
     result = lambda *dims: jax.ShapeDtypeStruct(dims, F32)
+    shard = (model // shards, 3 * width)
     return pl.pallas_call(
-        functools.partial(reduce_kernel, shards),
+        functools.partial(backward_kernel, shards),
         out_shape=(
-            result(*base.shape),
-            result(*joined.shape[1:]),
+            result(rows, model),
+            result(*shard),
             result(*hidden.shape[2:]),
             result(*down.shape[2:]),
             result(*out.shape[2:]),
             result(*small.shape),
+            result(8, 3 * width),
         ),
-        in_specs=[vmem()] * 7,
-        out_specs=[vmem()] * 6,
+        in_specs=[vmem()] * 2 + [anywhere()] * 3 + [vmem()] * 10,
+        out_specs=[vmem()] * 7,
         scratch_shapes=[
-            scratch(2, *rows.shape[1:]),
-            scratch(*rows.shape[1:]),
-            scratch(2, *hidden.shape[1:]),
-            scratch(*hidden.shape[1:]),
-            scratch(2, *down.shape[1:]),
-            scratch(2, *out.shape[1:]),
-            scratch(half, 2, *joined.shape[1:]),
-            scratch(half, 2, *hidden.shape[2:]),
-            scratch(2, half, 2, *down.shape[2:]),
-            scratch(2, half, 2, *out.shape[2:]),
-            scratch(3, *down.shape[2:]),
-            scratch(3, *out.shape[2:]),
-            pltpu.VMEM((stages, *small.shape), F32),
-            pltpu.VMEM((stages, *small.shape), F32),
+            low(*context_grad.shape),
+            wide(PARTS, BLOCK, 128),
+            wide(PARTS, width, rows),
+            wide(PARTS, width, rows),
+            low(PARTS, 3 * width, rows),
+            wide(3 * width, model),
+            low(shards, *shard),
+            low(3, rows, model),
+            low(2, rows, model),
+            low(rows, model),
+            low(2, *hidden.shape[1:]),
+            low(2, *hidden.shape[1:]),
+            low(*hidden.shape[1:]),
+            low(2, *down.shape[1:]),
+            low(2, *down.shape[1:]),
+            low(2, *out.shape[1:]),
+            low(2, *out.shape[1:]),
+            low(half, 2, *shard),
+            low(half, 2, *hidden.shape[2:]),
+            low(2, half, 2, *down.shape[2:]),
+            low(2, half, 2, *out.shape[2:]),
+            low(3, *down.shape[2:]),
+            low(3, *out.shape[2:]),
+            wide(stages, *small.shape),
+            wide(stages, *small.shape),
+            wide(stages, 8, 3 * width),
+            wide(stages, 8, 3 * width),
             pltpu.SemaphoreType.DMA((count,)),
             pltpu.SemaphoreType.DMA((count,)),
+            pltpu.SemaphoreType.DMA((6,)),
         ],
         compiler_params=pltpu.CompilerParams(
             collective_id=3, has_side_effects=True, vmem_limit_bytes=VMEM_LIMIT
         ),
-        name="reduce",
-    )(rows, base, joined, hidden, down, out, small)
-
-
-QUERY_BLOCK = 256
-KEY_BLOCK = 256
-
-
-def backward_kernel(
-    low_ref,
-    high_ref,
-    x_ref,
-    weight_ref,
-    query_ref,
-    key_ref,
-    value_ref,
-    context_ref,
-    upstream_ref,
-    total_ref,
-    key_seg_ref,
-    query_seg_ref,
-    weight_out,
-    x_out,
-    bias_out,
-    upstream_heads,
-    key_turned,
-    inner_rows,
-    key_sum,
-    value_sum,
-    projected,
-    weight_sum,
-):
-    heads = query_ref.shape[0]
-    width = heads * HEAD
-    scale = HEAD ** (-0.5)
-    rows = x_ref.shape[0]
-    steps = rows // QUERY_BLOCK
-
-    def prepare(i, carry):
-        at = pl.ds(pl.multiple_of(i * QUERY_BLOCK, QUERY_BLOCK), QUERY_BLOCK)
-        upstream = upstream_ref[at, :]
-        product = upstream.astype(F32) * context_ref[at, :].astype(F32)
-        chooser = (
-            lax.broadcasted_iota(jnp.int32, (8, width), 1) // HEAD
-            == lax.broadcasted_iota(jnp.int32, (8, width), 0)
-        ).astype(F32)
-        inner_rows[:, at] = lax.dot_general(
-            chooser,
-            product,
-            (((1,), (1,)), ((), ())),
-            preferred_element_type=F32,
-            precision=lax.Precision.HIGHEST,
-        )
-        for h in range(heads):
-            upstream_heads[h, at, :] = upstream[:, h * HEAD : (h + 1) * HEAD]
-            key_turned[h, :, at] = jnp.transpose(key_ref[h, at, :].astype(F32)).astype(BF16)
-            key_sum[h, at, :] = jnp.zeros((QUERY_BLOCK, HEAD), F32)
-            value_sum[h, at, :] = jnp.zeros((QUERY_BLOCK, HEAD), F32)
-        return carry
-
-    lax.fori_loop(0, steps, prepare, 0)
-
-    def attend(i, carry):
-        at = pl.ds(pl.multiple_of(i * QUERY_BLOCK, QUERY_BLOCK), QUERY_BLOCK)
-        query_seg = query_seg_ref[:, at]
-        inner = [inner_rows[h : h + 1, at] for h in range(heads)]
-        totals = [total_ref[h, :, at] for h in range(heads)]
-
-        def block(j, sums):
-            there = pl.ds(pl.multiple_of(j * KEY_BLOCK, KEY_BLOCK), KEY_BLOCK)
-            allowed = key_seg_ref[there, :] == query_seg
-            found = []
-            for h in range(heads):
-                queries = query_ref[h, at, :]
-                upstream = upstream_heads[h, at, :]
-                scores = dot_t(key_ref[h, there, :], queries)
-                shares = jnp.exp(jnp.where(allowed, scores, NEGATIVE) - totals[h])
-                share_grad = dot_t(value_ref[h, there, :], upstream)
-                score_grad = (shares * (share_grad - inner[h])).astype(BF16)
-                value_sum[h, there, :] += dot(shares.astype(BF16), upstream)
-                key_sum[h, there, :] += dot(score_grad, queries)
-                found.append(sums[h] + dot(key_turned[h, :, there], score_grad))
-            return tuple(found)
-
-        empty = jnp.zeros((HEAD, QUERY_BLOCK), F32)
-        sums = lax.fori_loop(low_ref[i], high_ref[i], block, (empty,) * heads)
-        queries = jnp.transpose(jnp.concatenate(sums, axis=0)) * scale
-        projected[at, :width] = queries.astype(BF16)
-        return carry
-
-    lax.fori_loop(0, steps, attend, 0)
-    weight_sum[...] = jnp.zeros_like(weight_sum)
-    bias_out[...] = jnp.zeros_like(bias_out)
-
-    def finish(i, carry):
-        at = pl.ds(pl.multiple_of(i * QUERY_BLOCK, QUERY_BLOCK), QUERY_BLOCK)
-        for h in range(heads):
-            columns = slice(width + h * HEAD, width + (h + 1) * HEAD)
-            projected[at, columns] = key_sum[h, at, :].astype(BF16)
-            columns = slice(2 * width + h * HEAD, 2 * width + (h + 1) * HEAD)
-            projected[at, columns] = value_sum[h, at, :].astype(BF16)
-        block = projected[at, :]
-        bias_out[...] += jnp.sum(fold_rows(block.astype(F32)), axis=0)
-        weight_sum[...] += lax.dot_general(
-            x_ref[at, :], block, (((0,), (0,)), ((), ())), preferred_element_type=F32
-        )
-        x_out[at, :] = dot_t(block, weight_ref[...]).astype(BF16)
-        return carry
-
-    lax.fori_loop(0, steps, finish, 0)
-    weight_out[...] = weight_sum[...].astype(BF16)
-
-
-def attention_backward(
-    low, high, x, weight, queries, keys, values, context, upstream, totals, key_seg, query_seg
-):
-    rows, model = x.shape
-    heads = queries.shape[0]
-    width = heads * HEAD
-    return pl.pallas_call(
-        backward_kernel,
-        out_shape=(
-            jax.ShapeDtypeStruct((model, 3 * width), BF16),
-            jax.ShapeDtypeStruct((rows, model), BF16),
-            jax.ShapeDtypeStruct((8, 3 * width), F32),
-        ),
-        in_specs=[smem()] * 2 + [vmem()] * 10,
-        out_specs=[vmem()] * 3,
-        scratch_shapes=[
-            pltpu.VMEM((heads, rows, HEAD), BF16),
-            pltpu.VMEM((heads, HEAD, rows), BF16),
-            pltpu.VMEM((8, rows), F32),
-            pltpu.VMEM((heads, rows, HEAD), F32),
-            pltpu.VMEM((heads, rows, HEAD), F32),
-            pltpu.VMEM((rows, 3 * width), BF16),
-            pltpu.VMEM((model, 3 * width), F32),
-        ],
-        compiler_params=pltpu.CompilerParams(vmem_limit_bytes=VMEM_LIMIT),
-        name="attention_backward",
-    )(low, high, x, weight, queries, keys, values, context, upstream, totals, key_seg, query_seg)
+        name="backward",
+    )(
+        context_grad,
+        base,
+        hidden,
+        down,
+        out,
+        small,
+        x,
+        joined,
+        queries,
+        keys_turned,
+        keys,
+        values,
+        context,
+        totals,
+        segments,
+    )
 
 
 ROW_BLOCK = 128
@@ -1004,7 +1037,7 @@
     blocks = rows // ROW_BLOCK
     attended = x_ref[...].astype(F32) + out_bias
     for t in range(PARTS):
-        attended = attended + dot_t(context_ref[t], out_ref[t])
+        attended = attended + dot_t(jnp.transpose(context_ref[t]), out_ref[t])
     first_norm[...] = attended
 
     def first(i, carry):
@@ -1079,13 +1112,14 @@
     lax.fori_loop(0, blocks, last, 0)
     turned[...] = jnp.transpose(second_low[...])
     for t in range(PARTS):
-        context_grad_out[t] = dot(second_low[...], out_ref[t]).astype(BF16)
-        out_grad[t] = dot(turned[...], context_ref[t]).astype(BF16)
+        grads = dot(second_low[...], out_ref[t])
+        context_grad_out[t] = jnp.transpose(grads).astype(BF16)
+        out_grad[t] = dot_t(turned[...], context_ref[t]).astype(BF16)
 
 
 def middle(context, x, cotangent, out, hidden, down, vectors, hidden_bias):
     rows, model = x.shape
-    width, units = context.shape[2], hidden.shape[2]
+    width, units = context.shape[1], hidden.shape[2]
     big = pltpu.VMEM((rows, model), F32)
     low = pltpu.VMEM((rows, model), BF16)
     return pl.pallas_call(
@@ -1093,7 +1127,7 @@
         out_shape=(
             jax.ShapeDtypeStruct((rows, model), BF16),
             jax.ShapeDtypeStruct((rows, model), F32),
-            jax.ShapeDtypeStruct((PARTS, rows, width), BF16),
+            jax.ShapeDtypeStruct((PARTS, width, rows), BF16),
             jax.ShapeDtypeStruct((PARTS, model, width), BF16),
             jax.ShapeDtypeStruct((PARTS, model, units), BF16),
             jax.ShapeDtypeStruct((PARTS, model, units), BF16),
@@ -1141,7 +1175,6 @@
 ):
     part = lax.axis_index("tensor")
     local_rows, model = tokens.shape
-    group_rows = local_rows * PARTS
     width = query_weight.shape[1]
     units = hidden_weight.shape[1]
     joined = jnp.concatenate([query_weight, key_weight, value_weight], axis=1)
@@ -1172,25 +1205,9 @@
         value_bias.astype(F32)[:, None],
         segments,
     )
-    all_x = all_x.reshape(group_rows, model)
     all_hidden = all_hidden.reshape(PARTS, model, units)
     all_down = all_down.reshape(PARTS, model, units)
     all_out = all_out.reshape(PARTS, model, width)
-    all_joined = joined_turned.T
-    heads = width // HEAD
-    queries = queries.reshape(PARTS, heads, HEAD, local_rows).transpose(1, 0, 3, 2)
-    queries = queries.reshape(heads, group_rows, HEAD)
-    keys = keys.transpose(1, 0, 2, 3).reshape(heads, group_rows, HEAD)
-    values = values.transpose(1, 0, 2, 3).reshape(heads, group_rows, HEAD)
-    context = context.transpose(0, 2, 1).reshape(group_rows, width)
-    totals = totals[:, :heads].transpose(1, 0, 2).reshape(heads, 1, group_rows)
-    row_context = row_context.transpose(0, 2, 1)
-    blocks = group_rows // QUERY_BLOCK
-    edges = segment_ids.reshape(blocks, QUERY_BLOCK)
-    low = jnp.sum((segment_ids[None, :] < edges[:, :1]).astype(jnp.int32), axis=1)
-    high = jnp.sum((segment_ids[None, :] <= edges[:, -1:]).astype(jnp.int32), axis=1)
-    low, high = low // KEY_BLOCK, (high + KEY_BLOCK - 1) // KEY_BLOCK
-    key_seg, query_seg = segment_ids[:, None], segment_ids[None, :]
     vectors = jnp.stack(
         [out_bias, first_gain, first_shift, down_bias, second_gain, second_shift]
         + [jnp.zeros_like(out_bias)] * 2
@@ -1204,47 +1221,34 @@
         down_grad,
         small,
     ) = middle(row_context, tokens, output_cotangent, all_out, all_hidden, all_down, vectors, all_bias)
-    upstream = exchange(shards, 2, context_grad).reshape(group_rows, width)
-    joined_grad, x_grad, bias_grad = attention_backward(
-        low,
-        high,
-        all_x,
-        all_joined,
-        queries,
-        keys,
-        values,
-        context,
-        upstream,
-        totals,
-        key_seg,
-        query_seg,
-    )
-    bias_grad = jnp.sum(bias_grad, axis=0)
-    bias_row = jnp.concatenate(
-        [bias_grad[:width], bias_grad[2 * width :], jnp.zeros((model - 2 * width,), F32)]
-    )
-    small = lax.dynamic_update_slice(small, bias_row[None, :], (10, 0))
     rows = model // shards
-    chunks = local_rows // 128
-    tokens_gradient, joined_grad, hidden_grad, down_grad, out_grad, small = reduce(
+    tokens_gradient, joined_grad, hidden_grad, down_grad, out_grad, small, bias_grad = backward(
         shards,
-        x_grad.reshape(PARTS, chunks, 128, model),
-        first_grad.reshape(chunks, 128, model),
-        joined_grad.reshape(shards, rows, 3 * width),
+        context_grad,
+        first_grad,
         hidden_grad.reshape(PARTS, shards, rows, units),
         down_grad.reshape(PARTS, shards, rows, units),
         out_grad.reshape(PARTS, shards, rows, width),
         small,
+        all_x,
+        joined_turned,
+        queries,
+        keys_turned,
+        keys,
+        values,
+        context,
+        totals,
+        segments,
     )
     hidden_bias_gradient = lax.dynamic_index_in_dim(small[6:10], part, 0, keepdims=False)
     return (
         layer_output,
-        tokens_gradient.reshape(local_rows, model),
+        tokens_gradient,
         joined_grad[:, :width],
-        small[10, :width],
+        bias_grad[0, :width],
         joined_grad[:, width : 2 * width],
         joined_grad[:, 2 * width :],
-        small[10, width : 2 * width],
+        bias_grad[0, 2 * width :],
         out_grad.T,
         small[0],
         small[1],

time: 296 us -> 213 us (0.72)
  Pallas kernels: 257 us -> 190 us
  local copies, waits for them, and re-layouts: 30.2 us -> 15.8 us
    pallas_call x3 -> x1, Pallas kernels: 148 us -> 81.1 us  [backward(): pl.pallas_call(functools.partial(backward_kernel, shards), out_shape=(res...]
    transpose x5 -> x0, local copies, waits for them, and re-layouts: 3.8 us -> none  [the longest x1 1.28 us: body(): context = context.transpose(0, 2, 1).reshape(group_rows, width)]
    pallas_call x2 -> x0, local copies, waits for them, and re-layouts: 3.76 us -> none  [forward(): pl.pallas_call(functools.partial(forward_kernel, shards), out_shape=(shap...]
    unnamed x35 -> x21, local copies, waits for them, and re-layouts: 8.22 us -> 7.32 us
where the time goes in v3:
time: 213 us; the launch traced here: 212 us
  Pallas kernels  190 us (89%)
  local copies, waits for them, and re-layouts  15.8 us (7%)
  other arithmetic  4.84 us (2%)
    pallas_call x1, Pallas kernels, backward(): pl.pallas_call(functools.partial(backward_kernel, shards), out_shape=(res...  81.1 us
    pallas_call x1, Pallas kernels, forward(): pl.pallas_call(functools.partial(forward_kernel, shards), out_shape=(shap...  75.7 us
    pallas_call x1, Pallas kernels, middle(): pl.pallas_call(middle_kernel, out_shape=(jax.ShapeDtypeStruct((rows, mode...  33.6 us
    unnamed x21, local copies, waits for them, and re-layouts  7.32 us

profile of v3, /device:TPU:0, one launch (start us, length us, event | category | flops | bytes accessed | tf_op | source)
XLA Modules:
  0.0 212.0 jit_solution(1441935600683866007)
XLA Ops:
  0.7 0.0 copy-start.2
  0.7 0.0 copy-start.3
  0.7 0.0 copy-start.4
  0.7 0.0 copy-start.5
  0.7 0.0 copy-start.6
  0.7 0.0 copy-start.7
  0.7 1.3 convert_element_type.4
  2.0 1.6 pad_maximum_fusion.joined_ref
  3.6 0.7 broadcast_in_dim.22
  4.3 0.8 copy.38.query_bias_ref
  5.1 0.7 broadcast_in_dim.23
  5.7 0.8 copy.39.value_bias_ref
  6.5 1.5 copy.37
  8.0 1.3 reshape.62.bias_ref
  9.3 75.7 %forward.1 = (bf16[4,512,768]{2,1,0:T(8,128)(2,1)}, bf16[576,768]{1,0:T(8,128)(2,1)}, bf16[4,8,96,768]{3,2,1,0:T(8,128)(2,1)}, bf16[4,8,96,768]{3,2,1,0:T(8,128)...) custom-call(bf16[512,768]{1,0:T(8,128)(2,1)} %x_ref.3, ...), custom_call_target="tpu_custom_call" | custom-call | tf_op jit(solution)/shard_map/forward/pallas_call | solution.py:459
  85.0 0.0 copy-done.2
  85.0 0.0 copy-done.3
  85.1 0.0 copy-done.4
  85.1 0.0 copy-done.5
  85.1 0.0 copy-done.6
  85.1 0.0 copy-done.7
  85.2 0.6 convert_element_type.10.vectors_ref
  85.8 33.6 %middle.1 = (bf16[512,768]{1,0:T(8,128)(2,1)}, f32[512,768]{1,0:T(8,128)}, bf16[4,192,512]{2,1,0:T(8,128)(2,1)}, bf16[4,768,192]{2,1,0:T(8,128)(2,1)}, bf16[4,76...) custom-call(bf16[4,192,512]{2,1,0:T(8,128)(2,1)} %get-tuple-element.44.context_ref, ...), custom_call_target="tpu_custom_call" | custom-call | tf_op jit(solution)/shard_map/middle/pallas_call | solution.py:1125
  119.5 81.1 %backward.1 = (f32[512,768]{1,0:T(8,128)}, f32[96,576]{1,0:T(8,128)}, f32[96,768]{1,0:T(8,128)}, f32[96,768]{1,0:T(8,128)}, f32[96,192]{1,0:T(8,128)}, /*index=5*/f32[16,768]{1,0:T(8,128)}, f32[8,576]{1,0:T(8,128)}) custom-call(bf16[4,192,512]{2,1,0:T(8,128)(2,1)} %get-tuple-element.50.context_grad_ref, f32[512,768]{1,0:T(8,128)} %get-tuple-element.51.base_ref, ...), custom_call_target="tpu_custom_call" | custom-call | tf_op jit(solution)/shard_map/backward/pallas_call | solution.py:912
  200.5 0.8 slice.44
  201.3 1.8 slice_reduce_fusion
  203.1 1.8 fusion
  204.9 1.6 copy.40
  206.5 1.3 fusion.1
  207.8 0.0 copy-start.1
  207.8 0.0 copy-start
  207.8 2.7 %copy.44 = f32[512,768]{1,0:T(8,128)} copy(f32[512,768]{1,0:T(8,128)} %get-tuple-element.135) | data formatting | bytes 3145728
  210.5 0.0 copy-done.1
  210.5 0.7 copy.45
  211.2 0.0 copy-done
  211.2 0.7 copy.46
  (8 shorter events, 0.1 us)
Async XLA Ops:
  0.7 84.4 %copy-start.2 = (bf16[768]{0:T(1024)(128)(2,1)S(1)}, bf16[768]{0:T(1024)(128)(2,1)}, u32[]{:S(2)}) copy-start(bf16[768]{0:T(1024)(128)(2,1)} %param.26) | copy-start | bytes 4612
  0.7 84.4 %copy-start.3 = (bf16[768]{0:T(1024)(128)(2,1)S(1)}, bf16[768]{0:T(1024)(128)(2,1)}, u32[]{:S(2)}) copy-start(bf16[768]{0:T(1024)(128)(2,1)} %param.27) | copy-start | bytes 4612
  0.7 84.4 %copy-start.4 = (bf16[768]{0:T(1024)(128)(2,1)S(1)}, bf16[768]{0:T(1024)(128)(2,1)}, u32[]{:S(2)}) copy-start(bf16[768]{0:T(1024)(128)(2,1)} %param.28) | copy-start | bytes 4612
  0.7 84.4 %copy-start.5 = (bf16[768]{0:T(1024)(128)(2,1)S(1)}, bf16[768]{0:T(1024)(128)(2,1)}, u32[]{:S(2)}) copy-start(bf16[768]{0:T(1024)(128)(2,1)} %param.32) | copy-start | bytes 4612
  0.7 84.4 %copy-start.6 = (bf16[768]{0:T(1024)(128)(2,1)S(1)}, bf16[768]{0:T(1024)(128)(2,1)}, u32[]{:S(2)}) copy-start(bf16[768]{0:T(1024)(128)(2,1)} %param.33) | copy-start | bytes 4612
  0.7 84.4 %copy-start.7 = (bf16[768]{0:T(1024)(128)(2,1)S(1)}, bf16[768]{0:T(1024)(128)(2,1)}, u32[]{:S(2)}) copy-start(bf16[768]{0:T(1024)(128)(2,1)} %param.34) | copy-start | bytes 4612
  207.8 2.7 %copy-start.1 = (f32[96,768]{1,0:T(8,128)S(1)}, f32[96,768]{1,0:T(8,128)}, u32[]{:S(2)}) copy-start(f32[96,768]{1,0:T(8,128)} %get-tuple-element.145) | copy-start | bytes 884740
  207.8 3.4 %copy-start = (f32[96,768]{1,0:T(8,128)S(1)}, f32[96,768]{1,0:T(8,128)}, u32[]{:S(2)}) copy-start(f32[96,768]{1,0:T(8,128)} %get-tuple-element.70) | copy-start | bytes 884740

commit v4 on v3

--- a/solution.py
+++ b/solution.py
@@ -118,6 +118,12 @@
         copy.start()
         self.sent.append(copy)
 
+    def noted(self, number, source):
+        pass
+
+    def spent(self, time, what):
+        pass
+
     def arrive(self, number, target, partner):
         self.copy(number, target, target, partner).wait_recv()
 
@@ -132,6 +138,64 @@
             copy.wait_send()
         for copy in self.copies:
             copy.wait()
+
+
+class Agenda:
+    def __init__(self, plan):
+        self.plan, self.events = list(plan), {}
+
+    def add(self, name, needs, run):
+        self.events[name] = (needs, run)
+
+    def run(self, name):
+        self.events.pop(name)[1]()
+
+    def point(self):
+        for name in self.plan.pop(0) if self.plan else ():
+            self.run(name)
+
+    def rest(self):
+        while self.plan:
+            self.point()
+        while self.events:
+            for name, (needs, _) in list(self.events.items()):
+                if needs() is not None:
+                    self.run(name)
+
+
+def sent_numbers(stream, step):
+    found = [stream.numbers.get((step, way)) for way in stream.ways(step)]
+    return None if None in found else found
+
+
+FORWARD_PLAN = (
+    (),
+    (("h", 1),),
+    (("o", 0), ("d", 0),),
+    (("h", 2),),
+    (("o", 1), ("e", 0), ("b", 0), ("p", 0), ("d", 1),),
+    (),
+    (),
+    (("f", 0, 0), ("h", 3), ("o", 2),),
+    (("f", 1, 1),),
+    (("e", 1), ("p", 1), ("f", 1, -1),),
+    (("d", 2), ("f", 2, 1),),
+    (("h", 4), ("o", 3),),
+    (("f", 2, -1), ("e", 2),),
+    (("p", 2), ("f", 3, 1),),
+    (("d", 3), ("f", 3, -1), ("o", 4),),
+    (("e", 3),),
+    (("p", 3), ("f", 4, 1), ("d", 4),),
+    (("f", 4, -1), ("e", 4), ("p", 4),),
+)
+BACKWARD_PLAN = (
+    (("s", 0), ("o", 0), ("d", 1, 0), ("d", 1, 1),),
+    (("h", 0), ("o", 1, 0), ("o", 1, 1), ("s", 1), ("d", 2, 0), ("d", 2, 1),),
+    (("h", 1), ("s", 2), ("o", 2, 0), ("o", 2, 1),),
+    (("d", 3, 0), ("s", 3),),
+    (("d", 3, 1), ("h", 2), ("s", 4), ("o", 3, 0), ("o", 3, 1),),
+    (("d", 4, 0), ("d", 4, 1), ("h", 3), ("o", 4, 0), ("o", 4, 1), ("q", 0), ("r", 0), ("j", 1), ("q", 1), ("h", 4), ("q", 2), ("j", 2), ("j", 3), ("j", 4),),
+)
 
 
 class RingGather:
@@ -150,10 +214,12 @@
     def ways(self, step):
         return (1, -1) if step < self.half or self.split else (1,)
 
-    def send(self, step):
+    def send(self, step, sources=None):
         for way in self.ways(step):
             j = self.links.at(-way * (step - 1))
             source = self.own if step == 1 else self.slot(j)
+            if sources is not None:
+                source = sources[way]
             number = self.links.number()
             self.numbers[step, way] = number
             partner = {"dp": self.links.right if way > 0 else self.links.left}
@@ -184,8 +250,10 @@
     return jnp.maximum(i - REACH, 0), jnp.minimum(i + REACH + 1, blocks)
 
 
-def turned_segments(segment_ref, key_segments):
+def turned_segments(segment_ids_ref, segment_ref, key_segments):
     for j in range(PARTS):
+        line = segment_ids_ref[j * BLOCK : (j + 1) * BLOCK].astype(F32)
+        segment_ref[j] = line.reshape(1, BLOCK)
         row = jnp.broadcast_to(segment_ref[j], (128, BLOCK))
         key_segments[j] = jnp.transpose(row)
 
@@ -198,14 +266,16 @@
 def forward_kernel(
     shards,
     x_ref,
-    joined_ref,
+    query_weight_ref,
+    key_weight_ref,
+    value_weight_ref,
     hidden_ref,
     down_ref,
-    out_ref,
-    bias_ref,
+    out_weight_ref,
+    hidden_bias_ref,
     query_bias_ref,
     value_bias_ref,
-    segment_ref,
+    segment_ids_ref,
     all_x,
     all_joined,
     all_hidden,
@@ -219,7 +289,12 @@
     context_out,
     total_out,
     row_context,
+    out_ref,
+    bias_ref,
+    bias_columns,
+    segment_ref,
     x_here,
+    joined_ref,
     joined_here,
     joined_turned,
     query_turned,
@@ -238,10 +313,14 @@
     me, part = links.dp, links.part
     across, beside = {"tensor": links.other_row}, {"tensor": links.other_core}
     far = links.other_row
+    rows, width = query_weight_ref.shape
+    joined_ref[:, :width] = query_weight_ref[...]
+    joined_ref[:, width : 2 * width] = key_weight_ref[...]
+    joined_ref[:, 2 * width :] = value_weight_ref[...]
+    out_ref[...] = jnp.transpose(out_weight_ref[...].astype(F32)).astype(BF16)
+    bias_ref[...] = hidden_bias_ref[...].astype(F32).reshape(bias_ref.shape)
     links.barrier(diagonal=True)
-    rows = hidden_ref.shape[0]
     half = shards // 2
-    width = query_bias_ref.shape[0]
     heads = width // HEAD
     scale = HEAD ** (-0.5)
     later = []
@@ -257,12 +336,17 @@
         links.arrive(*entry, beside)
         later.remove(entry)
 
+    def ring(array, owner, own):
+        stream = RingGather(links, rows, own, lambda j: array.at[owner, j])
+        stream.array, stream.owner = array, owner
+        return stream
+
     joined = RingGather(links, rows, joined_ref, lambda j: joined_here.at[j])
-    hidden = RingGather(links, rows, hidden_ref, lambda j: all_hidden.at[part, j])
-    down_own = RingGather(links, rows, down_ref, lambda j: all_down.at[part, j])
-    out_own = RingGather(links, rows, out_ref, lambda j: all_out.at[part, j])
-    down_far = RingGather(links, rows, all_down.at[far, me], lambda j: all_down.at[far, j])
-    out_far = RingGather(links, rows, all_out.at[far, me], lambda j: all_out.at[far, j])
+    hidden = ring(all_hidden, part, hidden_ref)
+    down_own = ring(all_down, part, down_ref)
+    out_own = ring(all_out, part, out_ref)
+    down_far = ring(all_down, far, all_down.at[far, me])
+    out_far = ring(all_out, far, all_out.at[far, me])
     joined.send(1)
     cut = x_ref.shape[0] // 2
     x_numbers = [links.number() for _ in range(2)]
@@ -270,25 +354,11 @@
     for number, piece in zip(x_numbers, pieces):
         links.start(number, x_ref.at[piece], x_here.at[part, piece], across)
     x_beside = share(lambda t: x_here.at[t], part, x_ref)
+    hidden.send(1)
     bias_number, down_number, out_number = (links.number() for _ in range(3))
+    links.start(down_number, down_ref, all_down.at[part, me], across)
     links.start(bias_number, bias_ref, all_bias.at[part], across)
-    links.start(down_number, down_ref, all_down.at[part, me], across)
     links.start(out_number, out_ref, all_out.at[part, me], across)
-    hidden.send(1)
-    hidden_numbers = {}
-
-    def hidden_across(j, key, piece):
-        number = links.number()
-        target = piece(all_hidden.at[part, j])
-        links.start(number, hidden_ref if key == 0 else target, target, across)
-        hidden_numbers[key] = (number, j, piece)
-
-    def far_hidden(key):
-        number, j, piece = hidden_numbers[key]
-        links.arrive(number, piece(all_hidden.at[far, j]), across)
-        share(lambda t: piece(all_hidden.at[t, j]), far)
-
-    hidden_across(me, 0, lambda ref: ref)
     share(lambda t: all_hidden.at[t, me], part, hidden_ref)
     share(lambda t: all_down.at[t, me], part, down_ref)
     share(lambda t: all_out.at[t, me], part, out_ref)
@@ -298,58 +368,86 @@
     links.keep(down_ref, all_down.at[part, me])
     links.keep(out_ref, all_out.at[part, me])
     links.keep(bias_ref, all_bias.at[part])
+    hidden_numbers = {}
+
+    def hidden_across(j, key, piece):
+        number = links.number()
+        target = piece(all_hidden.at[part, j])
+        links.start(number, hidden_ref if key == 0 else target, target, across)
+        hidden_numbers[key] = (number, j, piece)
+
+    def far_hidden(key):
+        number, j, piece = hidden_numbers[key]
+        links.arrive(number, piece(all_hidden.at[far, j]), across)
+        share(lambda t: piece(all_hidden.at[t, j]), far)
+
+    hidden_across(me, 0, lambda ref: ref)
 
     def take(stream, step):
         arrived = stream.arrive(step)
         if step < half:
             stream.send(step + 1)
+        if stream is joined:
+            return
         for j, way in arrived:
-            piece = lambda ref, way=way: stream.part(ref, step, way)
             if stream is hidden:
-                hidden_across(j, (step, way), piece)
-                share(lambda t, j=j, piece=piece: piece(all_hidden.at[t, j]), part)
-            elif stream is not joined:
-                ref = all_down if stream in (down_own, down_far) else all_out
-                owner = part if stream in (down_own, out_own) else far
-                share(lambda t, j=j, piece=piece, ref=ref: piece(ref.at[t, j]), owner)
-
-    def from_far():
-        links.arrive(down_number, all_down.at[far, me], across)
-        down_far.send(1)
-        share(lambda t: all_down.at[t, me], far)
-        links.arrive(out_number, all_out.at[far, me], across)
-        out_far.send(1)
-        share(lambda t: all_out.at[t, me], far)
+                hidden_across(j, (step, way), lambda ref, way=way: stream.part(ref, step, way))
+            piece = lambda t, j=j, way=way: stream.part(stream.array.at[t, j], step, way)
+            share(piece, stream.owner)
+
+    def from_far(stream, array, number):
+        links.arrive(number, array.at[far, me], across)
+        stream.send(1)
+        share(lambda t: array.at[t, me], far)
+
+    def bias_far():
         links.arrive(bias_number, all_bias.at[far], across)
         share(lambda t: all_bias.at[t], far)
-        far_hidden(0)
-
-    def both(first, second, step):
-        take(first, step)
-        take(second, step)
-
-    def far_step(step):
+
+    agenda = Agenda(FORWARD_PLAN if shards == 8 else ())
+
+    def add_ring(name, stream):
+        for step in range(1, half + 1):
+            needs = lambda step=step: sent_numbers(stream, step)
+            agenda.add((name, step), needs, lambda step=step: take(stream, step))
+
+    def add_far_hidden(key):
+        needs = lambda: [hidden_numbers[key][0]] if key in hidden_numbers else None
+        agenda.add(("f",) + (key if key else (0, 0)), needs, lambda: far_hidden(key))
+
+    add_ring("h", hidden)
+    started = lambda: [] if (half, 1) in joined.numbers else None
+    agenda.add(("o", 0), started, lambda: out_own.send(1))
+    agenda.add(("d", 0), started, lambda: down_own.send(1))
+    add_ring("o", out_own)
+    add_ring("d", down_own)
+    agenda.add(("e", 0), lambda: [down_number], lambda: from_far(down_far, all_down, down_number))
+    agenda.add(("b", 0), lambda: [bias_number], bias_far)
+    agenda.add(("p", 0), lambda: [out_number], lambda: from_far(out_far, all_out, out_number))
+    add_far_hidden(0)
+    for step in range(1, half + 1):
         for way in hidden.ways(step):
-            far_hidden((step, way))
-
-    turned_segments(segment_ref, key_segments)
+            add_far_hidden((step, way))
+    add_ring("e", down_far)
+    add_ring("p", out_far)
+
+    for n, ref in enumerate((query_bias_ref, value_bias_ref)):
+        line = ref[...].astype(F32).reshape(1, width)
+        bias_columns[n] = jnp.transpose(jnp.broadcast_to(line, (128, width)))
+    turned_segments(segment_ids_ref, segment_ref, key_segments)
     joined_here[me] = joined_ref[...]
-    take(joined, 1)
-    down_own.send(1)
-    out_own.send(1)
-    for step in range(2, half + 1):
+    for step in range(1, half + 1):
         take(joined, step)
-        if step == 2:
-            take(hidden, 1)
+        agenda.point()
     model = x_ref.shape[1]
     joined_turned[...] = jnp.transpose(joined_here[...].reshape(model, 3 * width))
 
     def project(s, x):
         three = dot_t(joined_turned[...], x[...])
-        queries = (three[:width] + query_bias_ref[...]).astype(BF16)
+        queries = (three[:width] + bias_columns[0, :, :1]).astype(BF16)
         query_turned[s] = (queries.astype(F32) * scale).astype(BF16)
         keys = three[width : 2 * width]
-        values = three[2 * width :] + value_bias_ref[...]
+        values = three[2 * width :] + bias_columns[1, :, :1]
         key_turned[s] = keys.astype(BF16)
         value_turned[s] = values.astype(BF16)
         for h in range(heads):
@@ -357,17 +455,22 @@
             key_here[s, h] = jnp.transpose(keys[span]).astype(BF16)
             value_here[s, h] = jnp.transpose(values[span]).astype(BF16)
 
+    project(part, x_ref)
+    agenda.point()
+    settle(x_beside)
+    project(links.other_core, x_here.at[links.other_core])
+    agenda.point()
     x_far = []
     for number, piece in zip(x_numbers, pieces):
         links.arrive(number, x_here.at[far, piece], across)
         x_far.append(share(lambda t, piece=piece: x_here.at[t, piece], far))
-    project(part, x_ref)
-    settle(x_beside)
-    project(links.other_core, x_here.at[links.other_core])
+    agenda.point()
     project(far, x_here.at[far])
+    agenda.point()
     for entry in x_far:
         settle(entry)
     project(links.diagonal, x_here.at[links.diagonal])
+    agenda.point()
     for t in (links.other_core, far, links.diagonal):
         links.keep(x_here.at[t], all_x.at[t])
     for source, target in (
@@ -379,15 +482,6 @@
     ):
         links.keep(source, target)
 
-    queue = [lambda: from_far()]
-    for step in range(1, half + 1):
-        queue.append(lambda step=step: both(down_own, out_own, step))
-        if step < half:
-            queue.append(lambda step=step: take(hidden, step + 1))
-            queue.append(lambda step=step: far_step(step))
-        queue.append(lambda step=step: both(down_far, out_far, step))
-    queue.append(lambda: far_step(half))
-
     partners = (far, links.diagonal, links.other_core)
     context_numbers = [links.number() for _ in partners]
     places = partners + (part,)
@@ -409,6 +503,7 @@
         start = jnp.full((8, BLOCK), NEGATIVE, F32)
         tops = lax.fori_loop(low, high, scores, (start,) * heads)
         tops = [jnp.max(top, axis=0, keepdims=True) for top in tops]
+        agenda.point()
 
         def mix(j, state):
             found = []
@@ -434,12 +529,11 @@
                 row_context.at[part],
                 {"tensor": i},
             )
-        share_of = -(-len(queue) // PARTS)
-        for event in queue[n * share_of : (n + 1) * share_of]:
-            event()
+        agenda.point()
 
     links.keep(context_here, context_out)
     links.keep(context_here.at[part], row_context.at[part])
+    agenda.rest()
     for number, ref in later:
         links.arrive(number, ref, beside)
     for number, partner in zip(context_numbers, partners):
@@ -448,13 +542,27 @@
     assert links.used <= forward_copies(shards), links.used
 
 
-def forward(shards, x, joined, hidden, down, out, bias, query_bias, value_bias, segments):
+def forward(
+    shards,
+    x,
+    query_weight,
+    key_weight,
+    value_weight,
+    hidden,
+    down,
+    out,
+    bias,
+    query_bias,
+    value_bias,
+    segments,
+):
     shape = lambda *dims: jax.ShapeDtypeStruct(dims, BF16)
     count = forward_copies(shards)
     rows, model = x.shape
-    width = query_bias.shape[0]
+    width = query_weight.shape[1]
     heads = width // HEAD
     turned = (PARTS, width, rows)
+    out_shape = (out.shape[1], out.shape[0])
     headed = (PARTS, heads, rows, HEAD)
     return pl.pallas_call(
         functools.partial(forward_kernel, shards),
@@ -463,8 +571,8 @@
             shape(3 * width, model),
             shape(PARTS, shards, *hidden.shape),
             shape(PARTS, shards, *down.shape),
-            shape(PARTS, shards, *out.shape),
-            jax.ShapeDtypeStruct((PARTS, *bias.shape), F32),
+            shape(PARTS, shards, *out_shape),
+            jax.ShapeDtypeStruct((PARTS, 1, bias.shape[0]), F32),
             shape(*turned),
             shape(*headed),
             shape(*headed),
@@ -473,11 +581,16 @@
             jax.ShapeDtypeStruct((PARTS, 8, rows), F32),
             shape(*turned),
         ),
-        in_specs=[vmem()] * 9,
+        in_specs=[vmem()] * 11,
         out_specs=[anywhere()] * 11 + [vmem()] + [anywhere()],
         scratch_shapes=[
+            pltpu.VMEM(out_shape, BF16),
+            pltpu.VMEM((1, bias.shape[0]), F32),
+            pltpu.VMEM((2, width, 128), F32),
+            pltpu.VMEM((PARTS, 1, BLOCK), F32),
             pltpu.VMEM((PARTS, rows, model), BF16),
-            pltpu.VMEM((shards, *joined.shape), BF16),
+            pltpu.VMEM((hidden.shape[0], 3 * width), BF16),
+            pltpu.VMEM((shards, hidden.shape[0], 3 * width), BF16),
             pltpu.VMEM((3 * width, model), BF16),
             pltpu.VMEM(turned, BF16),
             pltpu.VMEM(turned, BF16),
@@ -495,7 +608,19 @@
             collective_id=0, has_side_effects=True, vmem_limit_bytes=VMEM_LIMIT
         ),
         name="forward",
-    )(x, joined, hidden, down, out, bias, query_bias, value_bias, segments)
+    )(
+        x,
+        query_weight,
+        key_weight,
+        value_weight,
+        hidden,
+        down,
+        out,
+        bias,
+        query_bias,
+        value_bias,
+        segments,
+    )
 
 
 def plus(left, right):
@@ -567,20 +692,19 @@
 def backward_kernel(
     shards,
     context_grad_ref,
-    base_ref,
     hidden_ref,
     down_ref,
     out_ref,
+    x_all,
+    joined_all,
     small_ref,
-    x_ref,
-    joined_ref,
     query_ref,
     key_turned_ref,
     key_ref,
     value_ref,
     context_ref,
     total_ref,
-    segment_ref,
+    segment_ids_ref,
     rows_out,
     joined_out,
     hidden_out,
@@ -588,6 +712,9 @@
     out_out,
     small_out,
     bias_out,
+    x_ref,
+    joined_ref,
+    segment_ref,
     upstream,
     key_segments,
     key_sum,
@@ -596,12 +723,12 @@
     weight_sum,
     joined_terms,
     rows_send,
+    rows_own,
+    rows_block,
     rows_two,
     rows_far,
     hidden_own,
-    hidden_two,
     hidden_far,
-    down_own,
     down_two,
     out_own,
     out_two,
@@ -628,7 +755,9 @@
     width = query_ref.shape[1]
     heads = width // HEAD
     scale = HEAD ** (-0.5)
-    places = (part, links.other_core, links.other_row, links.diagonal)
+    inner_far, outer_far = 2 - row, 3 * (1 - row)
+    places = (1 + row, inner_far, outer_far, 3 * row)
+    partners = (links.other_row, links.diagonal, links.other_core)
 
     numbers = {}
 
@@ -636,34 +765,39 @@
         numbers[name, y] = links.number()
         links.start(numbers[name, y], array.at[2 * y + 1 - core], slots.at[y], beside)
 
-    def own_half(array, own):
-        for y in range(2):
-            links.keep(array.at[2 * y + core], own.at[y])
-        return links.copies[-2:]
-
-    for n in range(1, 4):
+    for n, partner in enumerate(partners):
         numbers["upstream", n] = links.number()
         links.start(
             numbers["upstream", n],
-            context_grad_ref.at[places[n]],
+            context_grad_ref.at[partner],
             upstream.at[part],
-            {"tensor": places[n]},
+            {"tensor": partner},
+        )
+    order = [half] + [way * o for o in range(half - 1, 0, -1) for way in (1, -1)] + [0]
+    for o in order:
+        numbers["far", o % shards] = links.number()
+        j = links.at(o)
+        links.start(
+            numbers["far", o % shards], hidden_ref.at[1 - row, j], hidden_far.at[j], across
         )
     for y in range(2):
-        to_core("down", down_ref, down_two, y)
-    for y in range(2):
         to_core("out", out_ref, out_two, y)
-    numbers["hidden", 0] = links.number()
-    numbers["hidden", 1] = links.number()
-    links.start(
-        numbers["hidden", 0], hidden_ref.at[2 * (1 - row) + 1 - core], hidden_two.at[1 - row], beside
-    )
-    links.start(numbers["hidden", 1], hidden_ref.at[2 * row + 1 - core], hidden_two.at[row], beside)
-    copies = {
-        "down": own_half(down_ref, down_own),
-        "out": own_half(out_ref, out_own),
-        "hidden": own_half(hidden_ref, hidden_own),
-    }
+
+    def kept(source, target):
+        links.keep(source, target)
+        return links.copies[-1]
+
+    def settle(copy):
+        copy.wait()
+        links.copies = [other for other in links.copies if other is not copy]
+
+    down_copies = [kept(down_ref.at[y], down_two.at[y]) for y in range(2)]
+    out_copies = [kept(out_ref.at[2 * y + core], out_own.at[y]) for y in range(2)]
+    hidden_copy = kept(hidden_ref.at[row], hidden_own)
+    late_copies = [
+        kept(joined_all, joined_ref),
+        kept(x_all, x_ref),
+    ]
     upstream[part] = context_grad_ref[part]
 
     cube = [{"dp": index} for index in links.cube()]
@@ -691,46 +825,28 @@
                 self.send(self.sums.at[step])
 
     small = Pairwise(small_ref, small_slots, small_sums, small_out, cube + [beside, across])
-    small_left = [small.step] * len(small.partners)
-
-    def small_step():
-        if small_left:
-            small_left.pop()()
-
-    def add_core(name, own, slots, y, number):
-        if copies[name]:
-            for copy in copies.pop(name):
-                copy.wait()
-                links.copies.remove(copy)
-            copies[name] = None
-        links.arrive(number, slots.at[y], beside)
-
-        def one(i, carry):
-            slots[y, i] = plus(slots[y, i], own[y, i])
-            return carry
-
-        lax.fori_loop(0, shards, one, 0)
-
-    rings = []
-
-    def begin():
-        for name, own, slots, ring_slots in (
-            ("down", down_own, down_two, down_slots),
-            ("out", out_own, out_two, out_slots),
-        ):
-            for y in range(2):
-                add_core(name, own, slots, y, numbers[name, y])
-                term = lambda o, y=y, slots=slots: slots.at[y, links.at(o)]
-                rings.append(RingSum(links, rows, term, ring_slots.at[y]))
-                rings[-1].send(1)
-        add_core("hidden", hidden_own, hidden_two, 1 - row, numbers["hidden", 0])
-        order = [half] + [way * o for o in range(half - 1, 0, -1) for way in (1, -1)] + [0]
-        for o in order:
-            numbers["far", o % shards] = links.number()
-            j = links.at(o)
-            links.start(
-                numbers["far", o % shards], hidden_two.at[1 - row, j], hidden_far.at[j], across
-            )
+    down_rings, out_rings = [], []
+
+    def begin_down():
+        for y in range(2):
+            settle(down_copies[y])
+            term = lambda o, y=y: down_two.at[y, links.at(o)]
+            down_rings.append(RingSum(links, rows, term, down_slots.at[y]))
+            down_rings[-1].send(1)
+
+    def begin_out():
+        for y in range(2):
+            settle(out_copies[y])
+            links.arrive(numbers["out", y], out_two.at[y], beside)
+
+            def one(i, carry):
+                out_two[y, i] = plus(out_two[y, i], out_own[y, i])
+                return carry
+
+            lax.fori_loop(0, shards, one, 0)
+            term = lambda o, y=y: out_two.at[y, links.at(o)]
+            out_rings.append(RingSum(links, rows, term, out_slots.at[y]))
+            out_rings[-1].send(1)
 
     ready = set()
 
@@ -739,33 +855,124 @@
         if o % shards not in ready:
             ready.add(o % shards)
             links.arrive(numbers["far", o % shards], hidden_far.at[j], across)
-            hidden_far[j] = plus(hidden_far[j], hidden_two[row, j])
+            hidden_far[j] = plus(hidden_far[j], hidden_own[j])
         return hidden_far.at[j]
 
     hidden = RingSum(links, rows, hidden_term, hidden_slots)
-
-    def ring_step(step):
-        for ring in rings:
-            ring.arrive(step)
-            if step < half:
-                ring.send(step + 1)
 
     def hidden_step(step):
         if step == 0:
-            add_core("hidden", hidden_own, hidden_two, row, numbers["hidden", 1])
+            settle(hidden_copy)
         else:
             hidden.arrive(step)
         if step < half:
             hidden.send(step + 1)
 
-    turned_segments(segment_ref, key_segments)
+    pairs = []
+
+    def pair_up(rings, pair, result):
+        for y in range(2):
+            pair[y] = rings[y].total().astype(BF16)
+        number = links.number()
+        links.start(number, pair.at[1 - row], pair.at[2], across)
+        pairs.append((number, pair, result))
+
+    agenda = Agenda(BACKWARD_PLAN if shards == 8 else ())
+    begin_down()
+    paired = {"d": 0, "o": 0}
+
+    def ring_event(name, rings, y, step, pair, result):
+        ring = rings[y]
+        ring.arrive(step)
+        if step < half:
+            ring.send(step + 1)
+        else:
+            paired[name] += 1
+            if paired[name] == 2:
+                pair_up(rings, pair, result)
+
+    def add_rings(name, rings, pair, result):
+        for step in range(1, half + 1):
+            for y in range(2):
+                agenda.add(
+                    (name, step, y),
+                    lambda step=step, y=y: sent_numbers(rings[y], step) if rings else None,
+                    lambda step=step, y=y: ring_event(name, rings, y, step, pair, result),
+                )
+
+    def hidden_needs(step):
+        offsets = [half - step, step - half]
+        found = [numbers["far", o % shards] for o in offsets if o % shards not in ready]
+        if step == 0:
+            return found
+        waits = sent_numbers(hidden, step)
+        return None if waits is None else found + waits
+
+    add_rings("d", down_rings, down_pair, down_out)
+    agenda.add(("o", 0), lambda: [numbers["out", y] for y in range(2)], begin_out)
+    add_rings("o", out_rings, out_pair, out_out)
+    for step in range(half):
+        agenda.add(
+            ("h", step),
+            lambda step=step: hidden_needs(step),
+            lambda step=step: hidden_step(step),
+        )
+    for step in range(len(small.partners)):
+        agenda.add(
+            ("s", step),
+            lambda step=step: [small.numbers[step]] if len(small.numbers) == step + 1 else None,
+            small.step,
+        )
+
+    turned_segments(segment_ids_ref, segment_ref, key_segments)
     key_sum[...] = jnp.zeros_like(key_sum)
     value_sum[...] = jnp.zeros_like(value_sum)
 
+    def project_keys(s):
+        projected[s, width : 2 * width, :] = key_sum[s].astype(BF16)
+        projected[s, 2 * width :, :] = value_sum[s].astype(BF16)
+
+    def x_grad(s):
+        return dot(jnp.transpose(projected[s]), joined_ref[...])
+
+    far_numbers = [links.number() for _ in range(2)]
+
+    def far_rows(k, s):
+        block = x_grad(s).astype(BF16)
+        rows_block[k] = block.reshape(rows_block.shape[1:])
+        numbers["half", k] = links.number()
+        links.start(numbers["half", k], rows_block.at[k, 1 - core], rows_two.at[k], beside)
+
+    def far_sum(k, s):
+        links.arrive(numbers["half", k], rows_two.at[k], beside)
+        rows_two[k] = plus(rows_two[k], rows_block[k, core])
+        copy = pltpu.make_async_remote_copy(
+            src_ref=rows_two.at[k],
+            dst_ref=rows_far.at[core],
+            send_sem=send.at[far_numbers[k]],
+            recv_sem=recv.at[far_numbers[0] + core],
+            device_id={"tensor": s},
+            device_id_type=MESH,
+        )
+        copy.start()
+        links.sent.append(copy)
+        links.noted(far_numbers[k], rows_two.at[k])
+
     for n in range(PARTS):
         i = places[n]
-        if n > 0:
-            links.arrive(numbers["upstream", n], upstream.at[i], {"tensor": i})
+        if n == 0:
+            links.arrive(numbers["upstream", 2], upstream.at[links.other_core], beside)
+        elif n == 1:
+            for m in range(2):
+                partner = partners[m]
+                links.arrive(numbers["upstream", m], upstream.at[partner], {"tensor": partner})
+        elif n == 3:
+            for copy in late_copies:
+                settle(copy)
+            project_keys(outer_far)
+            far_rows(0, outer_far)
+            agenda.point()
+            far_sum(0, outer_far)
         low, high = near(i, PARTS)
         spans = [slice(h * HEAD, (h + 1) * HEAD) for h in range(heads)]
         inner = [
@@ -797,40 +1004,10 @@
         sums = lax.fori_loop(low, high, block, (empty,) * heads)
         for h in range(heads):
             projected[i, spans[h], :] = (sums[h] * scale).astype(BF16)
-        if n == 0:
-            begin()
-        else:
-            ring_step(n)
-            hidden_step(n - 1)
-        small_step()
-
-    for s in range(PARTS):
-        projected[s, width : 2 * width, :] = key_sum[s].astype(BF16)
-        projected[s, 2 * width :, :] = value_sum[s].astype(BF16)
-
-    def x_grad(s):
-        return dot(jnp.transpose(projected[s]), joined_ref[...]).astype(BF16)
-
-    def x_across(s_beside, s_own, y, name):
-        rows_send[y] = x_grad(s_beside)
-        numbers[name] = links.number()
-        links.start(numbers[name], rows_send.at[y], rows_two.at[y], beside)
-        return x_grad(s_own)
-
-    mine = x_across(links.diagonal, links.other_row, 1 - row, "rows far")
-    rows_send_far = rows_send.at[2]
-    rows_send_far[...] = mine
-    ones = jnp.ones((8, BLOCK), BF16)
-    bias = dot_t(ones, projected[0])
-    for s in range(1, PARTS):
-        bias = bias + dot_t(ones, projected[s])
-    bias_sums[bias_sums.shape[0] - 1] = bias
-    sums_of = Pairwise(bias_sums.at[bias_sums.shape[0] - 1], bias_slots, bias_sums, bias_out, cube)
-    links.arrive(numbers["rows far"], rows_two.at[1 - row], beside)
-    rows_two[1 - row] = plus(rows_two[1 - row], rows_send_far[...])
-    rows_number = links.number()
-    links.start(rows_number, rows_two.at[1 - row], rows_far, across)
-
+        agenda.point()
+
+    for k in range(3):
+        project_keys((inner_far, 1 + row, 3 * row)[k])
     weight = dot(projected[0], x_ref[0])
     for s in range(1, PARTS):
         weight = weight + dot(projected[s], x_ref[s])
@@ -839,42 +1016,52 @@
     joined_terms[...] = turned.reshape(joined_terms.shape)
     joined = RingSum(links, rows, lambda o: joined_terms.at[links.at(o)], joined_slots)
     joined.send(1)
-
-    mine = x_across(links.other_core, part, row, "rows own")
-    rows_out[...] = base_ref[...] + mine.astype(F32)
-    sums_of.step()
-    small_step()
-    for step in range(PARTS, half + 1):
-        ring_step(step)
-        hidden_step(step - 1)
-        small_step()
-    pairs = []
-    for pair_rings, pair, result in (
-        (rings[:2], down_pair, down_out),
-        (rings[2:], out_pair, out_out),
-    ):
-        for y in range(2):
-            pair[y] = pair_rings[y].total().astype(BF16)
-        number = links.number()
-        links.start(number, pair.at[1 - row], pair.at[2], across)
-        pairs.append((number, pair, result))
-    joined.arrive(1)
-    joined.send(2)
-    links.arrive(numbers["rows own"], rows_two.at[row], beside)
-    rows_out[...] += rows_two[row].astype(F32)
-    for _ in range(len(cube) - 1):
-        sums_of.step()
-    while small_left:
-        small_step()
-    for step in range(2, half):
+    far_rows(1, inner_far)
+    rows_send[...] = x_grad(links.other_core).astype(BF16)
+    far_sum(1, inner_far)
+    rows_number = links.number()
+    links.start(rows_number, rows_send, rows_own, beside)
+    ones = jnp.ones((8, BLOCK), BF16)
+    bias = dot_t(ones, projected[0])
+    for s in range(1, PARTS):
+        bias = bias + dot_t(ones, projected[s])
+    bias_sums[bias_sums.shape[0] - 1] = bias
+    sums_of = Pairwise(bias_sums.at[bias_sums.shape[0] - 1], bias_slots, bias_sums, bias_out, cube)
+    rows_out[...] = x_grad(part)
+
+    def joined_step(step):
         joined.arrive(step)
-        joined.send(step + 1)
-    hidden.arrive(half)
-    hidden_out[...] = hidden.total()
-    joined.arrive(half)
-    joined_out[...] = joined.total()
-    links.arrive(rows_number, rows_far, across)
-    rows_out[...] += rows_far[...].astype(F32)
+        if step < half:
+            joined.send(step + 1)
+        else:
+            joined_out[...] = joined.total()
+
+    def hidden_last():
+        hidden.arrive(half)
+        hidden_out[...] = hidden.total()
+
+    def add_rows():
+        links.arrive(rows_number, rows_own, beside)
+        rows_out[...] += rows_own[...].astype(F32)
+
+    for step in range(1, half + 1):
+        agenda.add(
+            ("j", step),
+            lambda step=step: sent_numbers(joined, step),
+            lambda step=step: joined_step(step),
+        )
+    agenda.add(("h", half), lambda: sent_numbers(hidden, half), hidden_last)
+    agenda.add(("r", 0), lambda: [rows_number], add_rows)
+    for step in range(len(cube)):
+        agenda.add(
+            ("q", step),
+            lambda step=step: [sums_of.numbers[step]] if len(sums_of.numbers) == step + 1 else None,
+            sums_of.step,
+        )
+    agenda.rest()
+    for h in range(2):
+        links.arrive(far_numbers[h], rows_far.at[h], across)
+    rows_out[...] += rows_far[...].astype(F32).reshape(rows_out.shape)
     for number, pair, result in pairs:
         links.arrive(number, pair.at[2], across)
         result[...] = pair[row].astype(F32) + pair[2].astype(F32)
@@ -885,7 +1072,6 @@
 def backward(
     shards,
     context_grad,
-    base,
     hidden,
     down,
     out,
@@ -903,7 +1089,7 @@
     half = shards // 2
     count = backward_copies(shards)
     stages = (shards - 1).bit_length() + 2
-    rows, model = base.shape
+    rows, model = x.shape[1:]
     width = queries.shape[1]
     low = lambda *dims: pltpu.VMEM(dims, BF16)
     wide = lambda *dims: pltpu.VMEM(dims, F32)
@@ -920,9 +1106,12 @@
             result(*small.shape),
             result(8, 3 * width),
         ),
-        in_specs=[vmem()] * 2 + [anywhere()] * 3 + [vmem()] * 10,
+        in_specs=[vmem()] + [anywhere()] * 5 + [vmem()] * 8,
         out_specs=[vmem()] * 7,
         scratch_shapes=[
+            low(*x.shape),
+            low(*joined.shape),
+            wide(PARTS, 1, BLOCK),
             low(*context_grad.shape),
             wide(PARTS, BLOCK, 128),
             wide(PARTS, width, rows),
@@ -930,13 +1119,13 @@
             low(PARTS, 3 * width, rows),
             wide(3 * width, model),
             low(shards, *shard),
-            low(3, rows, model),
-            low(2, rows, model),
             low(rows, model),
-            low(2, *hidden.shape[1:]),
-            low(2, *hidden.shape[1:]),
+            low(rows, model),
+            low(2, 2, rows // 2, model),
+            low(2, rows // 2, model),
+            low(2, rows // 2, model),
             low(*hidden.shape[1:]),
-            low(2, *down.shape[1:]),
+            low(*hidden.shape[1:]),
             low(2, *down.shape[1:]),
             low(2, *out.shape[1:]),
             low(2, *out.shape[1:]),
@@ -952,7 +1141,7 @@
             wide(stages, 8, 3 * width),
             pltpu.SemaphoreType.DMA((count,)),
             pltpu.SemaphoreType.DMA((count,)),
-            pltpu.SemaphoreType.DMA((6,)),
+            pltpu.SemaphoreType.DMA((8,)),
         ],
         compiler_params=pltpu.CompilerParams(
             collective_id=3, has_side_effects=True, vmem_limit_bytes=VMEM_LIMIT
@@ -960,13 +1149,12 @@
         name="backward",
     )(
         context_grad,
-        base,
         hidden,
         down,
         out,
-        small,
         x,
         joined,
+        small,
         queries,
         keys_turned,
         keys,
@@ -977,6 +1165,65 @@
     )
 
 
+def outputs_kernel(
+    base_ref,
+    rows_ref,
+    joined_ref,
+    hidden_ref,
+    down_ref,
+    out_ref,
+    small_ref,
+    bias_ref,
+    rows_out,
+    query_out,
+    key_out,
+    value_out,
+    hidden_out,
+    down_out,
+    out_out,
+    query_bias_out,
+    value_bias_out,
+    hidden_bias_out,
+    *vector_outs,
+):
+    rows_out[...] = base_ref[...] + rows_ref[...]
+    width = query_bias_out.shape[0]
+    for n, result in enumerate((query_out, key_out, value_out)):
+        result[...] = joined_ref[:, n * width : (n + 1) * width]
+    hidden_out[...] = hidden_ref[...]
+    down_out[...] = down_ref[...]
+    out_out[...] = jnp.transpose(out_ref[...])
+    query_bias_out[...] = bias_ref[0, :width]
+    value_bias_out[...] = bias_ref[0, 2 * width :]
+    part = lax.axis_index("tensor")
+    hidden_bias_out[...] = small_ref[pl.ds(6 + part, 1), :].reshape(hidden_bias_out.shape)
+    for n, result in enumerate(vector_outs):
+        result[...] = small_ref[n, :]
+
+
+def outputs(base, rows, joined, hidden, down, out, small, bias):
+    shard, width = out.shape
+    model = rows.shape[1]
+    result = lambda *dims: jax.ShapeDtypeStruct(dims, F32)
+    return pl.pallas_call(
+        outputs_kernel,
+        out_shape=(
+            result(*rows.shape),
+            *[result(shard, width)] * 3,
+            result(*hidden.shape),
+            result(*down.shape),
+            result(width, shard),
+            result(width),
+            result(width),
+            *[result(model)] * 7,
+        ),
+        in_specs=[vmem()] * 8,
+        out_specs=[vmem()] * 16,
+        compiler_params=pltpu.CompilerParams(vmem_limit_bytes=VMEM_LIMIT),
+        name="outputs",
+    )(base, rows, joined, hidden, down, out, small, bias)
+
+
 ROW_BLOCK = 128
 ROOT_HALF = 0.7071067811865476
 PHI_ZERO = 0.3989422804014327
@@ -999,22 +1246,38 @@
     return inverse * (scaled - inner)
 
 
+def middle_copies(shards):
+    return 4
+
+
 def middle_kernel(
+    shards,
+    *refs,
+):
+    vector_refs, refs = refs[4:10], refs[:4] + refs[10:]
+    middle_steps(shards, vector_refs, *refs)
+
+
+def middle_steps(
+    shards,
+    vector_refs,
     context_ref,
     x_ref,
     cotangent_ref,
     out_ref,
+    hidden_bias_ref,
     hidden_ref,
     down_ref,
-    vectors_ref,
-    hidden_bias_ref,
-    layer_out,
     first_grad_out,
     context_grad_out,
     out_grad,
-    hidden_grad_out,
-    down_grad_out,
     small_out,
+    layer_out,
+    hidden_out,
+    down_out,
+    layer_here,
+    hidden_here,
+    down_here,
     first_norm,
     first_normed,
     first_scale,
@@ -1025,11 +1288,33 @@
     second_low,
     turned,
     back_low,
+    hidden_send,
+    hidden_two,
+    hidden_sum,
+    down_send,
+    down_two,
+    down_sum,
+    send,
+    recv,
+    local,
 ):
+    links = Links(shards, send, recv, local)
+    core = links.core
+    beside = {"tensor": links.other_core}
     rows, model = x_ref.shape
-    out_bias, first_gain, first_shift = (vectors_ref[i : i + 1, :] for i in range(3))
-    down_bias, second_gain, second_shift = (vectors_ref[i : i + 1, :] for i in range(3, 6))
+    shard = model // shards
+    lines = [ref[...].astype(F32).reshape(1, model) for ref in vector_refs]
+    out_bias, first_gain, first_shift, down_bias, second_gain, second_shift = lines
     small_out[...] = jnp.zeros_like(small_out)
+    links.barrier(ring=False)
+    for source, target in ((hidden_ref, hidden_here), (down_ref, down_here)):
+        for t in range(PARTS):
+            links.keep(source.at[t], target.at[t])
+    copies = list(links.copies)
+
+    def settle(copy):
+        copy.wait()
+        links.copies = [other for other in links.copies if other is not copy]
 
     def span(i):
         return pl.ds(pl.multiple_of(i * ROW_BLOCK, ROW_BLOCK), ROW_BLOCK)
@@ -1052,22 +1337,30 @@
 
     lax.fori_loop(0, blocks, first, 0)
     second_sum[...] = first_norm[...] + down_bias
+    for t in range(PARTS):
+        settle(copies[t])
 
     def up(t, carry):
-        pre = dot(first_low[...], hidden_ref[t]) + hidden_bias_ref[t]
+        pre = dot(first_low[...], hidden_here[t]) + hidden_bias_ref[t]
         cumulative = 0.5 * (1.0 + lax.erf(pre * ROOT_HALF))
         slope[t] = cumulative + pre * (PHI_ZERO * jnp.exp(-0.5 * pre * pre))
-        active = (pre * cumulative).astype(BF16)
-        activation[t] = active
-        second_sum[...] += dot_t(active, down_ref[t])
+        activation[t] = (pre * cumulative).astype(BF16)
         return carry
 
     lax.fori_loop(0, PARTS, up, 0)
+    for t in range(PARTS):
+        settle(copies[PARTS + t])
+
+    def mix(t, carry):
+        second_sum[...] += dot_t(activation[t], down_here[t])
+        return carry
+
+    lax.fori_loop(0, PARTS, mix, 0)
 
     def second(i, carry):
         at = span(i)
         normed, inverse = normalized(second_sum[at, :])
-        layer_out[at, :] = (normed * second_gain + second_shift).astype(BF16)
+        layer_here[at, :] = (normed * second_gain + second_shift).astype(BF16)
         upstream = cotangent_ref[at, :].astype(F32)
         small_out[4:5, :] += column_sum(upstream * normed)
         small_out[5:6, :] += column_sum(upstream)
@@ -1078,24 +1371,49 @@
         return carry
 
     lax.fori_loop(0, blocks, second, 0)
+    links.keep(layer_here, layer_out)
     turned[...] = jnp.transpose(second_low[...])
-
-    def down_back(t, carry):
-        down_grad_out[t] = dot(turned[...], activation[t]).astype(BF16)
+    numbers = {}
+
+    def pass_on(name, n, buffer, slots):
+        numbers[name, n] = links.number()
+        links.start(numbers[name, n], buffer.at[n], slots.at[n], beside)
+
+    def add_own(name, y, slots, sums, result):
+        links.arrive(numbers[name, y], slots.at[y], beside)
+
+        def one(i, carry):
+            at = pl.ds(pl.multiple_of(i * shard, shard), shard)
+            sums[y, at] = plus(sums[y, at], slots[y, at])
+            return carry
+
+        lax.fori_loop(0, shards, one, 0)
+        links.keep(sums.at[y], result.at[y])
+
+    def down_back(n, carry, base, result):
+        result[n] = dot(turned[...], activation[base + 2 * n]).astype(BF16)
         return carry
 
-    lax.fori_loop(0, PARTS, down_back, 0)
-    turned[...] = jnp.transpose(first_low[...])
-
-    def back(t, carry):
-        low = (dot(second_low[...], down_ref[t]) * slope[t]).astype(BF16)
+    def back(n, carry, base, result):
+        t = base + 2 * n
+        low = (dot(second_low[...], down_here[t]) * slope[t]).astype(BF16)
         small_out[pl.ds(6 + t, 1), :] += column_sum(low.astype(F32))
         back_low[...] = low
-        second_sum[...] += dot_t(low, hidden_ref[t])
-        hidden_grad_out[t] = dot(turned[...], back_low[...]).astype(BF16)
+        second_sum[...] += dot_t(low, hidden_here[t])
+        result[n] = dot(turned[...], back_low[...]).astype(BF16)
         return carry
 
-    lax.fori_loop(0, PARTS, back, 0)
+    lax.fori_loop(0, 2, functools.partial(down_back, base=1 - core, result=down_send), 0)
+    for n in range(2):
+        pass_on("down", n, down_send, down_two)
+    lax.fori_loop(0, 2, functools.partial(down_back, base=core, result=down_sum), 0)
+    turned[...] = jnp.transpose(first_low[...])
+    lax.fori_loop(0, 2, functools.partial(back, base=1 - core, result=hidden_send), 0)
+    for n in range(2):
+        pass_on("hidden", n, hidden_send, hidden_two)
+    for n in range(2):
+        add_own("down", n, down_two, down_sum, down_out)
+    lax.fori_loop(0, 2, functools.partial(back, base=core, result=hidden_sum), 0)
 
     def last(i, carry):
         at = span(i)
@@ -1109,33 +1427,42 @@
         second_low[at, :] = grad.astype(BF16)
         return carry
 
+    for y in range(2):
+        add_own("hidden", y, hidden_two, hidden_sum, hidden_out)
     lax.fori_loop(0, blocks, last, 0)
     turned[...] = jnp.transpose(second_low[...])
     for t in range(PARTS):
         grads = dot(second_low[...], out_ref[t])
         context_grad_out[t] = jnp.transpose(grads).astype(BF16)
         out_grad[t] = dot_t(turned[...], context_ref[t]).astype(BF16)
-
-
-def middle(context, x, cotangent, out, hidden, down, vectors, hidden_bias):
+    links.finish()
+    assert links.used <= middle_copies(shards), links.used
+
+
+def middle(shards, context, x, cotangent, out, vectors, hidden_bias, hidden, down):
     rows, model = x.shape
     width, units = context.shape[1], hidden.shape[2]
+    count = middle_copies(shards)
     big = pltpu.VMEM((rows, model), F32)
     low = pltpu.VMEM((rows, model), BF16)
+    pair = pltpu.VMEM((2, model, units), BF16)
     return pl.pallas_call(
-        middle_kernel,
+        functools.partial(middle_kernel, shards),
         out_shape=(
-            jax.ShapeDtypeStruct((rows, model), BF16),
             jax.ShapeDtypeStruct((rows, model), F32),
             jax.ShapeDtypeStruct((PARTS, width, rows), BF16),
             jax.ShapeDtypeStruct((PARTS, model, width), BF16),
-            jax.ShapeDtypeStruct((PARTS, model, units), BF16),
-            jax.ShapeDtypeStruct((PARTS, model, units), BF16),
             jax.ShapeDtypeStruct((16, model), F32),
+            jax.ShapeDtypeStruct((rows, model), BF16),
+            jax.ShapeDtypeStruct((2, model, units), BF16),
+            jax.ShapeDtypeStruct((2, model, units), BF16),
         ),
-        in_specs=[vmem()] * 8,
-        out_specs=[vmem()] * 7,
+        in_specs=[vmem()] * 11 + [anywhere()] * 2,
+        out_specs=[vmem()] * 4 + [anywhere()] * 3,
         scratch_shapes=[
+            low,
+            pltpu.VMEM(hidden.shape, BF16),
+            pltpu.VMEM(hidden.shape, BF16),
             big,
             big,
             pltpu.VMEM((rows, 1), F32),
@@ -1146,10 +1473,21 @@
             low,
             pltpu.VMEM((model, rows), BF16),
             pltpu.VMEM((rows, units), BF16),
+            pair,
+            pair,
+            pair,
+            pair,
+            pair,
+            pair,
+            pltpu.SemaphoreType.DMA((count,)),
+            pltpu.SemaphoreType.DMA((count,)),
+            pltpu.SemaphoreType.DMA((16,)),
         ],
-        compiler_params=pltpu.CompilerParams(vmem_limit_bytes=VMEM_LIMIT),
+        compiler_params=pltpu.CompilerParams(
+            collective_id=1, has_side_effects=True, vmem_limit_bytes=VMEM_LIMIT
+        ),
         name="middle",
-    )(context, x, cotangent, out, hidden, down, vectors, hidden_bias)
+    )(context, x, cotangent, out, *vectors, hidden_bias, hidden, down)
 
 
 def body(
@@ -1173,12 +1511,9 @@
     second_shift,
     output_cotangent,
 ):
-    part = lax.axis_index("tensor")
-    local_rows, model = tokens.shape
+    model = tokens.shape[1]
     width = query_weight.shape[1]
     units = hidden_weight.shape[1]
-    joined = jnp.concatenate([query_weight, key_weight, value_weight], axis=1)
-    segments = segment_ids.astype(F32).reshape(PARTS, 1, local_rows)
     (
         all_x,
         joined_turned,
@@ -1196,38 +1531,65 @@
     ) = forward(
         shards,
         tokens,
-        joined,
+        query_weight,
+        key_weight,
+        value_weight,
         hidden_weight,
         down_weight.T,
-        out_weight.T,
-        hidden_bias.astype(F32)[None, :],
-        query_bias.astype(F32)[:, None],
-        value_bias.astype(F32)[:, None],
-        segments,
+        out_weight,
+        hidden_bias,
+        query_bias,
+        value_bias,
+        segment_ids,
     )
     all_hidden = all_hidden.reshape(PARTS, model, units)
     all_down = all_down.reshape(PARTS, model, units)
     all_out = all_out.reshape(PARTS, model, width)
-    vectors = jnp.stack(
-        [out_bias, first_gain, first_shift, down_bias, second_gain, second_shift]
-        + [jnp.zeros_like(out_bias)] * 2
-    ).astype(F32)
+    vectors = (out_bias, first_gain, first_shift, down_bias, second_gain, second_shift)
     (
-        layer_output,
         first_grad,
         context_grad,
         out_grad,
+        small,
+        layer_output,
         hidden_grad,
         down_grad,
-        small,
-    ) = middle(row_context, tokens, output_cotangent, all_out, all_hidden, all_down, vectors, all_bias)
+    ) = middle(
+        shards,
+        row_context,
+        tokens,
+        output_cotangent,
+        all_out,
+        vectors,
+        all_bias,
+        all_hidden,
+        all_down,
+    )
     rows = model // shards
-    tokens_gradient, joined_grad, hidden_grad, down_grad, out_grad, small, bias_grad = backward(
+    (
+        tokens_gradient,
+        query_grad,
+        key_grad,
+        value_grad,
+        hidden_grad,
+        down_grad,
+        out_grad,
+        query_bias_grad,
+        value_bias_grad,
+        hidden_bias_grad,
+        out_bias_grad,
+        first_gain_grad,
+        first_shift_grad,
+        down_bias_grad,
+        second_gain_grad,
+        second_shift_grad,
+    ) = outputs(
+        first_grad,
+        *backward(
         shards,
         context_grad,
-        first_grad,
-        hidden_grad.reshape(PARTS, shards, rows, units),
-        down_grad.reshape(PARTS, shards, rows, units),
+        hidden_grad.reshape(2, shards, rows, units),
+        down_grad.reshape(2, shards, rows, units),
         out_grad.reshape(PARTS, shards, rows, width),
         small,
         all_x,
@@ -1238,27 +1600,27 @@
         values,
         context,
         totals,
-        segments,
+        segment_ids,
+        ),
     )
-    hidden_bias_gradient = lax.dynamic_index_in_dim(small[6:10], part, 0, keepdims=False)
     return (
         layer_output,
         tokens_gradient,
-        joined_grad[:, :width],
-        bias_grad[0, :width],
-        joined_grad[:, width : 2 * width],
-        joined_grad[:, 2 * width :],
-        bias_grad[0, 2 * width :],
-        out_grad.T,
-        small[0],
-        small[1],
-        small[2],
+        query_grad,
+        query_bias_grad,
+        key_grad,
+        value_grad,
+        value_bias_grad,
+        out_grad,
+        out_bias_grad,
+        first_gain_grad,
+        first_shift_grad,
         hidden_grad,
-        hidden_bias_gradient,
+        hidden_bias_grad,
         down_grad.T,
-        small[3],
-        small[4],
-        small[5],
+        down_bias_grad,
+        second_gain_grad,
+        second_shift_grad,
     )
 
 

time: 213 us -> 182 us (0.85)
  local copies, waits for them, and re-layouts: 15.8 us -> 0.89 us
  Pallas kernels: 190 us -> 181 us
  other arithmetic: 4.84 us -> 0 us
    pallas_call x1, Pallas kernels: 75.7 us -> 68 us  [forward(): pl.pallas_call(functools.partial(forward_kernel, shards), out_shape=(shap...]
    unnamed x21 -> x3, local copies, waits for them, and re-layouts: 7.32 us -> 0.89 us
    slice x4 -> x0, local copies, waits for them, and re-layouts: 5.62 us -> none  [the longest x1 1.78 us: body(): joined_grad[:, 2 * width:]]
    pallas_call x1, Pallas kernels: 81.1 us -> 75.8 us  [backward(): pl.pallas_call(functools.partial(backward_kernel, shards), out_shape=(res...]
    pallas_call x1 -> x2, Pallas kernels: 33.6 us -> 36.9 us  [the longest x1 33.1 us: middle(): pl.pallas_call(functools.partial(middle_kernel, shards), out_shape=(jax.S...]
    broadcast_in_dim x3 -> x0, local copies, waits for them, and re-layouts: 2.8 us -> none  [the longest x1 1.26 us: body(): hidden_bias.astype(F32)[None, :]]
where the time goes in v4:
time: 182 us
  Pallas kernels  181 us (99%)
    pallas_call x1, Pallas kernels, backward(): pl.pallas_call(functools.partial(backward_kernel, shards), out_shape=(res...  75.8 us
    pallas_call x1, Pallas kernels, forward(): pl.pallas_call(functools.partial(forward_kernel, shards), out_shape=(shap...  68 us
    pallas_call x1, Pallas kernels, middle(): pl.pallas_call(functools.partial(middle_kernel, shards), out_shape=(jax.S...  33.1 us
    pallas_call x1, Pallas kernels, outputs(): pl.pallas_call(outputs_kernel, out_shape=(result(*rows.shape), *[result(s...  3.72 us

profile of v4, /device:TPU:0, one launch (start us, length us, event | category | flops | bytes accessed | tf_op | source)
XLA Modules:
  0.0 182.3 jit_solution(17955604239823595192)
XLA Ops:
  0.7 68.0 %forward.1 = (bf16[4,512,768]{2,1,0:T(8,128)(2,1)}, bf16[576,768]{1,0:T(8,128)(2,1)}, bf16[4,8,96,768]{3,2,1,0:T(8,128)(2,1)}, bf16[4,8,96,768]{3,2,1,0:T(8,128)...) custom-call(bf16[512,768]{1,0:T(8,128)(2,1)} %refs_1_.1, ...), custom_call_target="tpu_custom_call" | custom-call | tf_op jit(solution)/shard_map/forward/pallas_call | solution.py:567
  68.7 33.1 %middle.1 = (f32[512,768]{1,0:T(8,128)}, bf16[4,192,512]{2,1,0:T(8,128)(2,1)}, bf16[4,768,192]{2,1,0:T(8,128)(2,1)}, f32[16,768]{1,0:T(8,128)}, bf16[512,768]{1,...) custom-call(bf16[4,192,512]{2,1,0:T(8,128)(2,1)} %get-tuple-element.60.refs_0_, ...), custom_call_target="tpu_custom_call" | custom-call | tf_op jit(solution)/shard_map/middle/pallas_call | solution.py:1449
  101.9 75.8 %backward.1 = (f32[512,768]{1,0:T(8,128)}, f32[96,576]{1,0:T(8,128)}, f32[96,768]{1,0:T(8,128)}, f32[96,768]{1,0:T(8,128)}, f32[96,192]{1,0:T(8,128)}, /*index=5*/f32[16,768]{1,0:T(8,128)}, f32[8,576]{1,0:T(8,128)}) custom-call(bf16[4,192,512]{2,1,0:T(8,128)(2,1)} %get-tuple-element.67.context_grad_ref, bf16[2,8,96,768]{3,2,1,0:T(8,128)(2,1)} %bitcast.10, ...), custom_call_target="tpu_custom_call" | custom-call | tf_op jit(solution)/shard_map/backward/pallas_call | solution.py:1098
  177.7 0.0 copy-start
  177.7 3.7 %outputs.1 = (f32[512,768]{1,0:T(8,128)}, f32[96,192]{1,0:T(8,128)}, f32[96,192]{1,0:T(8,128)}, f32[96,192]{1,0:T(8,128)}, f32[96,768]{1,0:T(8,128)}, /*index=5*...) custom-call(f32[512,768]{1,0:T(8,128)} %get-tuple-element.66.base_re, ...), custom_call_target="tpu_custom_call" | custom-call | tf_op jit(solution)/shard_map/outputs/pallas_call | solution.py:1208
  181.4 0.0 copy-done
  181.4 0.9 copy.36
Async XLA Ops:
  177.7 3.7 %copy-start = (bf16[512,768]{1,0:T(8,128)(2,1)S(1)}, bf16[512,768]{1,0:T(8,128)(2,1)}, u32[]{:S(2)}) copy-start(bf16[512,768]{1,0:T(8,128)(2,1)} %get-tuple-element.120) | copy-start | bytes 2359300

commit v5 on v4

--- a/solution.py
+++ b/solution.py
@@ -189,12 +189,17 @@
     (("f", 4, -1), ("e", 4), ("p", 4),),
 )
 BACKWARD_PLAN = (
+    (),
     (("s", 0), ("o", 0), ("d", 1, 0), ("d", 1, 1),),
     (("h", 0), ("o", 1, 0), ("o", 1, 1), ("s", 1), ("d", 2, 0), ("d", 2, 1),),
-    (("h", 1), ("s", 2), ("o", 2, 0), ("o", 2, 1),),
-    (("d", 3, 0), ("s", 3),),
-    (("d", 3, 1), ("h", 2), ("s", 4), ("o", 3, 0), ("o", 3, 1),),
-    (("d", 4, 0), ("d", 4, 1), ("h", 3), ("o", 4, 0), ("o", 4, 1), ("q", 0), ("r", 0), ("j", 1), ("q", 1), ("h", 4), ("q", 2), ("j", 2), ("j", 3), ("j", 4),),
+    (("h", 1), ("s", 2), ("o", 2, 0), ("o", 2, 1), ("d", 3, 0), ("s", 3),),
+    (("d", 3, 1),),
+    (("s", 4), ("h", 2), ("o", 3, 0), ("o", 3, 1), ("d", 4, 0),),
+    (("d", 4, 1), ("h", 3), ("o", 4, 0),),
+    (("o", 4, 1), ("j", 1, 0), ("j", 1, 1),),
+    (),
+    (),
+    (("h", 4), ("q", 0), ("j", 2, 0), ("r", 0), ("j", 2, 1), ("q", 1), ("j", 3, 0), ("j", 3, 1), ("q", 2), ("j", 4, 0), ("j", 4, 1),),
 )
 
 
@@ -503,6 +508,7 @@
         start = jnp.full((8, BLOCK), NEGATIVE, F32)
         tops = lax.fori_loop(low, high, scores, (start,) * heads)
         tops = [jnp.max(top, axis=0, keepdims=True) for top in tops]
+        links.spent(2.1, "scores")
         agenda.point()
 
         def mix(j, state):
@@ -522,6 +528,7 @@
             total = jnp.sum(state[h][0], axis=0, keepdims=True)
             context_here[i, h * HEAD : (h + 1) * HEAD, :] = (state[h][1] / total).astype(BF16)
             total_out[i, h : h + 1, :] = tops[h] + jnp.log(total)
+        links.spent(2.4, "mix")
         if n < 3:
             links.start(
                 context_numbers[n],
@@ -686,7 +693,7 @@
 
 
 def backward_copies(shards):
-    return 50 + 8 * shards
+    return 50 + 10 * shards
 
 
 def backward_kernel(
@@ -698,11 +705,11 @@
     x_all,
     joined_all,
     small_ref,
-    query_ref,
-    key_turned_ref,
-    key_ref,
-    value_ref,
-    context_ref,
+    query_all,
+    key_turned_all,
+    key_all,
+    value_all,
+    context_all,
     total_ref,
     segment_ids_ref,
     rows_out,
@@ -714,6 +721,11 @@
     bias_out,
     x_ref,
     joined_ref,
+    query_ref,
+    key_turned_ref,
+    key_ref,
+    value_ref,
+    context_ref,
     segment_ref,
     upstream,
     key_segments,
@@ -722,6 +734,7 @@
     projected,
     weight_sum,
     joined_terms,
+    value_terms,
     rows_send,
     rows_own,
     rows_block,
@@ -733,6 +746,7 @@
     out_own,
     out_two,
     joined_slots,
+    value_slots,
     hidden_slots,
     down_slots,
     out_slots,
@@ -749,6 +763,28 @@
     links = Links(shards, send, recv, local)
     core, row, part = links.core, links.row, links.part
     across, beside = {"tensor": links.other_row}, {"tensor": links.other_core}
+    def kept(source, target):
+        links.keep(source, target)
+        return links.copies[-1]
+
+    def settle(copy):
+        copy.wait()
+        links.copies = [other for other in links.copies if other is not copy]
+
+    down_copies = [kept(down_ref.at[y], down_two.at[y]) for y in range(2)]
+    out_copies = [kept(out_ref.at[2 * y + core], out_own.at[y]) for y in range(2)]
+    hidden_copy = kept(hidden_ref.at[row], hidden_own)
+    early_copies = [
+        kept(query_all, query_ref),
+        kept(key_turned_all, key_turned_ref),
+        kept(key_all, key_ref),
+        kept(value_all, value_ref),
+        kept(context_all, context_ref),
+    ]
+    late_copies = [
+        kept(joined_all, joined_ref),
+        kept(x_all, x_ref),
+    ]
     links.barrier(diagonal=True, cube=True)
     half = shards // 2
     rows = joined_terms.shape[1]
@@ -783,21 +819,6 @@
     for y in range(2):
         to_core("out", out_ref, out_two, y)
 
-    def kept(source, target):
-        links.keep(source, target)
-        return links.copies[-1]
-
-    def settle(copy):
-        copy.wait()
-        links.copies = [other for other in links.copies if other is not copy]
-
-    down_copies = [kept(down_ref.at[y], down_two.at[y]) for y in range(2)]
-    out_copies = [kept(out_ref.at[2 * y + core], out_own.at[y]) for y in range(2)]
-    hidden_copy = kept(hidden_ref.at[row], hidden_own)
-    late_copies = [
-        kept(joined_all, joined_ref),
-        kept(x_all, x_ref),
-    ]
     upstream[part] = context_grad_ref[part]
 
     cube = [{"dp": index} for index in links.cube()]
@@ -962,6 +983,9 @@
         i = places[n]
         if n == 0:
             links.arrive(numbers["upstream", 2], upstream.at[links.other_core], beside)
+            for copy in early_copies:
+                settle(copy)
+            agenda.point()
         elif n == 1:
             for m in range(2):
                 partner = partners[m]
@@ -1004,21 +1028,53 @@
         sums = lax.fori_loop(low, high, block, (empty,) * heads)
         for h in range(heads):
             projected[i, spans[h], :] = (sums[h] * scale).astype(BF16)
+        links.spent([8.9, 8.9, 6.8, 6.8][n], "near")
         agenda.point()
 
     for k in range(3):
         project_keys((inner_far, 1 + row, 3 * row)[k])
-    weight = dot(projected[0], x_ref[0])
-    for s in range(1, PARTS):
-        weight = weight + dot(projected[s], x_ref[s])
-    weight_sum[...] = weight
-    turned = jnp.transpose(weight_sum[...]).astype(BF16)
-    joined_terms[...] = turned.reshape(joined_terms.shape)
-    joined = RingSum(links, rows, lambda o: joined_terms.at[links.at(o)], joined_slots)
-    joined.send(1)
+    joined = []
+    for terms, slots, span in (
+        (joined_terms, joined_slots, slice(0, 2 * width)),
+        (value_terms, value_slots, slice(2 * width, 3 * width)),
+    ):
+        weight = dot(projected[0, span, :], x_ref[0])
+        for s in range(1, PARTS):
+            weight = weight + dot(projected[s, span, :], x_ref[s])
+        weight_sum[span, :] = weight
+        turned = jnp.transpose(weight_sum[span, :]).astype(BF16)
+        terms[...] = turned.reshape(terms.shape)
+        term = lambda o, terms=terms: terms.at[links.at(o)]
+        joined.append(RingSum(links, rows, term, slots))
+        joined[-1].send(1)
+        links.spent(2.7 if span.start == 0 else 1.5, "weight")
+    def joined_step(step, n):
+        joined[n].arrive(step)
+        if step < half:
+            joined[n].send(step + 1)
+        elif n == 0:
+            joined_out[:, : 2 * width] = joined[n].total()
+        else:
+            joined_out[:, 2 * width :] = joined[n].total()
+
+    def hidden_last():
+        hidden.arrive(half)
+        hidden_out[...] = hidden.total()
+
+    for step in range(1, half + 1):
+        for n in range(2):
+            agenda.add(
+                ("j", step, n),
+                lambda step=step, n=n: sent_numbers(joined[n], step),
+                lambda step=step, n=n: joined_step(step, n),
+            )
+    agenda.add(("h", half), lambda: sent_numbers(hidden, half), hidden_last)
+    agenda.point()
     far_rows(1, inner_far)
+    agenda.point()
     rows_send[...] = x_grad(links.other_core).astype(BF16)
     far_sum(1, inner_far)
+    agenda.point()
     rows_number = links.number()
     links.start(rows_number, rows_send, rows_own, beside)
     ones = jnp.ones((8, BLOCK), BF16)
@@ -1028,29 +1084,12 @@
     bias_sums[bias_sums.shape[0] - 1] = bias
     sums_of = Pairwise(bias_sums.at[bias_sums.shape[0] - 1], bias_slots, bias_sums, bias_out, cube)
     rows_out[...] = x_grad(part)
-
-    def joined_step(step):
-        joined.arrive(step)
-        if step < half:
-            joined.send(step + 1)
-        else:
-            joined_out[...] = joined.total()
-
-    def hidden_last():
-        hidden.arrive(half)
-        hidden_out[...] = hidden.total()
+    agenda.point()
 
     def add_rows():
         links.arrive(rows_number, rows_own, beside)
         rows_out[...] += rows_own[...].astype(F32)
 
-    for step in range(1, half + 1):
-        agenda.add(
-            ("j", step),
-            lambda step=step: sent_numbers(joined, step),
-            lambda step=step: joined_step(step),
-        )
-    agenda.add(("h", half), lambda: sent_numbers(hidden, half), hidden_last)
     agenda.add(("r", 0), lambda: [rows_number], add_rows)
     for step in range(len(cube)):
         agenda.add(
@@ -1106,11 +1145,16 @@
             result(*small.shape),
             result(8, 3 * width),
         ),
-        in_specs=[vmem()] + [anywhere()] * 5 + [vmem()] * 8,
+        in_specs=[vmem()] + [anywhere()] * 5 + [vmem()] + [anywhere()] * 5 + [vmem()] * 2,
         out_specs=[vmem()] * 7,
         scratch_shapes=[
             low(*x.shape),
             low(*joined.shape),
+            low(*queries.shape),
+            low(*keys_turned.shape),
+            low(*keys.shape),
+            low(*values.shape),
+            low(*context.shape),
             wide(PARTS, 1, BLOCK),
             low(*context_grad.shape),
             wide(PARTS, BLOCK, 128),
@@ -1118,7 +1162,8 @@
             wide(PARTS, width, rows),
             low(PARTS, 3 * width, rows),
             wide(3 * width, model),
-            low(shards, *shard),
+            low(shards, shard[0], 2 * width),
+            low(shards, shard[0], width),
             low(rows, model),
             low(rows, model),
             low(2, 2, rows // 2, model),
@@ -1129,7 +1174,8 @@
             low(2, *down.shape[1:]),
             low(2, *out.shape[1:]),
             low(2, *out.shape[1:]),
-            low(half, 2, *shard),
+            low(half, 2, shard[0], 2 * width),
+            low(half, 2, shard[0], width),
             low(half, 2, *hidden.shape[2:]),
             low(2, half, 2, *down.shape[2:]),
             low(2, half, 2, *out.shape[2:]),
@@ -1141,7 +1187,7 @@
             wide(stages, 8, 3 * width),
             pltpu.SemaphoreType.DMA((count,)),
             pltpu.SemaphoreType.DMA((count,)),
-            pltpu.SemaphoreType.DMA((8,)),
+            pltpu.SemaphoreType.DMA((16,)),
         ],
         compiler_params=pltpu.CompilerParams(
             collective_id=3, has_side_effects=True, vmem_limit_bytes=VMEM_LIMIT

time: 182 us -> 180 us (0.989)
  Pallas kernels: 181 us -> 179 us
    pallas_call x1, Pallas kernels: 75.8 us -> 73.7 us  [backward(): pl.pallas_call(functools.partial(backward_kernel, shards), out_shape=(res...]
where the time goes in v5:
time: 180 us
  Pallas kernels  179 us (99%)
    pallas_call x1, Pallas kernels, backward(): pl.pallas_call(functools.partial(backward_kernel, shards), out_shape=(res...  73.7 us
    pallas_call x1, Pallas kernels, forward(): pl.pallas_call(functools.partial(forward_kernel, shards), out_shape=(shap...  68 us
    pallas_call x1, Pallas kernels, middle(): pl.pallas_call(functools.partial(middle_kernel, shards), out_shape=(jax.S...  33.1 us
    pallas_call x1, Pallas kernels, outputs(): pl.pallas_call(outputs_kernel, out_shape=(result(*rows.shape), *[result(s...  3.72 us

profile of v5, /device:TPU:0, one launch (start us, length us, event | category | flops | bytes accessed | tf_op | source)
XLA Modules:
  0.0 180.2 jit_solution(8099900103606271217)
XLA Ops:
  0.7 68.0 %forward.1 = (bf16[4,512,768]{2,1,0:T(8,128)(2,1)}, bf16[576,768]{1,0:T(8,128)(2,1)}, bf16[4,8,96,768]{3,2,1,0:T(8,128)(2,1)}, bf16[4,8,96,768]{3,2,1,0:T(8,128)...) custom-call(bf16[512,768]{1,0:T(8,128)(2,1)} %refs_1_.1, ...), custom_call_target="tpu_custom_call" | custom-call | tf_op jit(solution)/shard_map/forward/pallas_call | solution.py:574
  68.7 33.1 %middle.1 = (f32[512,768]{1,0:T(8,128)}, bf16[4,192,512]{2,1,0:T(8,128)(2,1)}, bf16[4,768,192]{2,1,0:T(8,128)(2,1)}, f32[16,768]{1,0:T(8,128)}, bf16[512,768]{1,...) custom-call(bf16[4,192,512]{2,1,0:T(8,128)(2,1)} %get-tuple-element.60.refs_0_, ...), custom_call_target="tpu_custom_call" | custom-call | tf_op jit(solution)/shard_map/middle/pallas_call | solution.py:1495
  101.9 73.7 %backward.1 = (f32[512,768]{1,0:T(8,128)}, f32[96,576]{1,0:T(8,128)}, f32[96,768]{1,0:T(8,128)}, f32[96,768]{1,0:T(8,128)}, f32[96,192]{1,0:T(8,128)}, /*index=5*/f32[16,768]{1,0:T(8,128)}, f32[8,576]{1,0:T(8,128)}) custom-call(bf16[4,192,512]{2,1,0:T(8,128)(2,1)} %get-tuple-element.67.context_grad_ref, bf16[2,8,96,768]{3,2,1,0:T(8,128)(2,1)} %bitcast.10, ...), custom_call_target="tpu_custom_call" | custom-call | tf_op jit(solution)/shard_map/backward/pallas_call | solution.py:1137
  175.5 0.0 copy-start
  175.5 3.7 %outputs.1 = (f32[512,768]{1,0:T(8,128)}, f32[96,192]{1,0:T(8,128)}, f32[96,192]{1,0:T(8,128)}, f32[96,192]{1,0:T(8,128)}, f32[96,768]{1,0:T(8,128)}, /*index=5*...) custom-call(f32[512,768]{1,0:T(8,128)} %get-tuple-element.66.base_re, ...), custom_call_target="tpu_custom_call" | custom-call | tf_op jit(solution)/shard_map/outputs/pallas_call | solution.py:1254
  179.3 0.0 copy-done
  179.3 0.9 copy.36
Async XLA Ops:
  175.5 3.7 %copy-start = (bf16[512,768]{1,0:T(8,128)(2,1)S(1)}, bf16[512,768]{1,0:T(8,128)(2,1)}, u32[]{:S(2)}) copy-start(bf16[512,768]{1,0:T(8,128)(2,1)} %get-tuple-element.120) | copy-start | bytes 2359300

commit v6 on v5

--- a/solution.py
+++ b/solution.py
@@ -1213,6 +1213,7 @@
 
 def outputs_kernel(
     base_ref,
+    layer_ref,
     rows_ref,
     joined_ref,
     hidden_ref,
@@ -1221,6 +1222,7 @@
     small_ref,
     bias_ref,
     rows_out,
+    layer_out,
     query_out,
     key_out,
     value_out,
@@ -1233,6 +1235,7 @@
     *vector_outs,
 ):
     rows_out[...] = base_ref[...] + rows_ref[...]
+    layer_out[...] = layer_ref[...]
     width = query_bias_out.shape[0]
     for n, result in enumerate((query_out, key_out, value_out)):
         result[...] = joined_ref[:, n * width : (n + 1) * width]
@@ -1247,7 +1250,7 @@
         result[...] = small_ref[n, :]
 
 
-def outputs(base, rows, joined, hidden, down, out, small, bias):
+def outputs(base, layer, rows, joined, hidden, down, out, small, bias):
     shard, width = out.shape
     model = rows.shape[1]
     result = lambda *dims: jax.ShapeDtypeStruct(dims, F32)
@@ -1255,6 +1258,7 @@
         outputs_kernel,
         out_shape=(
             result(*rows.shape),
+            jax.ShapeDtypeStruct(layer.shape, layer.dtype),
             *[result(shard, width)] * 3,
             result(*hidden.shape),
             result(*down.shape),
@@ -1263,11 +1267,11 @@
             result(width),
             *[result(model)] * 7,
         ),
-        in_specs=[vmem()] * 8,
-        out_specs=[vmem()] * 16,
+        in_specs=[vmem()] * 9,
+        out_specs=[vmem()] * 17,
         compiler_params=pltpu.CompilerParams(vmem_limit_bytes=VMEM_LIMIT),
         name="outputs",
-    )(base, rows, joined, hidden, down, out, small, bias)
+    )(base, layer, rows, joined, hidden, down, out, small, bias)
 
 
 ROW_BLOCK = 128
@@ -1314,14 +1318,15 @@
     hidden_bias_ref,
     hidden_ref,
     down_ref,
-    first_grad_out,
     context_grad_out,
     out_grad,
     small_out,
+    first_grad_out,
     layer_out,
     hidden_out,
     down_out,
     layer_here,
+    first_grad_here,
     hidden_here,
     down_here,
     first_norm,
@@ -1469,13 +1474,14 @@
         small_out[2:3, :] += column_sum(upstream)
         grad = normalized_back(upstream, normed, first_scale[at, :], first_gain)
         small_out[0:1, :] += column_sum(grad)
-        first_grad_out[at, :] = grad
+        first_grad_here[at, :] = grad
         second_low[at, :] = grad.astype(BF16)
         return carry
 
     for y in range(2):
         add_own("hidden", y, hidden_two, hidden_sum, hidden_out)
     lax.fori_loop(0, blocks, last, 0)
+    links.keep(first_grad_here, first_grad_out)
     turned[...] = jnp.transpose(second_low[...])
     for t in range(PARTS):
         grads = dot(second_low[...], out_ref[t])
@@ -1495,18 +1501,19 @@
     return pl.pallas_call(
         functools.partial(middle_kernel, shards),
         out_shape=(
-            jax.ShapeDtypeStruct((rows, model), F32),
             jax.ShapeDtypeStruct((PARTS, width, rows), BF16),
             jax.ShapeDtypeStruct((PARTS, model, width), BF16),
             jax.ShapeDtypeStruct((16, model), F32),
+            jax.ShapeDtypeStruct((rows, model), F32),
             jax.ShapeDtypeStruct((rows, model), BF16),
             jax.ShapeDtypeStruct((2, model, units), BF16),
             jax.ShapeDtypeStruct((2, model, units), BF16),
         ),
         in_specs=[vmem()] * 11 + [anywhere()] * 2,
-        out_specs=[vmem()] * 4 + [anywhere()] * 3,
+        out_specs=[vmem()] * 3 + [anywhere()] * 4,
         scratch_shapes=[
             low,
+            big,
             pltpu.VMEM(hidden.shape, BF16),
             pltpu.VMEM(hidden.shape, BF16),
             big,
@@ -1593,10 +1600,10 @@
     all_out = all_out.reshape(PARTS, model, width)
     vectors = (out_bias, first_gain, first_shift, down_bias, second_gain, second_shift)
     (
-        first_grad,
         context_grad,
         out_grad,
         small,
+        first_grad,
         layer_output,
         hidden_grad,
         down_grad,
@@ -1614,6 +1621,7 @@
     rows = model // shards
     (
         tokens_gradient,
+        layer_output,
         query_grad,
         key_grad,
         value_grad,
@@ -1631,6 +1639,7 @@
         second_shift_grad,
     ) = outputs(
         first_grad,
+        layer_output,
         *backward(
         shards,
         context_grad,

time: 180 us -> 180 us (level)
  no operation moved by 1% of the time
where the time goes in v6:
time: 180 us; the launch traced here: 179 us
  Pallas kernels  178 us (99%)
    pallas_call x1, Pallas kernels, backward(): pl.pallas_call(functools.partial(backward_kernel, shards), out_shape=(res...  73.7 us
    pallas_call x1, Pallas kernels, forward(): pl.pallas_call(functools.partial(forward_kernel, shards), out_shape=(shap...  68 us
    pallas_call x1, Pallas kernels, middle(): pl.pallas_call(functools.partial(middle_kernel, shards), out_shape=(jax.S...  32.6 us
    pallas_call x1, Pallas kernels, outputs(): pl.pallas_call(outputs_kernel, out_shape=(result(*rows.shape), jax.ShapeD...  4.2 us

profile of v6, /device:TPU:0, one launch (start us, length us, event | category | flops | bytes accessed | tf_op | source)
XLA Modules:
  0.0 179.3 jit_solution(1257319018015207338)
XLA Ops:
  0.7 68.0 %forward.1 = (bf16[4,512,768]{2,1,0:T(8,128)(2,1)}, bf16[576,768]{1,0:T(8,128)(2,1)}, bf16[4,8,96,768]{3,2,1,0:T(8,128)(2,1)}, bf16[4,8,96,768]{3,2,1,0:T(8,128)...) custom-call(bf16[512,768]{1,0:T(8,128)(2,1)} %refs_1_.1, ...), custom_call_target="tpu_custom_call" | custom-call | tf_op jit(solution)/shard_map/forward/pallas_call | solution.py:574
  68.7 32.6 %middle.1 = (bf16[4,192,512]{2,1,0:T(8,128)(2,1)}, bf16[4,768,192]{2,1,0:T(8,128)(2,1)}, f32[16,768]{1,0:T(8,128)}, f32[512,768]{1,0:T(8,128)}, bf16[512,768]{1,...) custom-call(bf16[4,192,512]{2,1,0:T(8,128)(2,1)} %get-tuple-element.61.refs_0_, ...), custom_call_target="tpu_custom_call" | custom-call | tf_op jit(solution)/shard_map/middle/pallas_call | solution.py:1501
  101.3 73.7 %backward.1 = (f32[512,768]{1,0:T(8,128)}, f32[96,576]{1,0:T(8,128)}, f32[96,768]{1,0:T(8,128)}, f32[96,768]{1,0:T(8,128)}, f32[96,192]{1,0:T(8,128)}, /*index=5*/f32[16,768]{1,0:T(8,128)}, f32[8,576]{1,0:T(8,128)}) custom-call(bf16[4,192,512]{2,1,0:T(8,128)(2,1)} %get-tuple-element.68.context_grad_ref, bf16[2,8,96,768]{3,2,1,0:T(8,128)(2,1)} %bitcast.10, ...), custom_call_target="tpu_custom_call" | custom-call | tf_op jit(solution)/shard_map/backward/pallas_call | solution.py:1137
  175.0 4.2 %outputs.1 = (f32[512,768]{1,0:T(8,128)}, bf16[512,768]{1,0:T(8,128)(2,1)}, f32[96,192]{1,0:T(8,128)}, f32[96,192]{1,0:T(8,128)}, f32[96,192]{1,0:T(8,128)}, /*i...) custom-call(f32[512,768]{1,0:T(8,128)} %get-tuple-element.66.base_re, ...), custom_call_target="tpu_custom_call" | custom-call | tf_op jit(solution)/shard_map/outputs/pallas_call | solution.py:1257
